TPU v7x, 256 devices: a whole 4x4x8 slice. The times are simulated.
256 devices in a mesh: space: 16 (over z, x_hi), band: 16 (over y, x_lo, core).
Axes of the slice: x: 4 (x_hi: 2, x_lo: 2; x = x_hi * 2 + x_lo), y: 4, z: 8, core: 2. Of those that a mesh axis runs over, the one named last changes fastest.
Arguments:
- orbitals: float32 [192, 512, 256], P('space', 'band'), may hold values from -6 to 6
- potential: float32 [192, 256], P('space'), may hold values from -10 to 10
Outputs:
- rotated: float32 [192, 512, 256], P('space', 'band')
- correlation: float32 [512, 512], replicated
All inputs are finite; a program needn't handle non-finite values.
Results may differ from a plain program's by a relative error of at most 0.000098.
Values sent between devices are 32-bit elements; how exact they have to be, the bound alone decides.
No kernel may reach another device: no remote copies, remote signals or barrier semaphores. Data moves between devices by JAX's collectives and lax.ppermute only.
A program may use at most 320 MiB of HBM per device.

v0:
```python
import functools

import jax
import jax.numpy as jnp
import numpy as np
from jax import lax
from jax.experimental import pallas as pl
from jax.experimental.pallas import tpu as pltpu
from jax.sharding import Mesh
from jax.sharding import PartitionSpec as P

NX = 16
NY = 16
CELLS = NX * NY
COEFS = [12.0 / 7.0, -15.0 / 56.0, 10.0 / 189.0, -1.0 / 112.0, 2.0 / 1925.0, -1.0 / 16632.0]
CENTER_COEF = -5369.0 / 1800.0
INV_SPACING2 = 6.25
SHIFT_MID = 42.0
HALF_SPAN = 38.0
RADIUS = 6

SPACE = ("z", "xh")
TEAM = ("y", "xl")
BAND = ("y", "xl", "c")

BLOCKS = [[(0, 0), (1, 0), (1, 1), (2, 0), (2, 1)], [(2, 2), (3, 0), (3, 1), (3, 2), (3, 3)]]
TILE = 128
GROUP = 16

SCALE = -0.5 * INV_SPACING2 / HALF_SPAN


def plane_matrix():
    ring = np.zeros((NX, NX))
    for k, coef in enumerate(COEFS):
        for i in range(NX):
            ring[i, (i + k + 1) % NX] += coef
            ring[i, (i - k - 1) % NX] += coef
    one = np.eye(NX)
    full = np.kron(ring, one) + np.kron(one, ring) + 3.0 * CENTER_COEF * np.eye(CELLS)
    return (SCALE * full).astype(np.float32)


def dot32(a, b, dims):
    return lax.dot_general(
        a, b, (dims, ((), ())), precision=lax.Precision.HIGHEST, preferred_element_type=jnp.float32
    )


def filter_kernel(rows, planes, low, own, pot, high, mat, out, first):
    def field(p):
        if p < planes:
            return low[p * rows : (p + 1) * rows, :]
        if p < 2 * planes:
            return own[(p - planes) * rows : (p - planes + 1) * rows, :]
        return high[(p - 2 * planes) * rows : (p - 2 * planes + 1) * rows, :]

    def level(p):
        if p < planes:
            row = low[planes * rows + p : planes * rows + p + 1, :]
        elif p < 2 * planes:
            row = pot[p - planes : p - planes + 1, :]
        else:
            row = high[planes * rows + p - 2 * planes : planes * rows + p - 2 * planes + 1, :]
        return (row - SHIFT_MID) / HALF_SPAN

    half = RADIUS * rows
    first[0:half, :] = dot32(low[(planes - RADIUS) * rows : planes * rows, :], mat[...], ((1,), (0,)))
    first[half : half + planes * rows, :] = dot32(own[...], mat[...], ((1,), (0,)))
    first[half + planes * rows :, :] = dot32(high[0:half, :], mat[...], ((1,), (0,)))
    for q in range(planes + 2 * RADIUS):
        p = q + planes - RADIUS
        acc = first[q * rows : (q + 1) * rows, :] + level(p) * field(p)
        for k in range(RADIUS):
            acc = acc + (SCALE * COEFS[k]) * (field(p + k + 1) + field(p - k - 1))
        first[q * rows : (q + 1) * rows, :] = acc
    inner = dot32(first[half : half + planes * rows, :], mat[...], ((1,), (0,)))
    for z in range(planes):
        q = z + RADIUS
        centre = first[q * rows : (q + 1) * rows, :]
        acc = inner[z * rows : (z + 1) * rows, :] + level(z + planes) * centre
        for k in range(RADIUS):
            up = first[(q + k + 1) * rows : (q + k + 2) * rows, :]
            down = first[(q - k - 1) * rows : (q - k) * rows, :]
            acc = acc + (SCALE * COEFS[k]) * (up + down)
        second = 2.0 * acc - field(z + planes)
        out[2 * z] = second[:, :TILE]
        out[2 * z + 1] = second[:, TILE:]


def gram_kernel(scale, place, own, other, out, stack):
    c = place[0]
    rows = own.shape[2]
    for half, ref in ((c, own), (1 - c, other)):
        for s in range(own.shape[0]):
            for t in range(own.shape[1]):
                at = pl.multiple_of(s * 2 * rows + half * rows, rows)
                stack[pl.ds(at, rows), t * TILE : (t + 1) * TILE] = ref[s, t]
    for k in range(5):
        i = jnp.where(c == 0, BLOCKS[0][k][0], BLOCKS[1][k][0])
        j = jnp.where(c == 0, BLOCKS[0][k][1], BLOCKS[1][k][1])
        a = stack[pl.ds(pl.multiple_of(i * TILE, TILE), TILE), :]
        b = stack[pl.ds(pl.multiple_of(j * TILE, TILE), TILE), :]
        out[k * TILE : (k + 1) * TILE, :] = dot32(a, b, ((1,), (1,))) * scale


def line(block, row):
    return jnp.broadcast_to(block[row : row + 1, :], (8, TILE))


def factor_tile(ref, origin):
    lane = lax.broadcasted_iota(jnp.int32, (8, TILE), 1)
    sub = lax.broadcasted_iota(jnp.int32, (8, TILE), 0)
    lanes = slice(origin, origin + TILE)
    halves = range(GROUP // 8)
    for base in range(0, TILE, GROUP):
        inside = (lane >= base) & (lane < base + GROUP)
        place = [slice(origin + base + 8 * h, origin + base + 8 * h + 8) for h in halves]
        rows = [ref[place[h], lanes] for h in halves]
        col = [
            [jnp.broadcast_to(rows[h][:, base + k : base + k + 1], (8, TILE)) for k in range(GROUP)]
            for h in halves
        ]
        start = [
            jnp.where(inside, jnp.where(lane - base == sub + 8 * h, 1.0, 0.0), rows[h]) for h in halves
        ]
        low, full = list(start), list(start)
        scale = [jnp.zeros((8, TILE), jnp.float32) for _ in halves]
        for j in range(GROUP):
            h, r = divmod(j, 8)
            at = sub == r
            pivot = line(col[h][j], r)
            inv = 1.0 / pivot
            scale[h] = jnp.where(at, lax.rsqrt(pivot), scale[h])
            mine = [col[i][j] for i in halves]
            for k in range(j + 1, GROUP):
                ratio = line(col[h][k], r) * inv
                for i in halves:
                    new = col[i][k] - mine[i] * ratio
                    col[i][k] = jnp.where(at, ratio, new) if i == h else new
            ratio = line(low[h], r) * inv
            for i in range(h, GROUP // 8):
                low[i] = low[i] - (jnp.where(sub > r, mine[i], 0.0) if i == h else mine[i]) * ratio
            ratio = line(full[h], r) * inv
            for i in halves:
                new = full[i] - mine[i] * ratio
                full[i] = jnp.where(at, ratio, new) if i == h else new
        for h in halves:
            ref[place[h], lanes] = jnp.where(lane < base + GROUP, low[h] * scale[h], 0.0)
        for q in range(base + GROUP, TILE, 8):
            rest = ref[origin + q : origin + q + 8, lanes]
            acc = jnp.where(inside, 0.0, rest)
            for m in range(GROUP):
                acc = acc - jnp.broadcast_to(rest[:, base + m : base + m + 1], (8, TILE)) * line(
                    full[m // 8], m % 8
                )
            ref[origin + q : origin + q + 8, lanes] = acc


def factor_kernel(place, own, other, corr, weights, work):
    first = place[0] == 0
    for k in range(5):
        rows = slice(k * TILE, (k + 1) * TILE)
        a, b = own[rows, :], other[rows, :]
        for blocks, block in ((BLOCKS[0], jnp.where(first, a, b)), (BLOCKS[1], jnp.where(first, b, a))):
            i, j = blocks[k]
            corr[i * TILE : (i + 1) * TILE, j * TILE : (j + 1) * TILE] = block
            if i != j:
                corr[j * TILE : (j + 1) * TILE, i * TILE : (i + 1) * TILE] = block.T
    work[...] = corr[...]
    count = work.shape[0]
    for k in range(0, count, TILE):
        own_rows = slice(k, k + TILE)
        factor_tile(work, k)
        inverse = work[own_rows, own_rows]
        for side in (slice(0, k), slice(k + TILE, count)):
            if side.start < side.stop:
                work[own_rows, side] = dot32(inverse, work[own_rows, side], ((1,), (0,)))
        for r in range(k + TILE, count, TILE):
            rows = slice(r, r + TILE)
            lower = work[own_rows, rows].T
            for side in (slice(r, count), slice(0, k)):
                if side.start < side.stop:
                    work[rows, side] = work[rows, side] - dot32(lower, work[own_rows, side], ((1,), (0,)))
            work[rows, own_rows] = -dot32(lower, inverse, ((1,), (0,)))
    size = weights.shape[0]
    begin = pl.multiple_of(place[1] * size, size)
    limit = (place[1] * size // TILE + 1) * TILE
    column = lax.broadcasted_iota(jnp.int32, (size, count), 1)
    weights[...] = jnp.where(column < limit, work[pl.ds(begin, size), :], 0.0)


def rotate_kernel(weights, fields, out):
    for t in range(fields.shape[0] // 2):
        for h in range(2):
            out[t, :, h * TILE : (h + 1) * TILE] = dot32(
                weights[...], fields[2 * t + h], ((1,), (0,))
            )


VMEM = pl.BlockSpec(memory_space=pltpu.VMEM)
SMEM = pl.BlockSpec(memory_space=pltpu.SMEM)
PARAMS = pltpu.CompilerParams(vmem_limit_bytes=48 << 20)


def ring(axes, step):
    count = lax.axis_size(axes)
    return [(i, (i + step) % count) for i in range(count)]


def flip(axes, bits):
    return [(i, i ^ bits) for i in range(lax.axis_size(axes))]


def per_device(orbitals, potential):
    planes, rows, cells = orbitals.shape
    place = jnp.stack([lax.axis_index("c"), lax.axis_index(BAND)]).astype(jnp.int32)
    own = orbitals.reshape(planes * rows, cells)
    packed = jnp.concatenate([own, potential], axis=0)
    low = lax.ppermute(packed, SPACE, ring(SPACE, 1))
    high = lax.ppermute(packed, SPACE, ring(SPACE, -1))
    second = pl.pallas_call(
        functools.partial(filter_kernel, rows, planes),
        out_shape=jax.ShapeDtypeStruct((2 * planes, rows, TILE), jnp.float32),
        in_specs=[VMEM] * 5,
        out_specs=VMEM,
        scratch_shapes=[pltpu.VMEM(((planes + 2 * RADIUS) * rows, cells), jnp.float32)],
        compiler_params=PARAMS,
        name="filter",
    )(low, own, potential, high, jnp.asarray(plane_matrix()))

    team = lax.axis_size(TEAM)
    mine = lax.all_to_all(second.reshape(team, 2 * planes // team, rows, TILE), TEAM, 0, 0)
    theirs = lax.ppermute(mine, ("c",), flip("c", 1))
    count = 2 * team * rows
    total = float(planes * lax.axis_size(SPACE) * cells)
    part = pl.pallas_call(
        functools.partial(gram_kernel, 1.0 / total),
        out_shape=jax.ShapeDtypeStruct((5 * TILE, TILE), jnp.float32),
        in_specs=[SMEM, VMEM, VMEM],
        out_specs=VMEM,
        scratch_shapes=[pltpu.VMEM((count, mine.shape[1] * TILE), jnp.float32)],
        compiler_params=PARAMS,
        name="gram",
    )(place, mine, theirs)

    piece = lax.all_to_all(part.reshape(team, 5 * TILE // team, TILE), TEAM, 0, 0).sum(0)
    for bits in ((1, 2, 3), (4, 8, 12)):
        got = [lax.ppermute(piece, SPACE, flip(SPACE, b)) for b in bits]
        piece = (piece + got[0]) + (got[1] + got[2])
    spread = lax.all_to_all(jnp.broadcast_to(piece, (team,) + piece.shape), TEAM, 0, 0)
    mine_g = spread.reshape(5 * TILE, TILE)
    theirs_g = lax.ppermute(mine_g, ("c",), flip("c", 1))
    correlation, weights = pl.pallas_call(
        factor_kernel,
        out_shape=(
            jax.ShapeDtypeStruct((count, count), jnp.float32),
            jax.ShapeDtypeStruct((rows, count), jnp.float32),
        ),
        in_specs=[SMEM, VMEM, VMEM],
        out_specs=(VMEM, VMEM),
        scratch_shapes=[pltpu.VMEM((count, count), jnp.float32)],
        compiler_params=PARAMS,
        name="factor",
    )(place, mine_g, theirs_g)

    fields = lax.all_gather(second, BAND, axis=1, tiled=True)
    steps = 4
    rotated = pl.pallas_call(
        rotate_kernel,
        out_shape=jax.ShapeDtypeStruct((planes, rows, cells), jnp.float32),
        grid=(steps,),
        in_specs=[
            pl.BlockSpec((rows, count), lambda i: (0, 0)),
            pl.BlockSpec((2 * planes // steps, count, TILE), lambda i: (i, 0, 0)),
        ],
        out_specs=pl.BlockSpec((planes // steps, rows, cells), lambda i: (i, 0, 0)),
        compiler_params=PARAMS,
        name="rotate",
    )(weights, fields)
    return (rotated, correlation)


def solution(mesh):
    fine = Mesh(mesh.devices.reshape(8, 2, 4, 2, 2), ("z", "xh", "y", "xl", "c"))
    return jax.shard_map(
        per_device,
        mesh=fine,
        in_specs=(P(SPACE, BAND, None), P(SPACE, None)),
        out_specs=(P(SPACE, BAND, None), P()),
        check_vma=False,
    )
```

profile of v0, /device:TPU:1, one launch (start us, length us, event | category | flops | bytes accessed | tf_op | source)
XLA Modules:
  0.0 134.9 jit_solution(17487145656062028289)
XLA Ops:
  7.2 0.0 all-gather.2.cloned.1.call-start
  7.2 1.0 pad_maximum_fusion
  8.3 3.7 %collective-permute-start = (f32[396,256]{1,0:T(8,128)S(1)}, f32[396,256]{1,0:T(8,128)S(1)}, u32[]{:S(2)}, u32[]{:S(2)}) collective-permute-start(f32[396,256]{1,0:T(8,128)S(1)} %pad_maximum_fusion), channel_id=1, source_target_pairs={{0,16},{16,32},{32,48},{48,64},{64,80},{80,96},{96,112},{112,128},... | collective-permute-start | bytes 1216520 | tf_op jit(solution)/shard_map/ppermute | solution.py:220
  11.9 5.4 %collective-permute-start.1 = (f32[396,256]{1,0:T(8,128)S(1)}, f32[396,256]{1,0:T(8,128)S(1)}, u32[]{:S(2)}, u32[]{:S(2)}) collective-permute-start(f32[396,256]{1,0:T(8,128)S(1)} %pad_maximum_fusion), channel_id=1, source_target_pairs={{0,240},{16,0},{32,16},{48,32},{64,48},{80,64},{96,80},{112,96},{1... | collective-permute-start | bytes 1216520 | tf_op jit(solution)/shard_map/ppermute | solution.py:221
  17.3 11.5 %collective-permute-done.low = f32[396,256]{1,0:T(8,128)S(1)} collective-permute-done((f32[396,256]{1,0:T(8,128)S(1)}, f32[396,256]{1,0:T(8,128)S(1)}, u32[]{:S(2)}, u32[]{:S(2)}) %collective-permute-start) | collective-permute-done | bytes 405536 | tf_op jit(solution)/shard_map/ppermute | solution.py:220
  28.8 3.4 %collective-permute-done.1.high = f32[396,256]{1,0:T(8,128)S(1)} collective-permute-done((f32[396,256]{1,0:T(8,128)S(1)}, f32[396,256]{1,0:T(8,128)S(1)}, u32[]{:S(2)}, u32[]{:S(2)}) %collective-permute-start.1) | collective-permute-done | bytes 405536 | tf_op jit(solution)/shard_map/ppermute | solution.py:221
  32.2 0.0 copy-start
  32.2 1.0 copy-done
  33.2 0.0 copy-start.1
  33.2 0.9 copy-done.1
  34.2 0.0 copy-start.2
  34.2 0.7 copy-done.2
  34.9 2.6 %filter.1 = f32[24,32,128]{2,1,0:T(8,128)} custom-call(f32[396,256]{1,0:T(8,128)S(1)} %collective-permute-done.low, f32[384,256]{1,0:T(8,128)S(1)} %bitcast.7, f32[12,256]{1,0:T(8,128)S(1)} %copy-done.2, f32[396,256]{1,0:T(8,128)S(1)} %collective-permute-done.1.high, f32[256,256]{1,0:T(8,128)S(1)} %copy-done.1), custom_call_target="tpu_custom_call" | custom-call | tf_op jit(solution)/shard_map/filter/pallas_call | solution.py:222
  37.5 0.0 all-gather.2.cloned.1.call-update
  37.5 11.3 %all_to_all.15.own = f32[8,3,32,128]{3,2,1,0:T(8,128)S(1)} all-to-all(f32[8,3,32,128]{3,2,1,0:T(8,128)} %bitcast.3), channel_id=1, replica_groups=mesh['z'=8,'xh'=2,'y'=4,'xl'=2,'c'=2] {'y','xl'}, dimensions={0} | all-to-all | bytes 786432 | tf_op jit(solution)/shard_map/all_to_all | solution.py:233
  48.8 3.2 %collective-permute-start.2 = (f32[8,3,32,128]{3,2,1,0:T(8,128)S(1)}, f32[8,3,32,128]{3,2,1,0:T(8,128)S(1)}, u32[]{:S(2)}, u32[]{:S(2)}) collective-permute-start(f32[8,3,32,128]{3,2,1,0:T(8,128)S(1)} %all_to_all.15.own), channel_id=1, source_target_pairs={{0,1},{1,0},{2,3},{3,2},{4,5},{5,4},{6,7},{7,6},{8,9},{9,8},{10,11... | collective-permute-start | bytes 1179656 | tf_op jit(solution)/shard_map/ppermute | solution.py:234
  52.0 0.1 pad_add_fusion.place
  52.1 1.3 collective-permute-done.2.other
  53.4 1.9 %gram.1 = f32[640,128]{1,0:T(8,128)S(1)} custom-call(s32[2]{0:T(128)S(1)} %pad_add_fusion.place, f32[8,3,32,128]{3,2,1,0:T(8,128)S(1)} %all_to_all.15.own, f32[8,3,32,128]{3,2,1,0:T(8,128)S(1)} %collective-permute-done.2.other), custom_call_target="tpu_custom_call" | custom-call | tf_op jit(solution)/shard_map/gram/pallas_call | solution.py:237
  55.3 13.8 %all_to_all.16 = f32[8,80,128]{2,1,0:T(8,128)S(1)} all-to-all(f32[8,80,128]{2,1,0:T(8,128)S(1)} %bitcast.10), channel_id=1, replica_groups=mesh['z'=8,'xh'=2,'y'=4,'xl'=2,'c'=2] {'y','xl'}, dimensions={0} | all-to-all | bytes 655360 | tf_op jit(solution)/shard_map/all_to_all | solution.py:247
  69.1 0.7 collective-permute-start.3
  69.8 1.6 %collective-permute-start.4 = (f32[80,128]{1,0:T(8,128)S(1)}, f32[80,128]{1,0:T(8,128)S(1)}, u32[]{:S(2)}, u32[]{:S(2)}) collective-permute-start(f32[80,128]{1,0:T(8,128)S(1)} %reduce_sum.9), channel_id=1, source_target_pairs={{0,32},{16,48},{32,0},{48,16},{64,96},{80,112},{96,64},{112,80},{1... | collective-permute-start | bytes 122888 | tf_op jit(solution)/shard_map/ppermute | solution.py:249
  71.5 2.0 %collective-permute-start.5 = (f32[80,128]{1,0:T(8,128)S(1)}, f32[80,128]{1,0:T(8,128)S(1)}, u32[]{:S(2)}, u32[]{:S(2)}) collective-permute-start(f32[80,128]{1,0:T(8,128)S(1)} %reduce_sum.9), channel_id=1, source_target_pairs={{0,48},{16,32},{32,16},{48,0},{64,112},{80,96},{96,80},{112,64},{1... | collective-permute-start | bytes 122888 | tf_op jit(solution)/shard_map/ppermute | solution.py:249
  73.5 0.8 collective-permute-done.3
  74.2 0.0 collective-permute-done.4
  74.2 2.6 %collective-permute-done.5 = f32[80,128]{1,0:T(8,128)S(1)} collective-permute-done((f32[80,128]{1,0:T(8,128)S(1)}, f32[80,128]{1,0:T(8,128)S(1)}, u32[]{:S(2)}, u32[]{:S(2)}) %collective-permute-start.5) | collective-permute-done | bytes 40992 | tf_op jit(solution)/shard_map/ppermute | solution.py:249
  76.9 3.8 %collective-permute-start.6 = (f32[80,128]{1,0:T(8,128)S(1)}, f32[80,128]{1,0:T(8,128)S(1)}, u32[]{:S(2)}, u32[]{:S(2)}) collective-permute-start(f32[80,128]{1,0:T(8,128)S(1)} %add_add_fusion.1), channel_id=1, source_target_pairs={{0,64},{16,80},{32,96},{48,112},{64,0},{80,16},{96,32},{112,48},{1... | collective-permute-start | bytes 122888 | tf_op jit(solution)/shard_map/ppermute | solution.py:249
  80.7 3.4 %collective-permute-start.7 = (f32[80,128]{1,0:T(8,128)S(1)}, f32[80,128]{1,0:T(8,128)S(1)}, u32[]{:S(2)}, u32[]{:S(2)}) collective-permute-start(f32[80,128]{1,0:T(8,128)S(1)} %add_add_fusion.1), channel_id=1, source_target_pairs={{0,128},{16,144},{32,160},{48,176},{64,192},{80,208},{96,224},{112... | collective-permute-start | bytes 122888 | tf_op jit(solution)/shard_map/ppermute | solution.py:249
  84.1 0.0 collective-permute-start.8
  84.1 0.0 collective-permute-done.6
  84.1 3.3 %collective-permute-done.7 = f32[80,128]{1,0:T(8,128)S(1)} collective-permute-done((f32[80,128]{1,0:T(8,128)S(1)}, f32[80,128]{1,0:T(8,128)S(1)}, u32[]{:S(2)}, u32[]{:S(2)}) %collective-permute-start.7) | collective-permute-done | bytes 40992 | tf_op jit(solution)/shard_map/ppermute | solution.py:249
  87.4 2.2 %collective-permute-done.8 = f32[80,128]{1,0:T(8,128)S(1)} collective-permute-done((f32[80,128]{1,0:T(8,128)S(1)}, f32[80,128]{1,0:T(8,128)S(1)}, u32[]{:S(2)}, u32[]{:S(2)}) %collective-permute-start.8) | collective-permute-done | bytes 40992 | tf_op jit(solution)/shard_map/ppermute | solution.py:249
  89.7 9.0 %all_to_all.17 = f32[8,80,128]{2,1,0:T(8,128)S(1)} all-to-all(f32[8,80,128]{2,1,0:T(8,128)S(1)} %broadcast_in_dim.3), channel_id=1, replica_groups=mesh['z'=8,'xh'=2,'y'=4,'xl'=2,'c'=2] {'y','xl'}, dimensions={0} | all-to-all | bytes 655360 | tf_op jit(solution)/shard_map/all_to_all | solution.py:251
  98.7 5.5 %collective-permute-start.9 = (f32[640,128]{1,0:T(8,128)S(1)}, f32[640,128]{1,0:T(8,128)S(1)}, u32[]{:S(2)}, u32[]{:S(2)}) collective-permute-start(f32[640,128]{1,0:T(8,128)S(1)} %bitcast.8), channel_id=1, source_target_pairs={{0,1},{1,0},{2,3},{3,2},{4,5},{5,4},{6,7},{7,6},{8,9},{9,8},{10,11... | collective-permute-start | bytes 983048 | tf_op jit(solution)/shard_map/ppermute | solution.py:253
  104.2 1.3 collective-permute-done.9.other
  105.5 16.6 %factor.1 = (f32[512,512]{1,0:T(8,128)}, f32[32,512]{1,0:T(8,128)S(1)}) custom-call(s32[2]{0:T(128)S(1)} %pad_add_fusion.place, f32[640,128]{1,0:T(8,128)S(1)} %bitcast.9, f32[640,128]{1,0:T(8,128)S(1)} %collective-permute-done.9.other), custom_call_target="tpu_custom_call" | custom-call | tf_op jit(solution)/shard_map/factor/pallas_call | solution.py:254
  122.1 0.0 all-gather.2.cloned.1.call-done.fields
  122.1 6.0 %rotate.1 = f32[12,32,256]{2,1,0:T(8,128)} custom-call(f32[32,512]{1,0:T(8,128)S(1)} %get-tuple-element.4.weights, f32[24,512,128]{2,1,0:T(8,128)} %all-gather.2.cloned.1.call-done.fields), custom_call_target="tpu_custom_call" | custom-call | tf_op jit(solution)/shard_map/rotate/pallas_call | solution.py:269
  (4 shorter events, 0.1 us)
Async XLA Ops:
  7.2 114.9 %all-gather.2.cloned.1.call-start = ((), (), s32[]{:S(2)}) async-start(), calls=%async_computation.3 | async-start | bytes 6684672 | tf_op jit(solution)/shard_map/all_gather | solution.py:267
  8.3 20.6 %collective-permute-start = (f32[396,256]{1,0:T(8,128)S(1)}, f32[396,256]{1,0:T(8,128)S(1)}, u32[]{:S(2)}, u32[]{:S(2)}) collective-permute-start(f32[396,256]{1,0:T(8,128)S(1)} %pad_maximum_fusion), channel_id=1, source_target_pairs={{0,16},{16,32},{32,48},{48,64},{64,80},{80,96},{96,112},{112,128},... | collective-permute-start | bytes 1216520 | tf_op jit(solution)/shard_map/ppermute | solution.py:220
  11.9 20.3 %collective-permute-start.1 = (f32[396,256]{1,0:T(8,128)S(1)}, f32[396,256]{1,0:T(8,128)S(1)}, u32[]{:S(2)}, u32[]{:S(2)}) collective-permute-start(f32[396,256]{1,0:T(8,128)S(1)} %pad_maximum_fusion), channel_id=1, source_target_pairs={{0,240},{16,0},{32,16},{48,32},{64,48},{80,64},{96,80},{112,96},{1... | collective-permute-start | bytes 1216520 | tf_op jit(solution)/shard_map/ppermute | solution.py:221
  32.2 1.0 copy-start
  33.2 0.9 copy-start.1
  34.2 0.7 copy-start.2
  48.8 4.6 %collective-permute-start.2 = (f32[8,3,32,128]{3,2,1,0:T(8,128)S(1)}, f32[8,3,32,128]{3,2,1,0:T(8,128)S(1)}, u32[]{:S(2)}, u32[]{:S(2)}) collective-permute-start(f32[8,3,32,128]{3,2,1,0:T(8,128)S(1)} %all_to_all.15.own), channel_id=1, source_target_pairs={{0,1},{1,0},{2,3},{3,2},{4,5},{5,4},{6,7},{7,6},{8,9},{9,8},{10,11... | collective-permute-start | bytes 1179656 | tf_op jit(solution)/shard_map/ppermute | solution.py:234
  69.1 5.1 %collective-permute-start.3 = (f32[80,128]{1,0:T(8,128)S(1)}, f32[80,128]{1,0:T(8,128)S(1)}, u32[]{:S(2)}, u32[]{:S(2)}) collective-permute-start(f32[80,128]{1,0:T(8,128)S(1)} %reduce_sum.9), channel_id=1, source_target_pairs={{0,16},{16,0},{32,48},{48,32},{64,80},{80,64},{96,112},{112,96},{1... | collective-permute-start | bytes 122888 | tf_op jit(solution)/shard_map/ppermute | solution.py:249
  69.8 4.4 %collective-permute-start.4 = (f32[80,128]{1,0:T(8,128)S(1)}, f32[80,128]{1,0:T(8,128)S(1)}, u32[]{:S(2)}, u32[]{:S(2)}) collective-permute-start(f32[80,128]{1,0:T(8,128)S(1)} %reduce_sum.9), channel_id=1, source_target_pairs={{0,32},{16,48},{32,0},{48,16},{64,96},{80,112},{96,64},{112,80},{1... | collective-permute-start | bytes 122888 | tf_op jit(solution)/shard_map/ppermute | solution.py:249
  71.5 5.4 %collective-permute-start.5 = (f32[80,128]{1,0:T(8,128)S(1)}, f32[80,128]{1,0:T(8,128)S(1)}, u32[]{:S(2)}, u32[]{:S(2)}) collective-permute-start(f32[80,128]{1,0:T(8,128)S(1)} %reduce_sum.9), channel_id=1, source_target_pairs={{0,48},{16,32},{32,16},{48,0},{64,112},{80,96},{96,80},{112,64},{1... | collective-permute-start | bytes 122888 | tf_op jit(solution)/shard_map/ppermute | solution.py:249
  76.9 7.3 %collective-permute-start.6 = (f32[80,128]{1,0:T(8,128)S(1)}, f32[80,128]{1,0:T(8,128)S(1)}, u32[]{:S(2)}, u32[]{:S(2)}) collective-permute-start(f32[80,128]{1,0:T(8,128)S(1)} %add_add_fusion.1), channel_id=1, source_target_pairs={{0,64},{16,80},{32,96},{48,112},{64,0},{80,16},{96,32},{112,48},{1... | collective-permute-start | bytes 122888 | tf_op jit(solution)/shard_map/ppermute | solution.py:249
  80.7 6.8 %collective-permute-start.7 = (f32[80,128]{1,0:T(8,128)S(1)}, f32[80,128]{1,0:T(8,128)S(1)}, u32[]{:S(2)}, u32[]{:S(2)}) collective-permute-start(f32[80,128]{1,0:T(8,128)S(1)} %add_add_fusion.1), channel_id=1, source_target_pairs={{0,128},{16,144},{32,160},{48,176},{64,192},{80,208},{96,224},{112... | collective-permute-start | bytes 122888 | tf_op jit(solution)/shard_map/ppermute | solution.py:249
  84.1 5.5 %collective-permute-start.8 = (f32[80,128]{1,0:T(8,128)S(1)}, f32[80,128]{1,0:T(8,128)S(1)}, u32[]{:S(2)}, u32[]{:S(2)}) collective-permute-start(f32[80,128]{1,0:T(8,128)S(1)} %add_add_fusion.1), channel_id=1, source_target_pairs={{0,192},{16,208},{32,224},{48,240},{64,128},{80,144},{96,160},{112... | collective-permute-start | bytes 122888 | tf_op jit(solution)/shard_map/ppermute | solution.py:249
  98.7 6.8 %collective-permute-start.9 = (f32[640,128]{1,0:T(8,128)S(1)}, f32[640,128]{1,0:T(8,128)S(1)}, u32[]{:S(2)}, u32[]{:S(2)}) collective-permute-start(f32[640,128]{1,0:T(8,128)S(1)} %bitcast.8), channel_id=1, source_target_pairs={{0,1},{1,0},{2,3},{3,2},{4,5},{5,4},{6,7},{7,6},{8,9},{9,8},{10,11... | collective-permute-start | bytes 983048 | tf_op jit(solution)/shard_map/ppermute | solution.py:253
Sparse Core Ops, SparseCore 0:
  37.6 52.1 all-gather.1
where the time goes:
time: 135 us
  blocking collectives  34.1 us (25%)
  starting transfers between devices  29.4 us (22%)
  Pallas kernels  27.2 us (20%)
  waiting for transfers between devices  26.3 us (19%)
  between operations  14.1 us (10%)
  local copies, waits for them, and re-layouts  2.69 us (2%)
    pallas_call x1, Pallas kernels, per_device(): pl.pallas_call(factor_kernel, out_shape=(jax.ShapeDtypeStruct((count, cou...  16.6 us
    all_to_all x1, blocking collectives, per_device(): lax.all_to_all(part.reshape(team, 5 * TILE // team, TILE), TEAM, 0, 0)  13.8 us
    ppermute x6, starting transfers between devices, per_device(): got = [lax.ppermute(piece, SPACE, flip(SPACE, b)) for b in bits]  11.6 us
    ppermute x1, waiting for transfers between devices, per_device(): low = lax.ppermute(packed, SPACE, ring(SPACE, 1))  11.5 us
    all_to_all x1, blocking collectives, per_device(): lax.all_to_all(second.reshape(team, 2 * planes // team, rows, TILE), TEAM...  11.3 us
    all_to_all x1, blocking collectives, per_device(): lax.all_to_all(jnp.broadcast_to(piece, (team,) + piece.shape), TEAM, 0, 0)  8.98 us
    ppermute x6, waiting for transfers between devices, per_device(): got = [lax.ppermute(piece, SPACE, flip(SPACE, b)) for b in bits]  8.88 us
    pallas_call x1, Pallas kernels, per_device(): pl.pallas_call(rotate_kernel, out_shape=jax.ShapeDtypeStruct((planes, row...  5.98 us
  transfers between devices with their start and end apart: 11, of which 8 were waited for; matrix products, arithmetic and copies ran while one was open for 0% of the time, Pallas kernels for 14%

commit v1 on v0

--- a/solution.py
+++ b/solution.py
@@ -47,7 +47,14 @@
     )
 
 
-def filter_kernel(rows, planes, low, own, pot, high, mat, out, first):
+def filter_kernel(rows, planes, low_hbm, own, pot, high_hbm, mat, out, first, low, high, sem):
+    copies = [
+        pltpu.make_async_copy(src, dst, sem.at[i])
+        for i, (src, dst) in enumerate(((low_hbm, low), (high_hbm, high)))
+    ]
+    for copy in copies:
+        copy.start()
+
     def field(p):
         if p < planes:
             return low[p * rows : (p + 1) * rows, :]
@@ -65,8 +72,10 @@
         return (row - SHIFT_MID) / HALF_SPAN
 
     half = RADIUS * rows
+    first[half : half + planes * rows, :] = dot32(own[...], mat[...], ((1,), (0,)))
+    for copy in copies:
+        copy.wait()
     first[0:half, :] = dot32(low[(planes - RADIUS) * rows : planes * rows, :], mat[...], ((1,), (0,)))
-    first[half : half + planes * rows, :] = dot32(own[...], mat[...], ((1,), (0,)))
     first[half + planes * rows :, :] = dot32(high[0:half, :], mat[...], ((1,), (0,)))
     for q in range(planes + 2 * RADIUS):
         p = q + planes - RADIUS
@@ -157,7 +166,7 @@
             ref[origin + q : origin + q + 8, lanes] = acc
 
 
-def factor_kernel(place, own, other, corr, weights, work):
+def factor_kernel(place, own, other, fields, corr, out, work):
     first = place[0] == 0
     for k in range(5):
         rows = slice(k * TILE, (k + 1) * TILE)
@@ -169,6 +178,8 @@
                 corr[j * TILE : (j + 1) * TILE, i * TILE : (i + 1) * TILE] = block.T
     work[...] = corr[...]
     count = work.shape[0]
+    size = out.shape[2]
+    pairs = TILE // (2 * size)
     for k in range(0, count, TILE):
         own_rows = slice(k, k + TILE)
         factor_tile(work, k)
@@ -176,6 +187,14 @@
         for side in (slice(0, k), slice(k + TILE, count)):
             if side.start < side.stop:
                 work[own_rows, side] = dot32(inverse, work[own_rows, side], ((1,), (0,)))
+        mine = [
+            work[pl.ds(pl.multiple_of(k + 2 * i * size + place[0] * size, size), size), 0 : k + TILE]
+            for i in range(pairs)
+        ]
+        turned = dot32(jnp.concatenate(mine, axis=0), fields[0 : k + TILE, :], ((1,), (0,)))
+        for i in range(pairs):
+            for t in range(out.shape[1]):
+                out[k // TILE * pairs + i, t] = turned[i * size : (i + 1) * size, t * TILE : (t + 1) * TILE]
         for r in range(k + TILE, count, TILE):
             rows = slice(r, r + TILE)
             lower = work[own_rows, rows].T
@@ -183,22 +202,10 @@
                 if side.start < side.stop:
                     work[rows, side] = work[rows, side] - dot32(lower, work[own_rows, side], ((1,), (0,)))
             work[rows, own_rows] = -dot32(lower, inverse, ((1,), (0,)))
-    size = weights.shape[0]
-    begin = pl.multiple_of(place[1] * size, size)
-    limit = (place[1] * size // TILE + 1) * TILE
-    column = lax.broadcasted_iota(jnp.int32, (size, count), 1)
-    weights[...] = jnp.where(column < limit, work[pl.ds(begin, size), :], 0.0)
-
-
-def rotate_kernel(weights, fields, out):
-    for t in range(fields.shape[0] // 2):
-        for h in range(2):
-            out[t, :, h * TILE : (h + 1) * TILE] = dot32(
-                weights[...], fields[2 * t + h], ((1,), (0,))
-            )
 
 
 VMEM = pl.BlockSpec(memory_space=pltpu.VMEM)
+ANY = pl.BlockSpec(memory_space=pl.ANY)
 SMEM = pl.BlockSpec(memory_space=pltpu.SMEM)
 PARAMS = pltpu.CompilerParams(vmem_limit_bytes=48 << 20)
 
@@ -214,7 +221,7 @@
 
 def per_device(orbitals, potential):
     planes, rows, cells = orbitals.shape
-    place = jnp.stack([lax.axis_index("c"), lax.axis_index(BAND)]).astype(jnp.int32)
+    place = lax.axis_index("c").astype(jnp.int32).reshape(1)
     own = orbitals.reshape(planes * rows, cells)
     packed = jnp.concatenate([own, potential], axis=0)
     low = lax.ppermute(packed, SPACE, ring(SPACE, 1))
@@ -222,9 +229,14 @@
     second = pl.pallas_call(
         functools.partial(filter_kernel, rows, planes),
         out_shape=jax.ShapeDtypeStruct((2 * planes, rows, TILE), jnp.float32),
-        in_specs=[VMEM] * 5,
+        in_specs=[ANY, VMEM, VMEM, ANY, VMEM],
         out_specs=VMEM,
-        scratch_shapes=[pltpu.VMEM(((planes + 2 * RADIUS) * rows, cells), jnp.float32)],
+        scratch_shapes=[
+            pltpu.VMEM(((planes + 2 * RADIUS) * rows, cells), jnp.float32),
+            pltpu.VMEM(packed.shape, jnp.float32),
+            pltpu.VMEM(packed.shape, jnp.float32),
+            pltpu.SemaphoreType.DMA((2,)),
+        ],
         compiler_params=PARAMS,
         name="filter",
     )(low, own, potential, high, jnp.asarray(plane_matrix()))
@@ -234,12 +246,14 @@
     theirs = lax.ppermute(mine, ("c",), flip("c", 1))
     count = 2 * team * rows
     total = float(planes * lax.axis_size(SPACE) * cells)
-    part = pl.pallas_call(
+    part, fields = pl.pallas_call(
         functools.partial(gram_kernel, 1.0 / total),
-        out_shape=jax.ShapeDtypeStruct((5 * TILE, TILE), jnp.float32),
+        out_shape=(
+            jax.ShapeDtypeStruct((5 * TILE, TILE), jnp.float32),
+            jax.ShapeDtypeStruct((count, mine.shape[1] * TILE), jnp.float32),
+        ),
         in_specs=[SMEM, VMEM, VMEM],
-        out_specs=VMEM,
-        scratch_shapes=[pltpu.VMEM((count, mine.shape[1] * TILE), jnp.float32)],
+        out_specs=(VMEM, VMEM),
         compiler_params=PARAMS,
         name="gram",
     )(place, mine, theirs)
@@ -251,34 +265,20 @@
     spread = lax.all_to_all(jnp.broadcast_to(piece, (team,) + piece.shape), TEAM, 0, 0)
     mine_g = spread.reshape(5 * TILE, TILE)
     theirs_g = lax.ppermute(mine_g, ("c",), flip("c", 1))
-    correlation, weights = pl.pallas_call(
+    correlation, turned = pl.pallas_call(
         factor_kernel,
         out_shape=(
             jax.ShapeDtypeStruct((count, count), jnp.float32),
-            jax.ShapeDtypeStruct((rows, count), jnp.float32),
+            jax.ShapeDtypeStruct(mine.shape, jnp.float32),
         ),
-        in_specs=[SMEM, VMEM, VMEM],
+        in_specs=[SMEM, VMEM, VMEM, VMEM],
         out_specs=(VMEM, VMEM),
         scratch_shapes=[pltpu.VMEM((count, count), jnp.float32)],
         compiler_params=PARAMS,
         name="factor",
-    )(place, mine_g, theirs_g)
-
-    fields = lax.all_gather(second, BAND, axis=1, tiled=True)
-    steps = 4
-    rotated = pl.pallas_call(
-        rotate_kernel,
-        out_shape=jax.ShapeDtypeStruct((planes, rows, cells), jnp.float32),
-        grid=(steps,),
-        in_specs=[
-            pl.BlockSpec((rows, count), lambda i: (0, 0)),
-            pl.BlockSpec((2 * planes // steps, count, TILE), lambda i: (i, 0, 0)),
-        ],
-        out_specs=pl.BlockSpec((planes // steps, rows, cells), lambda i: (i, 0, 0)),
-        compiler_params=PARAMS,
-        name="rotate",
-    )(weights, fields)
-    return (rotated, correlation)
+    )(place, mine_g, theirs_g, fields)
+    back = lax.all_to_all(turned, TEAM, 0, 0).reshape(planes, 2, rows, TILE)
+    return (back.transpose(0, 2, 1, 3).reshape(planes, rows, cells), correlation)
 
 
 def solution(mesh):

time: 135 us -> 120 us (0.89)
  between operations: 14.1 us -> 0.71 us
  Pallas kernels: 27.2 us -> 20.4 us
  blocking collectives: 34.1 us -> 40.8 us
  starting transfers between devices: 29.4 us -> 31.3 us
  local copies, waits for them, and re-layouts: 2.69 us -> 0.81 us
    all_to_all x0 -> x1, blocking collectives: none -> 10.8 us  [per_device(): back = lax.all_to_all(turned, TEAM, 0, 0).reshape(planes, 2, rows, TILE)]
    pallas_call x2 -> x1, Pallas kernels: 7.9 us -> 1.38 us  [per_device(): pl.pallas_call(functools.partial(gram_kernel, 1.0 / total), out_shape=(ja...]
    ppermute x1, waiting for transfers between devices: 11.5 us -> 5.45 us  [per_device(): low = lax.ppermute(packed, SPACE, ring(SPACE, 1))]
    ppermute x1, waiting for transfers between devices: 3.39 us -> 8.17 us  [per_device(): high = lax.ppermute(packed, SPACE, ring(SPACE, -1))]
    all_to_all x1, blocking collectives: 13.8 us -> 9.94 us  [per_device(): lax.all_to_all(part.reshape(team, 5 * TILE // team, TILE), TEAM, 0, 0)]
    ppermute x1, starting transfers between devices: 3.65 us -> 0.01 us  [per_device(): low = lax.ppermute(packed, SPACE, ring(SPACE, 1))]
    ppermute x1, starting transfers between devices: 5.38 us -> 8.94 us  [per_device(): high = lax.ppermute(packed, SPACE, ring(SPACE, -1))]
    unnamed x6, local copies, waits for them, and re-layouts: 2.66 us -> 0.02 us
  transfers between devices with their start and end apart: 11 -> 10, of which waited for: 8 -> 8; matrix products, arithmetic and copies ran while one was open for 0% -> 0% of each run, Pallas kernels for 14% -> 0%
where the time goes in v1:
time: 120 us
  blocking collectives  40.8 us (34%)
  starting transfers between devices  31.3 us (26%)
  waiting for transfers between devices  25 us (21%)
  Pallas kernels  20.4 us (17%)
    pallas_call x1, Pallas kernels, per_device(): pl.pallas_call(factor_kernel, out_shape=(jax.ShapeDtypeStruct((count, cou...  16.6 us
    ppermute x6, starting transfers between devices, per_device(): got = [lax.ppermute(piece, SPACE, flip(SPACE, b)) for b in bits]  13.7 us
    all_to_all x1, blocking collectives, per_device(): lax.all_to_all(second.reshape(team, 2 * planes // team, rows, TILE), TEAM...  11.1 us
    all_to_all x1, blocking collectives, per_device(): back = lax.all_to_all(turned, TEAM, 0, 0).reshape(planes, 2, rows, TILE)  10.8 us
    all_to_all x1, blocking collectives, per_device(): lax.all_to_all(part.reshape(team, 5 * TILE // team, TILE), TEAM, 0, 0)  9.94 us
    all_to_all x1, blocking collectives, per_device(): lax.all_to_all(jnp.broadcast_to(piece, (team,) + piece.shape), TEAM, 0, 0)  8.98 us
    ppermute x1, starting transfers between devices, per_device(): high = lax.ppermute(packed, SPACE, ring(SPACE, -1))  8.94 us
    ppermute x6, waiting for transfers between devices, per_device(): got = [lax.ppermute(piece, SPACE, flip(SPACE, b)) for b in bits]  8.81 us
  transfers between devices with their start and end apart: 10, of which 8 were waited for; matrix products, arithmetic and copies ran while one was open for 0% of the time, Pallas kernels for 0%

profile of v1, /device:TPU:1, one launch (start us, length us, event | category | flops | bytes accessed | tf_op | source)
XLA Modules:
  0.0 120.2 jit_solution(17067556887209043685)
XLA Ops:
  0.6 0.0 copy-start
  0.6 0.0 copy-start.1
  0.7 0.0 copy-start.2
  0.7 1.1 pad_maximum_fusion
  1.8 8.9 %collective-permute-start.1 = (f32[396,256]{1,0:T(8,128)S(1)}, f32[396,256]{1,0:T(8,128)S(1)}, u32[]{:S(2)}, u32[]{:S(2)}) collective-permute-start(f32[396,256]{1,0:T(8,128)S(1)} %pad_maximum_fusion), channel_id=1, source_target_pairs={{0,240},{16,0},{32,16},{48,32},{64,48},{80,64},{96,80},{112,96},{1... | collective-permute-start | bytes 1216520 | tf_op jit(solution)/shard_map/ppermute | solution.py:228
  10.7 0.0 collective-permute-start
  10.7 8.2 %collective-permute-done.1.high_hbm = f32[396,256]{1,0:T(8,128)S(1)} collective-permute-done((f32[396,256]{1,0:T(8,128)S(1)}, f32[396,256]{1,0:T(8,128)S(1)}, u32[]{:S(2)}, u32[]{:S(2)}) %collective-permute-start.1) | collective-permute-done | bytes 405536 | tf_op jit(solution)/shard_map/ppermute | solution.py:228
  18.9 5.5 %collective-permute-done.low_hbm = f32[396,256]{1,0:T(8,128)S(1)} collective-permute-done((f32[396,256]{1,0:T(8,128)S(1)}, f32[396,256]{1,0:T(8,128)S(1)}, u32[]{:S(2)}, u32[]{:S(2)}) %collective-permute-start) | collective-permute-done | bytes 405536 | tf_op jit(solution)/shard_map/ppermute | solution.py:227
  24.3 0.0 copy-done
  24.3 0.0 copy-done.1
  24.3 0.0 copy-done.2
  24.4 2.4 %filter.1 = f32[24,32,128]{2,1,0:T(8,128)S(1)} custom-call(f32[396,256]{1,0:T(8,128)S(1)} %collective-permute-done.low_hbm, f32[384,256]{1,0:T(8,128)S(1)} %bitcast.13, f32[12,256]{1,0:T(8,128)S(1)} %copy-done.2, f32[396,256]{1,0:T(8,128)S(1)} %collective-permute-done.1.high_hbm, f32[256,256]{1,0:T(8,128)S(1)} %copy-done.1), custom_call_target="tpu_custom_call" | custom-call | tf_op jit(solution)/shard_map/filter/pallas_call | solution.py:229
  26.8 11.1 %all_to_all.20.own = f32[8,3,32,128]{3,2,1,0:T(8,128)S(1)} all-to-all(f32[8,3,32,128]{3,2,1,0:T(8,128)S(1)} %bitcast.14), channel_id=1, replica_groups=mesh['z'=8,'xh'=2,'y'=4,'xl'=2,'c'=2] {'y','xl'}, dimensions={0} | all-to-all | bytes 786432 | tf_op jit(solution)/shard_map/all_to_all | solution.py:245
  37.9 3.2 %collective-permute-start.2 = (f32[8,3,32,128]{3,2,1,0:T(8,128)S(1)}, f32[8,3,32,128]{3,2,1,0:T(8,128)S(1)}, u32[]{:S(2)}, u32[]{:S(2)}) collective-permute-start(f32[8,3,32,128]{3,2,1,0:T(8,128)S(1)} %all_to_all.20.own), channel_id=1, source_target_pairs={{0,1},{1,0},{2,3},{3,2},{4,5},{5,4},{6,7},{7,6},{8,9},{9,8},{10,11... | collective-permute-start | bytes 1179656 | tf_op jit(solution)/shard_map/ppermute | solution.py:246
  41.1 1.3 %collective-permute-done.2.other = f32[8,3,32,128]{3,2,1,0:T(8,128)S(1)} collective-permute-done((f32[8,3,32,128]{3,2,1,0:T(8,128)S(1)}, f32[8,3,32,128]{3,2,1,0:T(8,128)S(1)}, u32[]{:S(2)}, u32[]{:S(2)}) %collective-permute-start.2) | collective-permute-done | bytes 393248 | tf_op jit(solution)/shard_map/ppermute | solution.py:246
  42.4 1.4 %gram.1 = (f32[640,128]{1,0:T(8,128)S(1)}, f32[512,384]{1,0:T(8,128)S(1)}) custom-call(s32[1]{0:T(128)} %bitcast.place, f32[8,3,32,128]{3,2,1,0:T(8,128)S(1)} %all_to_all.20.own, f32[8,3,32,128]{3,2,1,0:T(8,128)S(1)} %collective-permute-done.2.other), custom_call_target="tpu_custom_call" | custom-call | tf_op jit(solution)/shard_map/gram/pallas_call | solution.py:249
  43.8 9.9 %all_to_all.21 = f32[8,80,128]{2,1,0:T(8,128)S(1)} all-to-all(f32[8,80,128]{2,1,0:T(8,128)S(1)} %bitcast.17), channel_id=1, replica_groups=mesh['z'=8,'xh'=2,'y'=4,'xl'=2,'c'=2] {'y','xl'}, dimensions={0} | all-to-all | bytes 655360 | tf_op jit(solution)/shard_map/all_to_all | solution.py:261
  53.8 5.2 %collective-permute-start.5 = (f32[80,128]{1,0:T(8,128)S(1)}, f32[80,128]{1,0:T(8,128)S(1)}, u32[]{:S(2)}, u32[]{:S(2)}) collective-permute-start(f32[80,128]{1,0:T(8,128)S(1)} %reduce_sum.9), channel_id=1, source_target_pairs={{0,48},{16,32},{32,16},{48,0},{64,112},{80,96},{96,80},{112,64},{1... | collective-permute-start | bytes 122888 | tf_op jit(solution)/shard_map/ppermute | solution.py:263
  59.0 0.0 collective-permute-start.4
  59.0 0.4 collective-permute-start.3
  59.3 1.0 collective-permute-done.5
  60.3 1.9 %collective-permute-done.4 = f32[80,128]{1,0:T(8,128)S(1)} collective-permute-done((f32[80,128]{1,0:T(8,128)S(1)}, f32[80,128]{1,0:T(8,128)S(1)}, u32[]{:S(2)}, u32[]{:S(2)}) %collective-permute-start.4) | collective-permute-done | bytes 40992 | tf_op jit(solution)/shard_map/ppermute | solution.py:263
  62.2 1.1 collective-permute-done.3
  63.3 5.9 %collective-permute-start.8 = (f32[80,128]{1,0:T(8,128)S(1)}, f32[80,128]{1,0:T(8,128)S(1)}, u32[]{:S(2)}, u32[]{:S(2)}) collective-permute-start(f32[80,128]{1,0:T(8,128)S(1)} %add_add_fusion.1), channel_id=1, source_target_pairs={{0,192},{16,208},{32,224},{48,240},{64,128},{80,144},{96,160},{112... | collective-permute-start | bytes 122888 | tf_op jit(solution)/shard_map/ppermute | solution.py:263
  69.3 1.0 collective-permute-start.7
  70.2 1.2 collective-permute-start.6
  71.5 0.0 collective-permute-done.8
  71.5 4.8 %collective-permute-done.7 = f32[80,128]{1,0:T(8,128)S(1)} collective-permute-done((f32[80,128]{1,0:T(8,128)S(1)}, f32[80,128]{1,0:T(8,128)S(1)}, u32[]{:S(2)}, u32[]{:S(2)}) %collective-permute-start.7) | collective-permute-done | bytes 40992 | tf_op jit(solution)/shard_map/ppermute | solution.py:263
  76.3 0.0 collective-permute-done.6
  76.3 9.0 %all_to_all.22 = f32[8,80,128]{2,1,0:T(8,128)S(1)} all-to-all(f32[8,80,128]{2,1,0:T(8,128)S(1)} %broadcast_in_dim.3), channel_id=1, replica_groups=mesh['z'=8,'xh'=2,'y'=4,'xl'=2,'c'=2] {'y','xl'}, dimensions={0} | all-to-all | bytes 655360 | tf_op jit(solution)/shard_map/all_to_all | solution.py:265
  85.3 5.5 %collective-permute-start.9 = (f32[640,128]{1,0:T(8,128)S(1)}, f32[640,128]{1,0:T(8,128)S(1)}, u32[]{:S(2)}, u32[]{:S(2)}) collective-permute-start(f32[640,128]{1,0:T(8,128)S(1)} %bitcast.15), channel_id=1, source_target_pairs={{0,1},{1,0},{2,3},{3,2},{4,5},{5,4},{6,7},{7,6},{8,9},{9,8},{10,11... | collective-permute-start | bytes 983048 | tf_op jit(solution)/shard_map/ppermute | solution.py:267
  90.8 1.3 %collective-permute-done.9.other = f32[640,128]{1,0:T(8,128)S(1)} collective-permute-done((f32[640,128]{1,0:T(8,128)S(1)}, f32[640,128]{1,0:T(8,128)S(1)}, u32[]{:S(2)}, u32[]{:S(2)}) %collective-permute-start.9) | collective-permute-done | bytes 327712 | tf_op jit(solution)/shard_map/ppermute | solution.py:267
  92.1 16.6 %factor.1 = (f32[512,512]{1,0:T(8,128)}, f32[8,3,32,128]{3,2,1,0:T(8,128)S(1)}) custom-call(s32[1]{0:T(128)} %bitcast.place, f32[640,128]{1,0:T(8,128)S(1)} %bitcast.16, f32[640,128]{1,0:T(8,128)S(1)} %collective-permute-done.9.other, f32[512,384]{1,0:T(8,128)S(1)} %get-tuple-element.7.fields), custom_call_target="tpu_custom_call" | custom-call | tf_op jit(solution)/shard_map/factor/pallas_call | solution.py:268
  108.6 10.8 %all_to_all.23 = f32[8,3,32,128]{3,2,1,0:T(8,128)S(1)} all-to-all(f32[8,3,32,128]{3,2,1,0:T(8,128)S(1)} %get-tuple-element.8), channel_id=1, replica_groups=mesh['z'=8,'xh'=2,'y'=4,'xl'=2,'c'=2] {'y','xl'}, dimensions={0} | all-to-all | bytes 786432 | tf_op jit(solution)/shard_map/all_to_all | solution.py:280
  119.4 0.8 copy.8
  (4 shorter events, 0.1 us)
Async XLA Ops:
  0.6 23.7 %copy-start = (f32[12,32,256]{2,1,0:T(8,128)S(1)}, f32[12,32,256]{2,1,0:T(8,128)}, u32[]{:S(2)}) copy-start(f32[12,32,256]{2,1,0:T(8,128)} %param.3) | copy-start | bytes 1179652
  0.6 23.7 %copy-start.1 = (f32[256,256]{1,0:T(8,128)S(1)}, f32[256,256]{1,0:T(8,128)}, u32[]{:S(2)}) copy-start(f32[256,256]{1,0:T(8,128)} %constant.8.clone.mat) | copy-start | bytes 786436
  0.7 23.7 %copy-start.2 = (f32[12,256]{1,0:T(8,128)S(1)}, f32[12,256]{1,0:T(8,128)}, u32[]{:S(2)}) copy-start(f32[12,256]{1,0:T(8,128)} %pot.1) | copy-start | bytes 36868
  1.8 17.1 %collective-permute-start.1 = (f32[396,256]{1,0:T(8,128)S(1)}, f32[396,256]{1,0:T(8,128)S(1)}, u32[]{:S(2)}, u32[]{:S(2)}) collective-permute-start(f32[396,256]{1,0:T(8,128)S(1)} %pad_maximum_fusion), channel_id=1, source_target_pairs={{0,240},{16,0},{32,16},{48,32},{64,48},{80,64},{96,80},{112,96},{1... | collective-permute-start | bytes 1216520 | tf_op jit(solution)/shard_map/ppermute | solution.py:228
  10.7 13.6 %collective-permute-start = (f32[396,256]{1,0:T(8,128)S(1)}, f32[396,256]{1,0:T(8,128)S(1)}, u32[]{:S(2)}, u32[]{:S(2)}) collective-permute-start(f32[396,256]{1,0:T(8,128)S(1)} %pad_maximum_fusion), channel_id=1, source_target_pairs={{0,16},{16,32},{32,48},{48,64},{64,80},{80,96},{96,112},{112,128},... | collective-permute-start | bytes 1216520 | tf_op jit(solution)/shard_map/ppermute | solution.py:227
  37.9 4.5 %collective-permute-start.2 = (f32[8,3,32,128]{3,2,1,0:T(8,128)S(1)}, f32[8,3,32,128]{3,2,1,0:T(8,128)S(1)}, u32[]{:S(2)}, u32[]{:S(2)}) collective-permute-start(f32[8,3,32,128]{3,2,1,0:T(8,128)S(1)} %all_to_all.20.own), channel_id=1, source_target_pairs={{0,1},{1,0},{2,3},{3,2},{4,5},{5,4},{6,7},{7,6},{8,9},{9,8},{10,11... | collective-permute-start | bytes 1179656 | tf_op jit(solution)/shard_map/ppermute | solution.py:246
  53.8 6.6 %collective-permute-start.5 = (f32[80,128]{1,0:T(8,128)S(1)}, f32[80,128]{1,0:T(8,128)S(1)}, u32[]{:S(2)}, u32[]{:S(2)}) collective-permute-start(f32[80,128]{1,0:T(8,128)S(1)} %reduce_sum.9), channel_id=1, source_target_pairs={{0,48},{16,32},{32,16},{48,0},{64,112},{80,96},{96,80},{112,64},{1... | collective-permute-start | bytes 122888 | tf_op jit(solution)/shard_map/ppermute | solution.py:263
  59.0 3.3 %collective-permute-start.4 = (f32[80,128]{1,0:T(8,128)S(1)}, f32[80,128]{1,0:T(8,128)S(1)}, u32[]{:S(2)}, u32[]{:S(2)}) collective-permute-start(f32[80,128]{1,0:T(8,128)S(1)} %reduce_sum.9), channel_id=1, source_target_pairs={{0,32},{16,48},{32,0},{48,16},{64,96},{80,112},{96,64},{112,80},{1... | collective-permute-start | bytes 122888 | tf_op jit(solution)/shard_map/ppermute | solution.py:263
  59.0 4.4 %collective-permute-start.3 = (f32[80,128]{1,0:T(8,128)S(1)}, f32[80,128]{1,0:T(8,128)S(1)}, u32[]{:S(2)}, u32[]{:S(2)}) collective-permute-start(f32[80,128]{1,0:T(8,128)S(1)} %reduce_sum.9), channel_id=1, source_target_pairs={{0,16},{16,0},{32,48},{48,32},{64,80},{80,64},{96,112},{112,96},{1... | collective-permute-start | bytes 122888 | tf_op jit(solution)/shard_map/ppermute | solution.py:263
  63.3 8.1 %collective-permute-start.8 = (f32[80,128]{1,0:T(8,128)S(1)}, f32[80,128]{1,0:T(8,128)S(1)}, u32[]{:S(2)}, u32[]{:S(2)}) collective-permute-start(f32[80,128]{1,0:T(8,128)S(1)} %add_add_fusion.1), channel_id=1, source_target_pairs={{0,192},{16,208},{32,224},{48,240},{64,128},{80,144},{96,160},{112... | collective-permute-start | bytes 122888 | tf_op jit(solution)/shard_map/ppermute | solution.py:263
  69.3 7.0 %collective-permute-start.7 = (f32[80,128]{1,0:T(8,128)S(1)}, f32[80,128]{1,0:T(8,128)S(1)}, u32[]{:S(2)}, u32[]{:S(2)}) collective-permute-start(f32[80,128]{1,0:T(8,128)S(1)} %add_add_fusion.1), channel_id=1, source_target_pairs={{0,128},{16,144},{32,160},{48,176},{64,192},{80,208},{96,224},{112... | collective-permute-start | bytes 122888 | tf_op jit(solution)/shard_map/ppermute | solution.py:263
  70.2 6.0 %collective-permute-start.6 = (f32[80,128]{1,0:T(8,128)S(1)}, f32[80,128]{1,0:T(8,128)S(1)}, u32[]{:S(2)}, u32[]{:S(2)}) collective-permute-start(f32[80,128]{1,0:T(8,128)S(1)} %add_add_fusion.1), channel_id=1, source_target_pairs={{0,64},{16,80},{32,96},{48,112},{64,0},{80,16},{96,32},{112,48},{1... | collective-permute-start | bytes 122888 | tf_op jit(solution)/shard_map/ppermute | solution.py:263
  85.3 6.8 %collective-permute-start.9 = (f32[640,128]{1,0:T(8,128)S(1)}, f32[640,128]{1,0:T(8,128)S(1)}, u32[]{:S(2)}, u32[]{:S(2)}) collective-permute-start(f32[640,128]{1,0:T(8,128)S(1)} %bitcast.15), channel_id=1, source_target_pairs={{0,1},{1,0},{2,3},{3,2},{4,5},{5,4},{6,7},{7,6},{8,9},{9,8},{10,11... | collective-permute-start | bytes 983048 | tf_op jit(solution)/shard_map/ppermute | solution.py:267

commit v2 on v1

--- a/solution.py
+++ b/solution.py
@@ -21,6 +21,7 @@
 
 SPACE = ("z", "xh")
 TEAM = ("y", "xl")
+LAYER = ("xh", "y", "xl")
 BAND = ("y", "xl", "c")
 
 BLOCKS = [[(0, 0), (1, 0), (1, 1), (2, 0), (2, 1)], [(2, 2), (3, 0), (3, 1), (3, 2), (3, 3)]]
@@ -47,47 +48,49 @@
     )
 
 
-def filter_kernel(rows, planes, low_hbm, own, pot, high_hbm, mat, out, first, low, high, sem):
-    copies = [
-        pltpu.make_async_copy(src, dst, sem.at[i])
-        for i, (src, dst) in enumerate(((low_hbm, low), (high_hbm, high)))
-    ]
-    for copy in copies:
-        copy.start()
-
+def level(pot, p):
+    return (pot[p : p + 1, :] - SHIFT_MID) / HALF_SPAN
+
+
+def begin_kernel(rows, planes, own, pot, mat, out):
+    flat = dot32(own[...], mat[...], ((1,), (0,)))
+    for z in range(planes):
+        acc = flat[z * rows : (z + 1) * rows, :] + level(pot, z) * own[z * rows : (z + 1) * rows, :]
+        for k in range(RADIUS):
+            near = [own[p * rows : (p + 1) * rows, :] for p in (z + k + 1, z - k - 1) if 0 <= p < planes]
+            acc = acc + (SCALE * COEFS[k]) * sum(near[1:], near[0])
+        out[z * rows : (z + 1) * rows, :] = acc
+
+
+def filter_kernel(rows, planes, low, own, high, pot_low, pot, pot_high, mat, part, out, first):
     def field(p):
-        if p < planes:
-            return low[p * rows : (p + 1) * rows, :]
-        if p < 2 * planes:
-            return own[(p - planes) * rows : (p - planes + 1) * rows, :]
-        return high[(p - 2 * planes) * rows : (p - 2 * planes + 1) * rows, :]
-
-    def level(p):
-        if p < planes:
-            row = low[planes * rows + p : planes * rows + p + 1, :]
-        elif p < 2 * planes:
-            row = pot[p - planes : p - planes + 1, :]
-        else:
-            row = high[planes * rows + p - 2 * planes : planes * rows + p - 2 * planes + 1, :]
-        return (row - SHIFT_MID) / HALF_SPAN
+        ref = (low, own, high)[p // planes]
+        return ref[p % planes * rows : (p % planes + 1) * rows, :]
+
+    def missing(acc, p, known):
+        for k in range(RADIUS):
+            far = [field(q) for q in (p + k + 1, p - k - 1) if not (known and planes <= q < 2 * planes)]
+            if far:
+                acc = acc + (SCALE * COEFS[k]) * sum(far[1:], far[0])
+        return acc
 
     half = RADIUS * rows
-    first[half : half + planes * rows, :] = dot32(own[...], mat[...], ((1,), (0,)))
-    for copy in copies:
-        copy.wait()
-    first[0:half, :] = dot32(low[(planes - RADIUS) * rows : planes * rows, :], mat[...], ((1,), (0,)))
-    first[half + planes * rows :, :] = dot32(high[0:half, :], mat[...], ((1,), (0,)))
+    size = planes * rows
+    first[0:half, :] = dot32(low[size - half : size, :], mat[...], ((1,), (0,)))
+    first[half + size :, :] = dot32(high[0:half, :], mat[...], ((1,), (0,)))
     for q in range(planes + 2 * RADIUS):
         p = q + planes - RADIUS
-        acc = first[q * rows : (q + 1) * rows, :] + level(p) * field(p)
-        for k in range(RADIUS):
-            acc = acc + (SCALE * COEFS[k]) * (field(p + k + 1) + field(p - k - 1))
-        first[q * rows : (q + 1) * rows, :] = acc
-    inner = dot32(first[half : half + planes * rows, :], mat[...], ((1,), (0,)))
+        at = slice(q * rows, (q + 1) * rows)
+        if planes <= p < 2 * planes:
+            first[at, :] = missing(part[(p - planes) * rows : (p - planes + 1) * rows, :], p, True)
+        else:
+            row = level((pot_low, pot, pot_high)[p // planes], p % planes)
+            first[at, :] = missing(first[at, :] + row * field(p), p, False)
+    inner = dot32(first[half : half + size, :], mat[...], ((1,), (0,)))
     for z in range(planes):
         q = z + RADIUS
         centre = first[q * rows : (q + 1) * rows, :]
-        acc = inner[z * rows : (z + 1) * rows, :] + level(z + planes) * centre
+        acc = inner[z * rows : (z + 1) * rows, :] + level(pot, z) * centre
         for k in range(RADIUS):
             up = first[(q + k + 1) * rows : (q + k + 2) * rows, :]
             down = first[(q - k - 1) * rows : (q - k) * rows, :]
@@ -156,7 +159,7 @@
                 full[i] = jnp.where(at, ratio, new) if i == h else new
         for h in halves:
             ref[place[h], lanes] = jnp.where(lane < base + GROUP, low[h] * scale[h], 0.0)
-        for q in range(base + GROUP, TILE, 8):
+        for q in range(base + GROUP, min(base + 2 * GROUP, TILE), 8):
             rest = ref[origin + q : origin + q + 8, lanes]
             acc = jnp.where(inside, 0.0, rest)
             for m in range(GROUP):
@@ -164,6 +167,17 @@
                     full[m // 8], m % 8
                 )
             ref[origin + q : origin + q + 8, lanes] = acc
+        if base + 2 * GROUP < TILE:
+            far = slice(origin + base + 2 * GROUP, origin + TILE)
+            rest = ref[far, lanes]
+            column = lax.broadcasted_iota(jnp.int32, rest.shape, 1)
+            among = (column >= base) & (column < base + GROUP)
+            after = jnp.zeros((TILE - GROUP - base, TILE), jnp.float32)
+            before = [jnp.zeros((base, TILE), jnp.float32)] if base else []
+            spread = jnp.concatenate(before + full + [after], axis=0)
+            ref[far, lanes] = jnp.where(among, 0.0, rest) - dot32(
+                jnp.where(among, rest, 0.0), spread, ((1,), (0,))
+            )
 
 
 def factor_kernel(place, own, other, fields, corr, out, work):
@@ -205,7 +219,6 @@
 
 
 VMEM = pl.BlockSpec(memory_space=pltpu.VMEM)
-ANY = pl.BlockSpec(memory_space=pl.ANY)
 SMEM = pl.BlockSpec(memory_space=pltpu.SMEM)
 PARAMS = pltpu.CompilerParams(vmem_limit_bytes=48 << 20)
 
@@ -223,23 +236,28 @@
     planes, rows, cells = orbitals.shape
     place = lax.axis_index("c").astype(jnp.int32).reshape(1)
     own = orbitals.reshape(planes * rows, cells)
-    packed = jnp.concatenate([own, potential], axis=0)
-    low = lax.ppermute(packed, SPACE, ring(SPACE, 1))
-    high = lax.ppermute(packed, SPACE, ring(SPACE, -1))
+    low = lax.ppermute(own, SPACE, ring(SPACE, 1))
+    high = lax.ppermute(own, SPACE, ring(SPACE, -1))
+    pot_low = lax.ppermute(potential, SPACE, ring(SPACE, 1))
+    pot_high = lax.ppermute(potential, SPACE, ring(SPACE, -1))
+    mat = jnp.asarray(plane_matrix())
+    begun = pl.pallas_call(
+        functools.partial(begin_kernel, rows, planes),
+        out_shape=jax.ShapeDtypeStruct(own.shape, jnp.float32),
+        in_specs=[VMEM] * 3,
+        out_specs=VMEM,
+        compiler_params=PARAMS,
+        name="begin",
+    )(own, potential, mat)
     second = pl.pallas_call(
         functools.partial(filter_kernel, rows, planes),
         out_shape=jax.ShapeDtypeStruct((2 * planes, rows, TILE), jnp.float32),
-        in_specs=[ANY, VMEM, VMEM, ANY, VMEM],
+        in_specs=[VMEM] * 8,
         out_specs=VMEM,
-        scratch_shapes=[
-            pltpu.VMEM(((planes + 2 * RADIUS) * rows, cells), jnp.float32),
-            pltpu.VMEM(packed.shape, jnp.float32),
-            pltpu.VMEM(packed.shape, jnp.float32),
-            pltpu.SemaphoreType.DMA((2,)),
-        ],
+        scratch_shapes=[pltpu.VMEM(((planes + 2 * RADIUS) * rows, cells), jnp.float32)],
         compiler_params=PARAMS,
         name="filter",
-    )(low, own, potential, high, jnp.asarray(plane_matrix()))
+    )(low, own, high, pot_low, potential, pot_high, mat, begun)
 
     team = lax.axis_size(TEAM)
     mine = lax.all_to_all(second.reshape(team, 2 * planes // team, rows, TILE), TEAM, 0, 0)
@@ -258,11 +276,12 @@
         name="gram",
     )(place, mine, theirs)
 
-    piece = lax.all_to_all(part.reshape(team, 5 * TILE // team, TILE), TEAM, 0, 0).sum(0)
-    for bits in ((1, 2, 3), (4, 8, 12)):
-        got = [lax.ppermute(piece, SPACE, flip(SPACE, b)) for b in bits]
-        piece = (piece + got[0]) + (got[1] + got[2])
-    spread = lax.all_to_all(jnp.broadcast_to(piece, (team,) + piece.shape), TEAM, 0, 0)
+    layer = lax.axis_size(LAYER)
+    piece = lax.all_to_all(part.reshape(layer, 5 * TILE // layer, TILE), LAYER, 0, 0).sum(0)
+    piece = piece + lax.ppermute(piece, "z", flip("z", 1))
+    got = [lax.ppermute(piece, "z", flip("z", b)) for b in (2, 4, 6)]
+    piece = (piece + got[0]) + (got[1] + got[2])
+    spread = lax.all_to_all(jnp.broadcast_to(piece, (layer,) + piece.shape), LAYER, 0, 0)
     mine_g = spread.reshape(5 * TILE, TILE)
     theirs_g = lax.ppermute(mine_g, ("c",), flip("c", 1))
     correlation, turned = pl.pallas_call(

time: 120 us -> 115 us (0.958)
  waiting for transfers between devices: 25 us -> 13.6 us
  blocking collectives: 40.8 us -> 47.1 us
  Pallas kernels: 20.4 us -> 17.3 us
  local copies, waits for them, and re-layouts: 0.81 us -> 3.46 us
    ppermute x8, waiting for transfers between devices: 22.4 us -> 11 us  [the longest x1 5.45 us: per_device(): pot_low = lax.ppermute(potential, SPACE, ring(SPACE, 1))]
    all_to_all x2, blocking collectives: 18.9 us -> 25.2 us  [the longest x1 14.1 us: per_device(): lax.all_to_all(part.reshape(layer, 5 * TILE // layer, TILE), LAYER, 0, 0)]
    unnamed x6, local copies, waits for them, and re-layouts: 0.02 us -> 2.66 us
    pallas_call x1, Pallas kernels: 16.6 us -> 14.1 us  [per_device(): pl.pallas_call(factor_kernel, out_shape=(jax.ShapeDtypeStruct((count, cou...]
  transfers between devices with their start and end apart: 10 -> 10, of which waited for: 8 -> 5; matrix products, arithmetic and copies ran while one was open for 0% -> 0% of each run, Pallas kernels for 0% -> 1%
where the time goes in v2:
time: 115 us; the launch traced here: 114 us
  blocking collectives  47.1 us (41%)
  starting transfers between devices  32.1 us (28%)
  Pallas kernels  17.3 us (15%)
  waiting for transfers between devices  13.6 us (12%)
  local copies, waits for them, and re-layouts  3.46 us (3%)
    all_to_all x1, blocking collectives, per_device(): lax.all_to_all(part.reshape(layer, 5 * TILE // layer, TILE), LAYER, 0, 0)  14.1 us
    pallas_call x1, Pallas kernels, per_device(): pl.pallas_call(factor_kernel, out_shape=(jax.ShapeDtypeStruct((count, cou...  14.1 us
    all_to_all x1, blocking collectives, per_device(): lax.all_to_all(jnp.broadcast_to(piece, (layer,) + piece.shape), LAYER, 0, 0)  11.1 us
    all_to_all x1, blocking collectives, per_device(): lax.all_to_all(second.reshape(team, 2 * planes // team, rows, TILE), TEAM...  11.1 us
    all_to_all x1, blocking collectives, per_device(): back = lax.all_to_all(turned, TEAM, 0, 0).reshape(planes, 2, rows, TILE)  10.8 us
    ppermute x1, starting transfers between devices, per_device(): high = lax.ppermute(own, SPACE, ring(SPACE, -1))  8.94 us
    ppermute x3, starting transfers between devices, per_device(): got = [lax.ppermute(piece, 'z', flip('z', b)) for b in (2, 4, 6)]  8.01 us
    ppermute x1, waiting for transfers between devices, per_device(): pot_low = lax.ppermute(potential, SPACE, ring(SPACE, 1))  5.45 us
  transfers between devices with their start and end apart: 10, of which 5 were waited for; matrix products, arithmetic and copies ran while one was open for 0% of the time, Pallas kernels for 1%

profile of v2, /device:TPU:1, one launch (start us, length us, event | category | flops | bytes accessed | tf_op | source)
XLA Modules:
  0.0 114.3 jit_solution(963709926649144026)
XLA Ops:
  0.6 8.9 %collective-permute-start.1 = (f32[384,256]{1,0:T(8,128)}, f32[384,256]{1,0:T(8,128)S(1)}, u32[]{:S(2)}, u32[]{:S(2)}) collective-permute-start(f32[384,256]{1,0:T(8,128)} %bitcast.12), channel_id=1, source_target_pairs={{0,240},{16,0},{32,16},{48,32},{64,48},{80,64},{96,80},{112,96},{1... | collective-permute-start | bytes 1179656 | tf_op jit(solution)/shard_map/ppermute | solution.py:240
  9.6 0.0 collective-permute-start
  9.6 5.1 %collective-permute-start.3 = (f32[12,256]{1,0:T(8,128)}, f32[12,256]{1,0:T(8,128)S(1)}, u32[]{:S(2)}, u32[]{:S(2)}) collective-permute-start(f32[12,256]{1,0:T(8,128)} %pot.3), channel_id=1, source_target_pairs={{0,240},{16,0},{32,16},{48,32},{64,48},{80,64},{96,80},{112,96},{1... | collective-permute-start | bytes 36872 | tf_op jit(solution)/shard_map/ppermute | solution.py:242
  14.7 0.0 collective-permute-start.2
  14.7 0.0 copy-start
  14.7 1.0 copy-done
  15.7 0.0 copy-start.1
  15.7 0.9 copy-done.1
  16.6 0.0 copy-start.2
  16.6 0.7 copy-done.2
  17.3 0.6 begin.1.part
  17.9 0.0 collective-permute-done.3.pot_high
  18.0 5.5 %collective-permute-done.2.pot_low = f32[12,256]{1,0:T(8,128)S(1)} collective-permute-done((f32[12,256]{1,0:T(8,128)}, f32[12,256]{1,0:T(8,128)S(1)}, u32[]{:S(2)}, u32[]{:S(2)}) %collective-permute-start.2) | collective-permute-done | bytes 12320 | tf_op jit(solution)/shard_map/ppermute | solution.py:241
  23.4 0.0 collective-permute-done.1.high
  23.4 0.0 collective-permute-done.low
  23.4 1.3 %filter.1 = f32[24,32,128]{2,1,0:T(8,128)S(1)} custom-call(f32[384,256]{1,0:T(8,128)S(1)} %collective-permute-done.low, f32[384,256]{1,0:T(8,128)S(1)} %bitcast.15, f32[384,256]{1,0:T(8,128)S(1)} %collective-permute-done.1.high, f32[12,256]{1,0:T(8,128)S(1)} %collective-permute-done.2.pot_low, f32[12,256]{1,0:T(8,128)S(1)} %copy-done.2, ...), custom_call_target="tpu_custom_call" | custom-call | tf_op jit(solution)/shard_map/filter/pallas_call | solution.py:252
  24.7 11.1 %all_to_all.20.own = f32[8,3,32,128]{3,2,1,0:T(8,128)S(1)} all-to-all(f32[8,3,32,128]{3,2,1,0:T(8,128)S(1)} %bitcast.16), channel_id=1, replica_groups=mesh['z'=8,'xh'=2,'y'=4,'xl'=2,'c'=2] {'y','xl'}, dimensions={0} | all-to-all | bytes 786432 | tf_op jit(solution)/shard_map/all_to_all | solution.py:263
  35.8 3.2 %collective-permute-start.4 = (f32[8,3,32,128]{3,2,1,0:T(8,128)S(1)}, f32[8,3,32,128]{3,2,1,0:T(8,128)S(1)}, u32[]{:S(2)}, u32[]{:S(2)}) collective-permute-start(f32[8,3,32,128]{3,2,1,0:T(8,128)S(1)} %all_to_all.20.own), channel_id=1, source_target_pairs={{0,1},{1,0},{2,3},{3,2},{4,5},{5,4},{6,7},{7,6},{8,9},{9,8},{10,11... | collective-permute-start | bytes 1179656 | tf_op jit(solution)/shard_map/ppermute | solution.py:264
  39.0 1.3 %collective-permute-done.4.other = f32[8,3,32,128]{3,2,1,0:T(8,128)S(1)} collective-permute-done((f32[8,3,32,128]{3,2,1,0:T(8,128)S(1)}, f32[8,3,32,128]{3,2,1,0:T(8,128)S(1)}, u32[]{:S(2)}, u32[]{:S(2)}) %collective-permute-start.4) | collective-permute-done | bytes 393248 | tf_op jit(solution)/shard_map/ppermute | solution.py:264
  40.3 1.4 %gram.1 = (f32[640,128]{1,0:T(8,128)S(1)}, f32[512,384]{1,0:T(8,128)S(1)}) custom-call(s32[1]{0:T(128)} %bitcast.place, f32[8,3,32,128]{3,2,1,0:T(8,128)S(1)} %all_to_all.20.own, f32[8,3,32,128]{3,2,1,0:T(8,128)S(1)} %collective-permute-done.4.other), custom_call_target="tpu_custom_call" | custom-call | tf_op jit(solution)/shard_map/gram/pallas_call | solution.py:267
  41.7 14.1 %all_to_all.21 = f32[16,40,128]{2,1,0:T(8,128)S(1)} all-to-all(f32[16,40,128]{2,1,0:T(8,128)S(1)} %bitcast.19), channel_id=1, replica_groups=mesh['z'=8,'xh'=2,'y'=4,'xl'=2,'c'=2] {'xh','y','xl'}, dimensions={0} | all-to-all | bytes 655360 | tf_op jit(solution)/shard_map/all_to_all | solution.py:280
  55.8 1.7 %collective-permute-start.5 = (f32[40,128]{1,0:T(8,128)S(1)}, f32[40,128]{1,0:T(8,128)S(1)}, u32[]{:S(2)}, u32[]{:S(2)}) collective-permute-start(f32[40,128]{1,0:T(8,128)S(1)} %reduce_sum.9), channel_id=1, source_target_pairs={{0,32},{32,0},{64,96},{96,64},{128,160},{160,128},{192,224},{224,1... | collective-permute-start | bytes 61448 | tf_op jit(solution)/shard_map/ppermute | solution.py:281
  57.6 1.2 %collective-permute-done.5 = f32[40,128]{1,0:T(8,128)S(1)} collective-permute-done((f32[40,128]{1,0:T(8,128)S(1)}, f32[40,128]{1,0:T(8,128)S(1)}, u32[]{:S(2)}, u32[]{:S(2)}) %collective-permute-start.5) | collective-permute-done | bytes 20512 | tf_op jit(solution)/shard_map/ppermute | solution.py:281
  58.8 5.8 %collective-permute-start.8 = (f32[40,128]{1,0:T(8,128)S(1)}, f32[40,128]{1,0:T(8,128)S(1)}, u32[]{:S(2)}, u32[]{:S(2)}) collective-permute-start(f32[40,128]{1,0:T(8,128)S(1)} %add.12), channel_id=1, source_target_pairs={{0,192},{32,224},{64,128},{96,160},{128,64},{160,96},{192,0},{224,... | collective-permute-start | bytes 61448 | tf_op jit(solution)/shard_map/ppermute | solution.py:282
  64.6 1.0 collective-permute-start.7
  65.6 1.2 %collective-permute-start.6 = (f32[40,128]{1,0:T(8,128)S(1)}, f32[40,128]{1,0:T(8,128)S(1)}, u32[]{:S(2)}, u32[]{:S(2)}) collective-permute-start(f32[40,128]{1,0:T(8,128)S(1)} %add.12), channel_id=1, source_target_pairs={{0,64},{32,96},{64,0},{96,32},{128,192},{160,224},{192,128},{224,1... | collective-permute-start | bytes 61448 | tf_op jit(solution)/shard_map/ppermute | solution.py:282
  66.8 0.0 collective-permute-done.8
  66.8 4.4 %collective-permute-done.7 = f32[40,128]{1,0:T(8,128)S(1)} collective-permute-done((f32[40,128]{1,0:T(8,128)S(1)}, f32[40,128]{1,0:T(8,128)S(1)}, u32[]{:S(2)}, u32[]{:S(2)}) %collective-permute-start.7) | collective-permute-done | bytes 20512 | tf_op jit(solution)/shard_map/ppermute | solution.py:282
  71.2 0.0 collective-permute-done.6
  71.2 11.1 %all_to_all.22 = f32[16,40,128]{2,1,0:T(8,128)S(1)} all-to-all(f32[16,40,128]{2,1,0:T(8,128)S(1)} %broadcast_in_dim.3), channel_id=1, replica_groups=mesh['z'=8,'xh'=2,'y'=4,'xl'=2,'c'=2] {'xh','y','xl'}, dimensions={0} | all-to-all | bytes 655360 | tf_op jit(solution)/shard_map/all_to_all | solution.py:284
  82.3 5.1 %collective-permute-start.9 = (f32[640,128]{1,0:T(8,128)S(1)}, f32[640,128]{1,0:T(8,128)S(1)}, u32[]{:S(2)}, u32[]{:S(2)}) collective-permute-start(f32[640,128]{1,0:T(8,128)S(1)} %bitcast.17), channel_id=1, source_target_pairs={{0,1},{1,0},{2,3},{3,2},{4,5},{5,4},{6,7},{7,6},{8,9},{9,8},{10,11... | collective-permute-start | bytes 983048 | tf_op jit(solution)/shard_map/ppermute | solution.py:286
  87.4 1.3 %collective-permute-done.9.other = f32[640,128]{1,0:T(8,128)S(1)} collective-permute-done((f32[640,128]{1,0:T(8,128)S(1)}, f32[640,128]{1,0:T(8,128)S(1)}, u32[]{:S(2)}, u32[]{:S(2)}) %collective-permute-start.9) | collective-permute-done | bytes 327712 | tf_op jit(solution)/shard_map/ppermute | solution.py:286
  88.7 14.1 %factor.1 = (f32[512,512]{1,0:T(8,128)}, f32[8,3,32,128]{3,2,1,0:T(8,128)S(1)}) custom-call(s32[1]{0:T(128)} %bitcast.place, f32[640,128]{1,0:T(8,128)S(1)} %bitcast.18, f32[640,128]{1,0:T(8,128)S(1)} %collective-permute-done.9.other, f32[512,384]{1,0:T(8,128)S(1)} %get-tuple-element.7.fields), custom_call_target="tpu_custom_call" | custom-call | tf_op jit(solution)/shard_map/factor/pallas_call | solution.py:287
  102.8 10.8 %all_to_all.23 = f32[8,3,32,128]{3,2,1,0:T(8,128)S(1)} all-to-all(f32[8,3,32,128]{3,2,1,0:T(8,128)S(1)} %get-tuple-element.8), channel_id=1, replica_groups=mesh['z'=8,'xh'=2,'y'=4,'xl'=2,'c'=2] {'y','xl'}, dimensions={0} | all-to-all | bytes 786432 | tf_op jit(solution)/shard_map/all_to_all | solution.py:299
  113.6 0.8 copy.8
  (4 shorter events, 0.1 us)
Async XLA Ops:
  0.6 22.8 %collective-permute-start.1 = (f32[384,256]{1,0:T(8,128)}, f32[384,256]{1,0:T(8,128)S(1)}, u32[]{:S(2)}, u32[]{:S(2)}) collective-permute-start(f32[384,256]{1,0:T(8,128)} %bitcast.12), channel_id=1, source_target_pairs={{0,240},{16,0},{32,16},{48,32},{64,48},{80,64},{96,80},{112,96},{1... | collective-permute-start | bytes 1179656 | tf_op jit(solution)/shard_map/ppermute | solution.py:240
  9.6 13.8 %collective-permute-start = (f32[384,256]{1,0:T(8,128)}, f32[384,256]{1,0:T(8,128)S(1)}, u32[]{:S(2)}, u32[]{:S(2)}) collective-permute-start(f32[384,256]{1,0:T(8,128)} %bitcast.13), channel_id=1, source_target_pairs={{0,16},{16,32},{32,48},{48,64},{64,80},{80,96},{96,112},{112,128},... | collective-permute-start | bytes 1179656 | tf_op jit(solution)/shard_map/ppermute | solution.py:239
  9.6 8.4 %collective-permute-start.3 = (f32[12,256]{1,0:T(8,128)}, f32[12,256]{1,0:T(8,128)S(1)}, u32[]{:S(2)}, u32[]{:S(2)}) collective-permute-start(f32[12,256]{1,0:T(8,128)} %pot.3), channel_id=1, source_target_pairs={{0,240},{16,0},{32,16},{48,32},{64,48},{80,64},{96,80},{112,96},{1... | collective-permute-start | bytes 36872 | tf_op jit(solution)/shard_map/ppermute | solution.py:242
  14.7 8.8 %collective-permute-start.2 = (f32[12,256]{1,0:T(8,128)}, f32[12,256]{1,0:T(8,128)S(1)}, u32[]{:S(2)}, u32[]{:S(2)}) collective-permute-start(f32[12,256]{1,0:T(8,128)} %pot.3), channel_id=1, source_target_pairs={{0,16},{16,32},{32,48},{48,64},{64,80},{80,96},{96,112},{112,128},... | collective-permute-start | bytes 36872 | tf_op jit(solution)/shard_map/ppermute | solution.py:241
  14.7 1.0 copy-start
  15.7 0.9 copy-start.1
  16.6 0.7 copy-start.2
  35.8 4.5 %collective-permute-start.4 = (f32[8,3,32,128]{3,2,1,0:T(8,128)S(1)}, f32[8,3,32,128]{3,2,1,0:T(8,128)S(1)}, u32[]{:S(2)}, u32[]{:S(2)}) collective-permute-start(f32[8,3,32,128]{3,2,1,0:T(8,128)S(1)} %all_to_all.20.own), channel_id=1, source_target_pairs={{0,1},{1,0},{2,3},{3,2},{4,5},{5,4},{6,7},{7,6},{8,9},{9,8},{10,11... | collective-permute-start | bytes 1179656 | tf_op jit(solution)/shard_map/ppermute | solution.py:264
  55.8 2.9 %collective-permute-start.5 = (f32[40,128]{1,0:T(8,128)S(1)}, f32[40,128]{1,0:T(8,128)S(1)}, u32[]{:S(2)}, u32[]{:S(2)}) collective-permute-start(f32[40,128]{1,0:T(8,128)S(1)} %reduce_sum.9), channel_id=1, source_target_pairs={{0,32},{32,0},{64,96},{96,64},{128,160},{160,128},{192,224},{224,1... | collective-permute-start | bytes 61448 | tf_op jit(solution)/shard_map/ppermute | solution.py:281
  58.8 8.0 %collective-permute-start.8 = (f32[40,128]{1,0:T(8,128)S(1)}, f32[40,128]{1,0:T(8,128)S(1)}, u32[]{:S(2)}, u32[]{:S(2)}) collective-permute-start(f32[40,128]{1,0:T(8,128)S(1)} %add.12), channel_id=1, source_target_pairs={{0,192},{32,224},{64,128},{96,160},{128,64},{160,96},{192,0},{224,... | collective-permute-start | bytes 61448 | tf_op jit(solution)/shard_map/ppermute | solution.py:282
  64.6 6.6 %collective-permute-start.7 = (f32[40,128]{1,0:T(8,128)S(1)}, f32[40,128]{1,0:T(8,128)S(1)}, u32[]{:S(2)}, u32[]{:S(2)}) collective-permute-start(f32[40,128]{1,0:T(8,128)S(1)} %add.12), channel_id=1, source_target_pairs={{0,128},{32,160},{64,192},{96,224},{128,0},{160,32},{192,64},{224,... | collective-permute-start | bytes 61448 | tf_op jit(solution)/shard_map/ppermute | solution.py:282
  65.6 5.6 %collective-permute-start.6 = (f32[40,128]{1,0:T(8,128)S(1)}, f32[40,128]{1,0:T(8,128)S(1)}, u32[]{:S(2)}, u32[]{:S(2)}) collective-permute-start(f32[40,128]{1,0:T(8,128)S(1)} %add.12), channel_id=1, source_target_pairs={{0,64},{32,96},{64,0},{96,32},{128,192},{160,224},{192,128},{224,1... | collective-permute-start | bytes 61448 | tf_op jit(solution)/shard_map/ppermute | solution.py:282
  82.3 6.4 %collective-permute-start.9 = (f32[640,128]{1,0:T(8,128)S(1)}, f32[640,128]{1,0:T(8,128)S(1)}, u32[]{:S(2)}, u32[]{:S(2)}) collective-permute-start(f32[640,128]{1,0:T(8,128)S(1)} %bitcast.17), channel_id=1, source_target_pairs={{0,1},{1,0},{2,3},{3,2},{4,5},{5,4},{6,7},{7,6},{8,9},{9,8},{10,11... | collective-permute-start | bytes 983048 | tf_op jit(solution)/shard_map/ppermute | solution.py:286

commit v3 on v2

--- a/solution.py
+++ b/solution.py
@@ -48,54 +48,42 @@
     )
 
 
-def level(pot, p):
-    return (pot[p : p + 1, :] - SHIFT_MID) / HALF_SPAN
-
-
-def begin_kernel(rows, planes, own, pot, mat, out):
-    flat = dot32(own[...], mat[...], ((1,), (0,)))
-    for z in range(planes):
-        acc = flat[z * rows : (z + 1) * rows, :] + level(pot, z) * own[z * rows : (z + 1) * rows, :]
+def filter_kernel(
+    rows, planes, place, own, swap, near, cross, pot, pot_swap, pot_near, pot_cross, mat, out, field, level, first
+):
+    h = place[1]
+    size = planes * rows
+    for k, data, values in (
+        (1 + h, own, pot),
+        (2 - h, swap, pot_swap),
+        (3 - 3 * h, near, pot_near),
+        (3 * h, cross, pot_cross),
+    ):
+        field[pl.ds(pl.multiple_of(k * size, size), size), :] = data[...]
+        level[k, 0:planes, :] = (values[...] - SHIFT_MID) / HALF_SPAN
+
+    def plane(ref, p):
+        return ref[p * rows : (p + 1) * rows, :]
+
+    def row(p):
+        return level[p // planes, p % planes : p % planes + 1, :]
+
+    skip = planes - RADIUS
+    count = 2 * planes + 2 * RADIUS
+    first[...] = dot32(field[skip * rows : (skip + count) * rows, :], mat[...], ((1,), (0,)))
+    for q in range(count):
+        p = q + skip
+        acc = plane(first, q) + row(p) * plane(field, p)
         for k in range(RADIUS):
-            near = [own[p * rows : (p + 1) * rows, :] for p in (z + k + 1, z - k - 1) if 0 <= p < planes]
-            acc = acc + (SCALE * COEFS[k]) * sum(near[1:], near[0])
-        out[z * rows : (z + 1) * rows, :] = acc
-
-
-def filter_kernel(rows, planes, low, own, high, pot_low, pot, pot_high, mat, part, out, first):
-    def field(p):
-        ref = (low, own, high)[p // planes]
-        return ref[p % planes * rows : (p % planes + 1) * rows, :]
-
-    def missing(acc, p, known):
+            acc = acc + (SCALE * COEFS[k]) * (plane(field, p + k + 1) + plane(field, p - k - 1))
+        first[q * rows : (q + 1) * rows, :] = acc
+    inner = dot32(first[RADIUS * rows : RADIUS * rows + 2 * size, :], mat[...], ((1,), (0,)))
+    for z in range(2 * planes):
+        q = z + RADIUS
+        acc = inner[z * rows : (z + 1) * rows, :] + row(z + planes) * plane(first, q)
         for k in range(RADIUS):
-            far = [field(q) for q in (p + k + 1, p - k - 1) if not (known and planes <= q < 2 * planes)]
-            if far:
-                acc = acc + (SCALE * COEFS[k]) * sum(far[1:], far[0])
-        return acc
-
-    half = RADIUS * rows
-    size = planes * rows
-    first[0:half, :] = dot32(low[size - half : size, :], mat[...], ((1,), (0,)))
-    first[half + size :, :] = dot32(high[0:half, :], mat[...], ((1,), (0,)))
-    for q in range(planes + 2 * RADIUS):
-        p = q + planes - RADIUS
-        at = slice(q * rows, (q + 1) * rows)
-        if planes <= p < 2 * planes:
-            first[at, :] = missing(part[(p - planes) * rows : (p - planes + 1) * rows, :], p, True)
-        else:
-            row = level((pot_low, pot, pot_high)[p // planes], p % planes)
-            first[at, :] = missing(first[at, :] + row * field(p), p, False)
-    inner = dot32(first[half : half + size, :], mat[...], ((1,), (0,)))
-    for z in range(planes):
-        q = z + RADIUS
-        centre = first[q * rows : (q + 1) * rows, :]
-        acc = inner[z * rows : (z + 1) * rows, :] + level(pot, z) * centre
-        for k in range(RADIUS):
-            up = first[(q + k + 1) * rows : (q + k + 2) * rows, :]
-            down = first[(q - k - 1) * rows : (q - k) * rows, :]
-            acc = acc + (SCALE * COEFS[k]) * (up + down)
-        second = 2.0 * acc - field(z + planes)
+            acc = acc + (SCALE * COEFS[k]) * (plane(first, q + k + 1) + plane(first, q - k - 1))
+        second = 2.0 * acc - plane(field, z + planes)
         out[2 * z] = second[:, :TILE]
         out[2 * z + 1] = second[:, TILE:]
 
@@ -103,10 +91,11 @@
 def gram_kernel(scale, place, own, other, out, stack):
     c = place[0]
     rows = own.shape[2]
+    team = own.shape[0] // 2
     for half, ref in ((c, own), (1 - c, other)):
         for s in range(own.shape[0]):
+            at = pl.multiple_of((s % team * 4 + half * 2 + s // team) * rows, rows)
             for t in range(own.shape[1]):
-                at = pl.multiple_of(s * 2 * rows + half * rows, rows)
                 stack[pl.ds(at, rows), t * TILE : (t + 1) * TILE] = ref[s, t]
     for k in range(5):
         i = jnp.where(c == 0, BLOCKS[0][k][0], BLOCKS[1][k][0])
@@ -223,44 +212,43 @@
 PARAMS = pltpu.CompilerParams(vmem_limit_bytes=48 << 20)
 
 
-def ring(axes, step):
-    count = lax.axis_size(axes)
-    return [(i, (i + step) % count) for i in range(count)]
-
-
 def flip(axes, bits):
     return [(i, i ^ bits) for i in range(lax.axis_size(axes))]
 
 
 def per_device(orbitals, potential):
     planes, rows, cells = orbitals.shape
-    place = lax.axis_index("c").astype(jnp.int32).reshape(1)
-    own = orbitals.reshape(planes * rows, cells)
-    low = lax.ppermute(own, SPACE, ring(SPACE, 1))
-    high = lax.ppermute(own, SPACE, ring(SPACE, -1))
-    pot_low = lax.ppermute(potential, SPACE, ring(SPACE, 1))
-    pot_high = lax.ppermute(potential, SPACE, ring(SPACE, -1))
-    mat = jnp.asarray(plane_matrix())
-    begun = pl.pallas_call(
-        functools.partial(begin_kernel, rows, planes),
-        out_shape=jax.ShapeDtypeStruct(own.shape, jnp.float32),
-        in_specs=[VMEM] * 3,
+    side = lax.axis_index("xh")
+    place = jnp.stack([lax.axis_index("c"), side]).astype(jnp.int32)
+    half = rows // 2
+    own, other = (
+        lax.dynamic_slice_in_dim(orbitals, at * half, half, 1).reshape(planes * half, cells)
+        for at in (side, 1 - side)
+    )
+    slabs = lax.axis_size(SPACE)
+    swap = [(s, s ^ 1) for s in range(slabs)]
+    near = [(s, (s + 2 * (2 * (s % 2) - 1)) % slabs) for s in range(slabs)]
+    cross = [(s, (s + 2 * (s % 2) - 1) % slabs) for s in range(slabs)]
+    data = [lax.ppermute(x, SPACE, pairs) for x, pairs in ((other, cross), (other, swap), (own, near))][::-1]
+    pots = [lax.ppermute(potential, SPACE, pairs) for pairs in (cross, swap, near)][::-1]
+    near, swap, cross = data
+    pot_near, pot_swap, pot_cross = pots
+    second = pl.pallas_call(
+        functools.partial(filter_kernel, half, planes),
+        out_shape=jax.ShapeDtypeStruct((4 * planes, half, TILE), jnp.float32),
+        in_specs=[SMEM] + [VMEM] * 9,
         out_specs=VMEM,
-        compiler_params=PARAMS,
-        name="begin",
-    )(own, potential, mat)
-    second = pl.pallas_call(
-        functools.partial(filter_kernel, rows, planes),
-        out_shape=jax.ShapeDtypeStruct((2 * planes, rows, TILE), jnp.float32),
-        in_specs=[VMEM] * 8,
-        out_specs=VMEM,
-        scratch_shapes=[pltpu.VMEM(((planes + 2 * RADIUS) * rows, cells), jnp.float32)],
+        scratch_shapes=[
+            pltpu.VMEM((4 * planes * half, cells), jnp.float32),
+            pltpu.VMEM((4, 16, cells), jnp.float32),
+            pltpu.VMEM(((2 * planes + 2 * RADIUS) * half, cells), jnp.float32),
+        ],
         compiler_params=PARAMS,
         name="filter",
-    )(low, own, high, pot_low, potential, pot_high, mat, begun)
-
-    team = lax.axis_size(TEAM)
-    mine = lax.all_to_all(second.reshape(team, 2 * planes // team, rows, TILE), TEAM, 0, 0)
+    )(place, own, swap, near, cross, potential, pot_swap, pot_near, pot_cross, jnp.asarray(plane_matrix()))
+
+    team, layer = lax.axis_size(TEAM), lax.axis_size(LAYER)
+    mine = lax.all_to_all(second.reshape(layer, 4 * planes // layer, half, TILE), LAYER, 0, 0)
     theirs = lax.ppermute(mine, ("c",), flip("c", 1))
     count = 2 * team * rows
     total = float(planes * lax.axis_size(SPACE) * cells)
@@ -276,7 +264,6 @@
         name="gram",
     )(place, mine, theirs)
 
-    layer = lax.axis_size(LAYER)
     piece = lax.all_to_all(part.reshape(layer, 5 * TILE // layer, TILE), LAYER, 0, 0).sum(0)
     piece = piece + lax.ppermute(piece, "z", flip("z", 1))
     got = [lax.ppermute(piece, "z", flip("z", b)) for b in (2, 4, 6)]
@@ -288,7 +275,7 @@
         factor_kernel,
         out_shape=(
             jax.ShapeDtypeStruct((count, count), jnp.float32),
-            jax.ShapeDtypeStruct(mine.shape, jnp.float32),
+            jax.ShapeDtypeStruct((team, mine.shape[1], rows, TILE), jnp.float32),
         ),
         in_specs=[SMEM, VMEM, VMEM, VMEM],
         out_specs=(VMEM, VMEM),

time: 115 us -> 114 us (level)
  Pallas kernels: 17.3 us -> 19.2 us
  local copies, waits for them, and re-layouts: 3.46 us -> 1.91 us
    all_to_all x1, blocking collectives: 11.1 us -> 14.1 us  [per_device(): lax.all_to_all(second.reshape(layer, 4 * planes // layer, half, TILE), LA...]
    all_to_all x1, blocking collectives: 14.1 us -> 11.2 us  [per_device(): lax.all_to_all(part.reshape(layer, 5 * TILE // layer, TILE), LAYER, 0, 0)]
    ppermute x4 -> x6, starting transfers between devices: 14 us -> 16.7 us  [the longest x3 9.04 us: per_device(): lax.ppermute(x, SPACE, pairs)]
    unnamed x6 -> x4, local copies, waits for them, and re-layouts: 2.66 us -> 0.01 us
    ppermute x3, starting transfers between devices: 8.01 us -> 5.66 us  [per_device(): got = [lax.ppermute(piece, 'z', flip('z', b)) for b in (2, 4, 6)]]
    ppermute x1, starting transfers between devices: 1.73 us -> 0.09 us  [per_device(): piece = piece + lax.ppermute(piece, 'z', flip('z', 1))]
    ppermute x1, waiting for transfers between devices: 1.17 us -> 2.62 us  [per_device(): piece = piece + lax.ppermute(piece, 'z', flip('z', 1))]
    ppermute x4 -> x6, waiting for transfers between devices: 5.47 us -> 4.5 us  [the longest x3 4.49 us: per_device(): lax.ppermute(potential, SPACE, pairs)]
  transfers between devices with their start and end apart: 10 -> 12, of which waited for: 5 -> 6; matrix products, arithmetic and copies ran while one was open for 0% -> 0% of each run, Pallas kernels for 1% -> 0%
where the time goes in v3:
time: 114 us; the launch traced here: 113 us
  blocking collectives  47.2 us (41%)
  starting transfers between devices  31.3 us (27%)
  Pallas kernels  19.2 us (17%)
  waiting for transfers between devices  13 us (11%)
  local copies, waits for them, and re-layouts  1.91 us (2%)
    pallas_call x1, Pallas kernels, per_device(): pl.pallas_call(factor_kernel, out_shape=(jax.ShapeDtypeStruct((count, cou...  14.6 us
    all_to_all x1, blocking collectives, per_device(): lax.all_to_all(second.reshape(layer, 4 * planes // layer, half, TILE), LA...  14.1 us
    all_to_all x1, blocking collectives, per_device(): lax.all_to_all(part.reshape(layer, 5 * TILE // layer, TILE), LAYER, 0, 0)  11.2 us
    all_to_all x1, blocking collectives, per_device(): lax.all_to_all(jnp.broadcast_to(piece, (layer,) + piece.shape), LAYER, 0, 0)  11.1 us
    all_to_all x1, blocking collectives, per_device(): back = lax.all_to_all(turned, TEAM, 0, 0).reshape(planes, 2, rows, TILE)  10.8 us
    ppermute x3, starting transfers between devices, per_device(): lax.ppermute(x, SPACE, pairs)  9.04 us
    ppermute x3, starting transfers between devices, per_device(): lax.ppermute(potential, SPACE, pairs)  7.68 us
    ppermute x3, starting transfers between devices, per_device(): got = [lax.ppermute(piece, 'z', flip('z', b)) for b in (2, 4, 6)]  5.66 us
  transfers between devices with their start and end apart: 12, of which 6 were waited for; matrix products, arithmetic and copies ran while one was open for 0% of the time, Pallas kernels for 0%

profile of v3, /device:TPU:1, one launch (start us, length us, event | category | flops | bytes accessed | tf_op | source)
XLA Modules:
  0.0 113.4 jit_solution(12846072084169351355)
XLA Ops:
  0.6 0.0 copy-start.1
  0.6 0.0 copy-start
  0.7 1.1 constant_dynamic-slice_fusion
  1.8 6.5 %collective-permute-start.1 = (f32[192,256]{1,0:T(8,128)S(1)}, f32[192,256]{1,0:T(8,128)S(1)}, u32[]{:S(2)}, u32[]{:S(2)}) collective-permute-start(f32[192,256]{1,0:T(8,128)S(1)} %bitcast.17), channel_id=1, source_target_pairs={{0,224},{16,48},{32,0},{48,80},{64,32},{80,112},{96,64},{112,144},... | collective-permute-start | bytes 589832 | tf_op jit(solution)/shard_map/ppermute | solution.py:232
  8.2 2.6 %collective-permute-start.2 = (f32[192,256]{1,0:T(8,128)S(1)}, f32[192,256]{1,0:T(8,128)S(1)}, u32[]{:S(2)}, u32[]{:S(2)}) collective-permute-start(f32[192,256]{1,0:T(8,128)S(1)} %bitcast.22), channel_id=1, source_target_pairs={{0,240},{16,32},{32,16},{48,64},{64,48},{80,96},{96,80},{112,128},... | collective-permute-start | bytes 589832 | tf_op jit(solution)/shard_map/ppermute | solution.py:232
  10.8 0.0 collective-permute-start
  10.8 0.0 copy-done.1
  10.8 2.8 %collective-permute-start.4 = (f32[12,256]{1,0:T(8,128)S(1)}, f32[12,256]{1,0:T(8,128)S(1)}, u32[]{:S(2)}, u32[]{:S(2)}) collective-permute-start(f32[12,256]{1,0:T(8,128)S(1)} %copy-done.1), channel_id=1, source_target_pairs={{0,224},{16,48},{32,0},{48,80},{64,32},{80,112},{96,64},{112,144},... | collective-permute-start | bytes 36872 | tf_op jit(solution)/shard_map/ppermute | solution.py:233
  13.6 0.2 collective-permute-start.3
  13.8 2.6 %collective-permute-done.4.pot_near = f32[12,256]{1,0:T(8,128)S(1)} collective-permute-done((f32[12,256]{1,0:T(8,128)S(1)}, f32[12,256]{1,0:T(8,128)S(1)}, u32[]{:S(2)}, u32[]{:S(2)}) %collective-permute-start.4) | collective-permute-done | bytes 12320 | tf_op jit(solution)/shard_map/ppermute | solution.py:233
  16.4 4.7 %collective-permute-start.5 = (f32[12,256]{1,0:T(8,128)S(1)}, f32[12,256]{1,0:T(8,128)S(1)}, u32[]{:S(2)}, u32[]{:S(2)}) collective-permute-start(f32[12,256]{1,0:T(8,128)S(1)} %copy-done.1), channel_id=1, source_target_pairs={{0,240},{16,32},{32,16},{48,64},{64,48},{80,96},{96,80},{112,128},... | collective-permute-start | bytes 36872 | tf_op jit(solution)/shard_map/ppermute | solution.py:233
  21.1 0.1 pad_add_fusion.place
  21.2 1.9 %collective-permute-done.3.pot_swap = f32[12,256]{1,0:T(8,128)S(1)} collective-permute-done((f32[12,256]{1,0:T(8,128)S(1)}, f32[12,256]{1,0:T(8,128)S(1)}, u32[]{:S(2)}, u32[]{:S(2)}) %collective-permute-start.3) | collective-permute-done | bytes 12320 | tf_op jit(solution)/shard_map/ppermute | solution.py:233
  23.1 0.0 collective-permute-done.5.pot_cross
  23.1 0.0 collective-permute-done.1.near
  23.1 0.0 collective-permute-done.2.cross
  23.1 0.0 collective-permute-done.swap
  23.1 0.0 copy-done
  23.1 2.6 %filter.1 = f32[48,16,128]{2,1,0:T(8,128)S(1)} custom-call(s32[2]{0:T(128)S(1)} %pad_add_fusion.place, f32[192,256]{1,0:T(8,128)S(1)} %bitcast.18, f32[192,256]{1,0:T(8,128)S(1)} %collective-permute-done.swap, f32[192,256]{1,0:T(8,128)S(1)} %collective-permute-done.1.near, f32[192,256]{1,0:T(8,128)S(1)} %collective-permute-done.2.cross, ...), custom_call_target="tpu_custom_call" | custom-call | tf_op jit(solution)/shard_map/filter/pallas_call | solution.py:236
  25.7 14.1 %all_to_all.20.own = f32[16,3,16,128]{3,2,1,0:T(8,128)S(1)} all-to-all(f32[16,3,16,128]{3,2,1,0:T(8,128)S(1)} %bitcast.14), channel_id=1, replica_groups=mesh['z'=8,'xh'=2,'y'=4,'xl'=2,'c'=2] {'xh','y','xl'}, dimensions={0} | all-to-all | bytes 786432 | tf_op jit(solution)/shard_map/all_to_all | solution.py:251
  39.7 4.0 %collective-permute-start.6 = (f32[16,3,16,128]{3,2,1,0:T(8,128)S(1)}, f32[16,3,16,128]{3,2,1,0:T(8,128)S(1)}, u32[]{:S(2)}, u32[]{:S(2)}) collective-permute-start(f32[16,3,16,128]{3,2,1,0:T(8,128)S(1)} %all_to_all.20.own), channel_id=1, source_target_pairs={{0,1},{1,0},{2,3},{3,2},{4,5},{5,4},{6,7},{7,6},{8,9},{9,8},{10,11... | collective-permute-start | bytes 1179656 | tf_op jit(solution)/shard_map/ppermute | solution.py:252
  43.7 1.3 %collective-permute-done.6.other = f32[16,3,16,128]{3,2,1,0:T(8,128)S(1)} collective-permute-done((f32[16,3,16,128]{3,2,1,0:T(8,128)S(1)}, f32[16,3,16,128]{3,2,1,0:T(8,128)S(1)}, u32[]{:S(2)}, u32[]{:S(2)}) %collective-permute-start.6) | collective-permute-done | bytes 393248 | tf_op jit(solution)/shard_map/ppermute | solution.py:252
  45.0 1.9 %gram.1 = (f32[640,128]{1,0:T(8,128)S(1)}, f32[512,384]{1,0:T(8,128)S(1)}) custom-call(s32[2]{0:T(128)S(1)} %pad_add_fusion.place, f32[16,3,16,128]{3,2,1,0:T(8,128)S(1)} %all_to_all.20.own, f32[16,3,16,128]{3,2,1,0:T(8,128)S(1)} %collective-permute-done.6.other), custom_call_target="tpu_custom_call" | custom-call | tf_op jit(solution)/shard_map/gram/pallas_call | solution.py:255
  47.0 11.2 %all_to_all.21 = f32[16,40,128]{2,1,0:T(8,128)S(1)} all-to-all(f32[16,40,128]{2,1,0:T(8,128)S(1)} %bitcast.19), channel_id=1, replica_groups=mesh['z'=8,'xh'=2,'y'=4,'xl'=2,'c'=2] {'xh','y','xl'}, dimensions={0} | all-to-all | bytes 655360 | tf_op jit(solution)/shard_map/all_to_all | solution.py:267
  58.2 0.1 collective-permute-start.7
  58.3 2.6 %collective-permute-done.7 = f32[40,128]{1,0:T(8,128)S(1)} collective-permute-done((f32[40,128]{1,0:T(8,128)S(1)}, f32[40,128]{1,0:T(8,128)S(1)}, u32[]{:S(2)}, u32[]{:S(2)}) %collective-permute-start.7) | collective-permute-done | bytes 20512 | tf_op jit(solution)/shard_map/ppermute | solution.py:268
  60.9 2.4 %collective-permute-start.10 = (f32[40,128]{1,0:T(8,128)S(1)}, f32[40,128]{1,0:T(8,128)S(1)}, u32[]{:S(2)}, u32[]{:S(2)}) collective-permute-start(f32[40,128]{1,0:T(8,128)S(1)} %add.20), channel_id=1, source_target_pairs={{0,192},{32,224},{64,128},{96,160},{128,64},{160,96},{192,0},{224,... | collective-permute-start | bytes 61448 | tf_op jit(solution)/shard_map/ppermute | solution.py:269
  63.3 1.8 %collective-permute-start.9 = (f32[40,128]{1,0:T(8,128)S(1)}, f32[40,128]{1,0:T(8,128)S(1)}, u32[]{:S(2)}, u32[]{:S(2)}) collective-permute-start(f32[40,128]{1,0:T(8,128)S(1)} %add.20), channel_id=1, source_target_pairs={{0,128},{32,160},{64,192},{96,224},{128,0},{160,32},{192,64},{224,... | collective-permute-start | bytes 61448 | tf_op jit(solution)/shard_map/ppermute | solution.py:269
  65.1 1.5 %collective-permute-start.8 = (f32[40,128]{1,0:T(8,128)S(1)}, f32[40,128]{1,0:T(8,128)S(1)}, u32[]{:S(2)}, u32[]{:S(2)}) collective-permute-start(f32[40,128]{1,0:T(8,128)S(1)} %add.20), channel_id=1, source_target_pairs={{0,64},{32,96},{64,0},{96,32},{128,192},{160,224},{192,128},{224,1... | collective-permute-start | bytes 61448 | tf_op jit(solution)/shard_map/ppermute | solution.py:269
  66.6 0.0 collective-permute-done.10
  66.6 3.3 %collective-permute-done.9 = f32[40,128]{1,0:T(8,128)S(1)} collective-permute-done((f32[40,128]{1,0:T(8,128)S(1)}, f32[40,128]{1,0:T(8,128)S(1)}, u32[]{:S(2)}, u32[]{:S(2)}) %collective-permute-start.9) | collective-permute-done | bytes 20512 | tf_op jit(solution)/shard_map/ppermute | solution.py:269
  69.9 0.0 collective-permute-done.8
  69.9 11.1 %all_to_all.22 = f32[16,40,128]{2,1,0:T(8,128)S(1)} all-to-all(f32[16,40,128]{2,1,0:T(8,128)S(1)} %broadcast_in_dim.3), channel_id=1, replica_groups=mesh['z'=8,'xh'=2,'y'=4,'xl'=2,'c'=2] {'xh','y','xl'}, dimensions={0} | all-to-all | bytes 655360 | tf_op jit(solution)/shard_map/all_to_all | solution.py:271
  81.0 4.9 %collective-permute-start.11 = (f32[640,128]{1,0:T(8,128)S(1)}, f32[640,128]{1,0:T(8,128)S(1)}, u32[]{:S(2)}, u32[]{:S(2)}) collective-permute-start(f32[640,128]{1,0:T(8,128)S(1)} %bitcast.15), channel_id=1, source_target_pairs={{0,1},{1,0},{2,3},{3,2},{4,5},{5,4},{6,7},{7,6},{8,9},{9,8},{10,11... | collective-permute-start | bytes 983048 | tf_op jit(solution)/shard_map/ppermute | solution.py:273
  85.9 1.3 %collective-permute-done.11.other = f32[640,128]{1,0:T(8,128)S(1)} collective-permute-done((f32[640,128]{1,0:T(8,128)S(1)}, f32[640,128]{1,0:T(8,128)S(1)}, u32[]{:S(2)}, u32[]{:S(2)}) %collective-permute-start.11) | collective-permute-done | bytes 327712 | tf_op jit(solution)/shard_map/ppermute | solution.py:273
  87.2 14.6 %factor.1 = (f32[512,512]{1,0:T(8,128)}, f32[8,3,32,128]{3,2,1,0:T(8,128)S(1)}) custom-call(s32[2]{0:T(128)S(1)} %pad_add_fusion.place, f32[640,128]{1,0:T(8,128)S(1)} %bitcast.16, f32[640,128]{1,0:T(8,128)S(1)} %collective-permute-done.11.other, f32[512,384]{1,0:T(8,128)S(1)} %get-tuple-element.7.fields), custom_call_target="tpu_custom_call" | custom-call | tf_op jit(solution)/shard_map/factor/pallas_call | solution.py:274
  101.8 10.8 %all_to_all.23 = f32[8,3,32,128]{3,2,1,0:T(8,128)S(1)} all-to-all(f32[8,3,32,128]{3,2,1,0:T(8,128)S(1)} %get-tuple-element.8), channel_id=1, replica_groups=mesh['z'=8,'xh'=2,'y'=4,'xl'=2,'c'=2] {'y','xl'}, dimensions={0} | all-to-all | bytes 786432 | tf_op jit(solution)/shard_map/all_to_all | solution.py:286
  112.6 0.8 copy.8
  (4 shorter events, 0.1 us)
Async XLA Ops:
  0.6 10.2 %copy-start.1 = (f32[12,256]{1,0:T(8,128)S(1)}, f32[12,256]{1,0:T(8,128)}, u32[]{:S(2)}) copy-start(f32[12,256]{1,0:T(8,128)} %pot.1) | copy-start | bytes 36868
  0.6 22.4 %copy-start = (f32[256,256]{1,0:T(8,128)S(1)}, f32[256,256]{1,0:T(8,128)}, u32[]{:S(2)}) copy-start(f32[256,256]{1,0:T(8,128)} %constant.20.clone.mat) | copy-start | bytes 786436
  1.8 21.3 %collective-permute-start.1 = (f32[192,256]{1,0:T(8,128)S(1)}, f32[192,256]{1,0:T(8,128)S(1)}, u32[]{:S(2)}, u32[]{:S(2)}) collective-permute-start(f32[192,256]{1,0:T(8,128)S(1)} %bitcast.17), channel_id=1, source_target_pairs={{0,224},{16,48},{32,0},{48,80},{64,32},{80,112},{96,64},{112,144},... | collective-permute-start | bytes 589832 | tf_op jit(solution)/shard_map/ppermute | solution.py:232
  8.2 14.8 %collective-permute-start.2 = (f32[192,256]{1,0:T(8,128)S(1)}, f32[192,256]{1,0:T(8,128)S(1)}, u32[]{:S(2)}, u32[]{:S(2)}) collective-permute-start(f32[192,256]{1,0:T(8,128)S(1)} %bitcast.22), channel_id=1, source_target_pairs={{0,240},{16,32},{32,16},{48,64},{64,48},{80,96},{96,80},{112,128},... | collective-permute-start | bytes 589832 | tf_op jit(solution)/shard_map/ppermute | solution.py:232
  10.8 12.3 %collective-permute-start = (f32[192,256]{1,0:T(8,128)S(1)}, f32[192,256]{1,0:T(8,128)S(1)}, u32[]{:S(2)}, u32[]{:S(2)}) collective-permute-start(f32[192,256]{1,0:T(8,128)S(1)} %bitcast.23), channel_id=1, source_target_pairs={{0,16},{16,0},{32,48},{48,32},{64,80},{80,64},{96,112},{112,96},{1... | collective-permute-start | bytes 589832 | tf_op jit(solution)/shard_map/ppermute | solution.py:232
  10.8 5.6 %collective-permute-start.4 = (f32[12,256]{1,0:T(8,128)S(1)}, f32[12,256]{1,0:T(8,128)S(1)}, u32[]{:S(2)}, u32[]{:S(2)}) collective-permute-start(f32[12,256]{1,0:T(8,128)S(1)} %copy-done.1), channel_id=1, source_target_pairs={{0,224},{16,48},{32,0},{48,80},{64,32},{80,112},{96,64},{112,144},... | collective-permute-start | bytes 36872 | tf_op jit(solution)/shard_map/ppermute | solution.py:233
  13.6 9.4 %collective-permute-start.3 = (f32[12,256]{1,0:T(8,128)S(1)}, f32[12,256]{1,0:T(8,128)S(1)}, u32[]{:S(2)}, u32[]{:S(2)}) collective-permute-start(f32[12,256]{1,0:T(8,128)S(1)} %copy-done.1), channel_id=1, source_target_pairs={{0,16},{16,0},{32,48},{48,32},{64,80},{80,64},{96,112},{112,96},{1... | collective-permute-start | bytes 36872 | tf_op jit(solution)/shard_map/ppermute | solution.py:233
  16.4 6.7 %collective-permute-start.5 = (f32[12,256]{1,0:T(8,128)S(1)}, f32[12,256]{1,0:T(8,128)S(1)}, u32[]{:S(2)}, u32[]{:S(2)}) collective-permute-start(f32[12,256]{1,0:T(8,128)S(1)} %copy-done.1), channel_id=1, source_target_pairs={{0,240},{16,32},{32,16},{48,64},{64,48},{80,96},{96,80},{112,128},... | collective-permute-start | bytes 36872 | tf_op jit(solution)/shard_map/ppermute | solution.py:233
  39.7 5.3 %collective-permute-start.6 = (f32[16,3,16,128]{3,2,1,0:T(8,128)S(1)}, f32[16,3,16,128]{3,2,1,0:T(8,128)S(1)}, u32[]{:S(2)}, u32[]{:S(2)}) collective-permute-start(f32[16,3,16,128]{3,2,1,0:T(8,128)S(1)} %all_to_all.20.own), channel_id=1, source_target_pairs={{0,1},{1,0},{2,3},{3,2},{4,5},{5,4},{6,7},{7,6},{8,9},{9,8},{10,11... | collective-permute-start | bytes 1179656 | tf_op jit(solution)/shard_map/ppermute | solution.py:252
  58.2 2.7 %collective-permute-start.7 = (f32[40,128]{1,0:T(8,128)S(1)}, f32[40,128]{1,0:T(8,128)S(1)}, u32[]{:S(2)}, u32[]{:S(2)}) collective-permute-start(f32[40,128]{1,0:T(8,128)S(1)} %reduce_sum.9), channel_id=1, source_target_pairs={{0,32},{32,0},{64,96},{96,64},{128,160},{160,128},{192,224},{224,1... | collective-permute-start | bytes 61448 | tf_op jit(solution)/shard_map/ppermute | solution.py:268
  60.9 5.7 %collective-permute-start.10 = (f32[40,128]{1,0:T(8,128)S(1)}, f32[40,128]{1,0:T(8,128)S(1)}, u32[]{:S(2)}, u32[]{:S(2)}) collective-permute-start(f32[40,128]{1,0:T(8,128)S(1)} %add.20), channel_id=1, source_target_pairs={{0,192},{32,224},{64,128},{96,160},{128,64},{160,96},{192,0},{224,... | collective-permute-start | bytes 61448 | tf_op jit(solution)/shard_map/ppermute | solution.py:269
  63.3 6.5 %collective-permute-start.9 = (f32[40,128]{1,0:T(8,128)S(1)}, f32[40,128]{1,0:T(8,128)S(1)}, u32[]{:S(2)}, u32[]{:S(2)}) collective-permute-start(f32[40,128]{1,0:T(8,128)S(1)} %add.20), channel_id=1, source_target_pairs={{0,128},{32,160},{64,192},{96,224},{128,0},{160,32},{192,64},{224,... | collective-permute-start | bytes 61448 | tf_op jit(solution)/shard_map/ppermute | solution.py:269
  65.1 4.8 %collective-permute-start.8 = (f32[40,128]{1,0:T(8,128)S(1)}, f32[40,128]{1,0:T(8,128)S(1)}, u32[]{:S(2)}, u32[]{:S(2)}) collective-permute-start(f32[40,128]{1,0:T(8,128)S(1)} %add.20), channel_id=1, source_target_pairs={{0,64},{32,96},{64,0},{96,32},{128,192},{160,224},{192,128},{224,1... | collective-permute-start | bytes 61448 | tf_op jit(solution)/shard_map/ppermute | solution.py:269
  81.0 6.1 %collective-permute-start.11 = (f32[640,128]{1,0:T(8,128)S(1)}, f32[640,128]{1,0:T(8,128)S(1)}, u32[]{:S(2)}, u32[]{:S(2)}) collective-permute-start(f32[640,128]{1,0:T(8,128)S(1)} %bitcast.15), channel_id=1, source_target_pairs={{0,1},{1,0},{2,3},{3,2},{4,5},{5,4},{6,7},{7,6},{8,9},{9,8},{10,11... | collective-permute-start | bytes 983048 | tf_op jit(solution)/shard_map/ppermute | solution.py:273

commit v4 on v3

--- a/solution.py
+++ b/solution.py
@@ -48,61 +48,76 @@
     )
 
 
-def filter_kernel(
-    rows, planes, place, own, swap, near, cross, pot, pot_swap, pot_near, pot_cross, mat, out, field, level, first
-):
-    h = place[1]
+def filter_kernel(rows, planes, side, own, swap, near, cross, mat, out, first):
     size = planes * rows
-    for k, data, values in (
-        (1 + h, own, pot),
-        (2 - h, swap, pot_swap),
-        (3 - 3 * h, near, pot_near),
-        (3 * h, cross, pot_cross),
-    ):
-        field[pl.ds(pl.multiple_of(k * size, size), size), :] = data[...]
-        level[k, 0:planes, :] = (values[...] - SHIFT_MID) / HALF_SPAN
-
-    def plane(ref, p):
-        return ref[p * rows : (p + 1) * rows, :]
-
-    def row(p):
-        return level[p // planes, p % planes : p % planes + 1, :]
-
-    skip = planes - RADIUS
     count = 2 * planes + 2 * RADIUS
-    first[...] = dot32(field[skip * rows : (skip + count) * rows, :], mat[...], ((1,), (0,)))
-    for q in range(count):
-        p = q + skip
-        acc = plane(first, q) + row(p) * plane(field, p)
-        for k in range(RADIUS):
-            acc = acc + (SCALE * COEFS[k]) * (plane(field, p + k + 1) + plane(field, p - k - 1))
-        first[q * rows : (q + 1) * rows, :] = acc
-    inner = dot32(first[RADIUS * rows : RADIUS * rows + 2 * size, :], mat[...], ((1,), (0,)))
-    for z in range(2 * planes):
-        q = z + RADIUS
-        acc = inner[z * rows : (z + 1) * rows, :] + row(z + planes) * plane(first, q)
-        for k in range(RADIUS):
-            acc = acc + (SCALE * COEFS[k]) * (plane(first, q + k + 1) + plane(first, q - k - 1))
-        second = 2.0 * acc - plane(field, z + planes)
-        out[2 * z] = second[:, :TILE]
-        out[2 * z + 1] = second[:, TILE:]
-
-
-def gram_kernel(scale, place, own, other, out, stack):
-    c = place[0]
+
+    def filter_slabs(slabs):
+        def field(p):
+            return slabs[p // planes][p % planes * rows : (p % planes + 1) * rows, :]
+
+        def level(p):
+            at = size + p % planes
+            return (slabs[p // planes][at : at + 1, :] - SHIFT_MID) / HALF_SPAN
+
+        def plane(q):
+            return first[q * rows : (q + 1) * rows, :]
+
+        skip = planes - RADIUS
+        for k, slab in enumerate(slabs):
+            begin, end = max(k * planes, skip), min((k + 1) * planes, skip + count)
+            part = slab[(begin - k * planes) * rows : (end - k * planes) * rows, :]
+            first[(begin - skip) * rows : (end - skip) * rows, :] = dot32(part, mat[...], ((1,), (0,)))
+        for q in range(count):
+            p = q + skip
+            acc = plane(q) + level(p) * field(p)
+            for k in range(RADIUS):
+                acc = acc + (SCALE * COEFS[k]) * (field(p + k + 1) + field(p - k - 1))
+            first[q * rows : (q + 1) * rows, :] = acc
+        inner = dot32(first[RADIUS * rows : RADIUS * rows + 2 * size, :], mat[...], ((1,), (0,)))
+        for z in range(2 * planes):
+            q = z + RADIUS
+            acc = inner[z * rows : (z + 1) * rows, :] + level(z + planes) * plane(q)
+            for k in range(RADIUS):
+                acc = acc + (SCALE * COEFS[k]) * (plane(q + k + 1) + plane(q - k - 1))
+            second = 2.0 * acc - field(z + planes)
+            out[2 * z] = second[:, :TILE]
+            out[2 * z + 1] = second[:, TILE:]
+
+    @pl.when(side[0] == 0)
+    def _():
+        filter_slabs((cross, own, swap, near))
+
+    @pl.when(side[0] == 1)
+    def _():
+        filter_slabs((near, swap, own, cross))
+
+
+def gram_kernel(scale, core, own, other, out, stack):
     rows = own.shape[2]
     team = own.shape[0] // 2
-    for half, ref in ((c, own), (1 - c, other)):
-        for s in range(own.shape[0]):
-            at = pl.multiple_of((s % team * 4 + half * 2 + s // team) * rows, rows)
-            for t in range(own.shape[1]):
-                stack[pl.ds(at, rows), t * TILE : (t + 1) * TILE] = ref[s, t]
-    for k in range(5):
-        i = jnp.where(c == 0, BLOCKS[0][k][0], BLOCKS[1][k][0])
-        j = jnp.where(c == 0, BLOCKS[0][k][1], BLOCKS[1][k][1])
-        a = stack[pl.ds(pl.multiple_of(i * TILE, TILE), TILE), :]
-        b = stack[pl.ds(pl.multiple_of(j * TILE, TILE), TILE), :]
-        out[k * TILE : (k + 1) * TILE, :] = dot32(a, b, ((1,), (1,))) * scale
+
+    def gram_tiles(c):
+        for half, ref in ((c, own), (1 - c, other)):
+            for s in range(own.shape[0]):
+                at = (s % team * 4 + half * 2 + s // team) * rows
+                for t in range(own.shape[1]):
+                    stack[at : at + rows, t * TILE : (t + 1) * TILE] = ref[s, t]
+        for k, wide in ((0, 1), (1, 2), (3, 2)):
+            i, j = BLOCKS[c][k]
+            tiles = scale * dot32(
+                stack[i * TILE : (i + 1) * TILE, :], stack[j * TILE : (j + wide) * TILE, :], ((1,), (1,))
+            )
+            for w in range(wide):
+                out[(k + w) * TILE : (k + w + 1) * TILE, :] = tiles[:, w * TILE : (w + 1) * TILE]
+
+    @pl.when(core[0] == 0)
+    def _():
+        gram_tiles(0)
+
+    @pl.when(core[0] == 1)
+    def _():
+        gram_tiles(1)
 
 
 def line(block, row):
@@ -169,8 +184,8 @@
             )
 
 
-def factor_kernel(place, own, other, fields, corr, out, work):
-    first = place[0] == 0
+def factor_kernel(core, own, other, fields, corr, out, work):
+    first = core[0] == 0
     for k in range(5):
         rows = slice(k * TILE, (k + 1) * TILE)
         a, b = own[rows, :], other[rows, :]
@@ -191,7 +206,7 @@
             if side.start < side.stop:
                 work[own_rows, side] = dot32(inverse, work[own_rows, side], ((1,), (0,)))
         mine = [
-            work[pl.ds(pl.multiple_of(k + 2 * i * size + place[0] * size, size), size), 0 : k + TILE]
+            work[pl.ds(pl.multiple_of(k + 2 * i * size + core[0] * size, size), size), 0 : k + TILE]
             for i in range(pairs)
         ]
         turned = dot32(jnp.concatenate(mine, axis=0), fields[0 : k + TILE, :], ((1,), (0,)))
@@ -219,33 +234,30 @@
 def per_device(orbitals, potential):
     planes, rows, cells = orbitals.shape
     side = lax.axis_index("xh")
-    place = jnp.stack([lax.axis_index("c"), side]).astype(jnp.int32)
+    core = lax.axis_index("c").astype(jnp.int32).reshape(1)
     half = rows // 2
     own, other = (
-        lax.dynamic_slice_in_dim(orbitals, at * half, half, 1).reshape(planes * half, cells)
+        jnp.concatenate(
+            [lax.dynamic_slice_in_dim(orbitals, at * half, half, 1).reshape(planes * half, cells), potential]
+        )
         for at in (side, 1 - side)
     )
     slabs = lax.axis_size(SPACE)
     swap = [(s, s ^ 1) for s in range(slabs)]
     near = [(s, (s + 2 * (2 * (s % 2) - 1)) % slabs) for s in range(slabs)]
     cross = [(s, (s + 2 * (s % 2) - 1) % slabs) for s in range(slabs)]
-    data = [lax.ppermute(x, SPACE, pairs) for x, pairs in ((other, cross), (other, swap), (own, near))][::-1]
-    pots = [lax.ppermute(potential, SPACE, pairs) for pairs in (cross, swap, near)][::-1]
-    near, swap, cross = data
-    pot_near, pot_swap, pot_cross = pots
+    cross, swap, near = (
+        lax.ppermute(x, SPACE, pairs) for x, pairs in ((other, cross), (other, swap), (own, near))
+    )
     second = pl.pallas_call(
         functools.partial(filter_kernel, half, planes),
         out_shape=jax.ShapeDtypeStruct((4 * planes, half, TILE), jnp.float32),
-        in_specs=[SMEM] + [VMEM] * 9,
+        in_specs=[SMEM] + [VMEM] * 5,
         out_specs=VMEM,
-        scratch_shapes=[
-            pltpu.VMEM((4 * planes * half, cells), jnp.float32),
-            pltpu.VMEM((4, 16, cells), jnp.float32),
-            pltpu.VMEM(((2 * planes + 2 * RADIUS) * half, cells), jnp.float32),
-        ],
+        scratch_shapes=[pltpu.VMEM(((2 * planes + 2 * RADIUS) * half, cells), jnp.float32)],
         compiler_params=PARAMS,
         name="filter",
-    )(place, own, swap, near, cross, potential, pot_swap, pot_near, pot_cross, jnp.asarray(plane_matrix()))
+    )(side.astype(jnp.int32).reshape(1), own, swap, near, cross, jnp.asarray(plane_matrix()))
 
     team, layer = lax.axis_size(TEAM), lax.axis_size(LAYER)
     mine = lax.all_to_all(second.reshape(layer, 4 * planes // layer, half, TILE), LAYER, 0, 0)
@@ -262,7 +274,7 @@
         out_specs=(VMEM, VMEM),
         compiler_params=PARAMS,
         name="gram",
-    )(place, mine, theirs)
+    )(core, mine, theirs)
 
     piece = lax.all_to_all(part.reshape(layer, 5 * TILE // layer, TILE), LAYER, 0, 0).sum(0)
     piece = piece + lax.ppermute(piece, "z", flip("z", 1))
@@ -282,7 +294,7 @@
         scratch_shapes=[pltpu.VMEM((count, count), jnp.float32)],
         compiler_params=PARAMS,
         name="factor",
-    )(place, mine_g, theirs_g, fields)
+    )(core, mine_g, theirs_g, fields)
     back = lax.all_to_all(turned, TEAM, 0, 0).reshape(planes, 2, rows, TILE)
     return (back.transpose(0, 2, 1, 3).reshape(planes, rows, cells), correlation)
 

time: 114 us -> 108 us (0.947)
  starting transfers between devices: 31.3 us -> 23.6 us
  waiting for transfers between devices: 13 us -> 19.2 us
  Pallas kernels: 19.2 us -> 17 us
  blocking collectives: 47.2 us -> 45.8 us
    ppermute x3, waiting for transfers between devices: 0.01 us -> 9.55 us  [per_device(): lax.ppermute(x, SPACE, pairs)]
    ppermute x3 -> x0, starting transfers between devices: 7.68 us -> none  [per_device(): lax.ppermute(potential, SPACE, pairs)]
    ppermute x3 -> x0, waiting for transfers between devices: 4.49 us -> none  [per_device(): lax.ppermute(potential, SPACE, pairs)]
    ppermute x1, starting transfers between devices: 3.96 us -> 2.45 us  [per_device(): theirs = lax.ppermute(mine, ('c',), flip('c', 1))]
    all_to_all x1, blocking collectives: 14.1 us -> 12.7 us  [per_device(): lax.all_to_all(second.reshape(layer, 4 * planes // layer, half, TILE), LA...]
  transfers between devices with their start and end apart: 12 -> 9, of which waited for: 6 -> 6; matrix products, arithmetic and copies ran while one was open for 0% -> 0% of each run, Pallas kernels for 0% -> 0%
where the time goes in v4:
time: 108 us
  blocking collectives  45.8 us (42%)
  starting transfers between devices  23.6 us (22%)
  waiting for transfers between devices  19.2 us (18%)
  Pallas kernels  17 us (16%)
  local copies, waits for them, and re-layouts  1.87 us (2%)
    pallas_call x1, Pallas kernels, per_device(): pl.pallas_call(factor_kernel, out_shape=(jax.ShapeDtypeStruct((count, cou...  14.1 us
    all_to_all x1, blocking collectives, per_device(): lax.all_to_all(second.reshape(layer, 4 * planes // layer, half, TILE), LA...  12.7 us
    all_to_all x1, blocking collectives, per_device(): lax.all_to_all(part.reshape(layer, 5 * TILE // layer, TILE), LAYER, 0, 0)  11.2 us
    all_to_all x1, blocking collectives, per_device(): lax.all_to_all(jnp.broadcast_to(piece, (layer,) + piece.shape), LAYER, 0, 0)  11.1 us
    all_to_all x1, blocking collectives, per_device(): back = lax.all_to_all(turned, TEAM, 0, 0).reshape(planes, 2, rows, TILE)  10.8 us
    ppermute x3, starting transfers between devices, per_device(): lax.ppermute(x, SPACE, pairs)  9.68 us
    ppermute x3, waiting for transfers between devices, per_device(): lax.ppermute(x, SPACE, pairs)  9.55 us
    ppermute x3, starting transfers between devices, per_device(): got = [lax.ppermute(piece, 'z', flip('z', b)) for b in (2, 4, 6)]  6.2 us
  transfers between devices with their start and end apart: 9, of which 6 were waited for; matrix products, arithmetic and copies ran while one was open for 0% of the time, Pallas kernels for 0%

profile of v4, /device:TPU:1, one launch (start us, length us, event | category | flops | bytes accessed | tf_op | source)
XLA Modules:
  0.0 108.2 jit_solution(16668456183249408384)
XLA Ops:
  0.6 0.0 copy-start.1
  0.6 1.1 constant_dynamic-slice_fusion
  1.7 0.0 copy-done.1
  1.7 0.0 copy-start
  1.8 9.0 %collective-permute-start.2 = (f32[204,256]{1,0:T(8,128)S(1)}, f32[204,256]{1,0:T(8,128)S(1)}, u32[]{:S(2)}, u32[]{:S(2)}) collective-permute-start(f32[204,256]{1,0:T(8,128)S(1)} %get-tuple-element.12), channel_id=1, source_target_pairs={{0,240},{16,32},{32,16},{48,64},{64,48},{80,96},{96,80},{112,128},... | collective-permute-start | bytes 626696 | tf_op jit(solution)/shard_map/ppermute | solution.py:250
  10.7 0.0 collective-permute-start
  10.7 0.7 collective-permute-start.1
  11.5 4.2 %collective-permute-done.2.cross = f32[204,256]{1,0:T(8,128)S(1)} collective-permute-done((f32[204,256]{1,0:T(8,128)S(1)}, f32[204,256]{1,0:T(8,128)S(1)}, u32[]{:S(2)}, u32[]{:S(2)}) %collective-permute-start.2) | collective-permute-done | bytes 208928 | tf_op jit(solution)/shard_map/ppermute | solution.py:250
  15.7 5.3 %collective-permute-done.swap = f32[204,256]{1,0:T(8,128)S(1)} collective-permute-done((f32[204,256]{1,0:T(8,128)S(1)}, f32[204,256]{1,0:T(8,128)S(1)}, u32[]{:S(2)}, u32[]{:S(2)}) %collective-permute-start) | collective-permute-done | bytes 208928 | tf_op jit(solution)/shard_map/ppermute | solution.py:250
  21.0 0.0 collective-permute-done.1.near
  21.0 0.0 copy-done
  21.0 1.8 %filter.1 = f32[48,16,128]{2,1,0:T(8,128)S(1)} custom-call(s32[1]{0:T(128)} %bitcast.1.side, f32[204,256]{1,0:T(8,128)S(1)} %get-tuple-element.13.own, f32[204,256]{1,0:T(8,128)S(1)} %collective-permute-done.swap, f32[204,256]{1,0:T(8,128)S(1)} %collective-permute-done.1.near, f32[204,256]{1,0:T(8,128)S(1)} %collective-permute-done.2.cross, ...), custom_call_target="tpu_custom_call" | custom-call | tf_op jit(solution)/shard_map/filter/pallas_call | solution.py:252
  22.8 12.7 %all_to_all.20.own = f32[16,3,16,128]{3,2,1,0:T(8,128)S(1)} all-to-all(f32[16,3,16,128]{3,2,1,0:T(8,128)S(1)} %bitcast.14), channel_id=1, replica_groups=mesh['z'=8,'xh'=2,'y'=4,'xl'=2,'c'=2] {'xh','y','xl'}, dimensions={0} | all-to-all | bytes 786432 | tf_op jit(solution)/shard_map/all_to_all | solution.py:263
  35.6 2.5 %collective-permute-start.3 = (f32[16,3,16,128]{3,2,1,0:T(8,128)S(1)}, f32[16,3,16,128]{3,2,1,0:T(8,128)S(1)}, u32[]{:S(2)}, u32[]{:S(2)}) collective-permute-start(f32[16,3,16,128]{3,2,1,0:T(8,128)S(1)} %all_to_all.20.own), channel_id=1, source_target_pairs={{0,1},{1,0},{2,3},{3,2},{4,5},{5,4},{6,7},{7,6},{8,9},{9,8},{10,11... | collective-permute-start | bytes 1179656 | tf_op jit(solution)/shard_map/ppermute | solution.py:264
  38.0 1.3 %collective-permute-done.3.other = f32[16,3,16,128]{3,2,1,0:T(8,128)S(1)} collective-permute-done((f32[16,3,16,128]{3,2,1,0:T(8,128)S(1)}, f32[16,3,16,128]{3,2,1,0:T(8,128)S(1)}, u32[]{:S(2)}, u32[]{:S(2)}) %collective-permute-start.3) | collective-permute-done | bytes 393248 | tf_op jit(solution)/shard_map/ppermute | solution.py:264
  39.4 1.1 %gram.1 = (f32[640,128]{1,0:T(8,128)S(1)}, f32[512,384]{1,0:T(8,128)S(1)}) custom-call(s32[1]{0:T(128)} %bitcast.core, f32[16,3,16,128]{3,2,1,0:T(8,128)S(1)} %all_to_all.20.own, f32[16,3,16,128]{3,2,1,0:T(8,128)S(1)} %collective-permute-done.3.other), custom_call_target="tpu_custom_call" | custom-call | tf_op jit(solution)/shard_map/gram/pallas_call | solution.py:267
  40.5 11.2 %all_to_all.21 = f32[16,40,128]{2,1,0:T(8,128)S(1)} all-to-all(f32[16,40,128]{2,1,0:T(8,128)S(1)} %bitcast.17), channel_id=1, replica_groups=mesh['z'=8,'xh'=2,'y'=4,'xl'=2,'c'=2] {'xh','y','xl'}, dimensions={0} | all-to-all | bytes 655360 | tf_op jit(solution)/shard_map/all_to_all | solution.py:279
  51.7 0.1 collective-permute-start.4
  51.8 2.6 %collective-permute-done.4 = f32[40,128]{1,0:T(8,128)S(1)} collective-permute-done((f32[40,128]{1,0:T(8,128)S(1)}, f32[40,128]{1,0:T(8,128)S(1)}, u32[]{:S(2)}, u32[]{:S(2)}) %collective-permute-start.4) | collective-permute-done | bytes 20512 | tf_op jit(solution)/shard_map/ppermute | solution.py:280
  54.4 4.0 %collective-permute-start.7 = (f32[40,128]{1,0:T(8,128)S(1)}, f32[40,128]{1,0:T(8,128)S(1)}, u32[]{:S(2)}, u32[]{:S(2)}) collective-permute-start(f32[40,128]{1,0:T(8,128)S(1)} %add.20), channel_id=1, source_target_pairs={{0,192},{32,224},{64,128},{96,160},{128,64},{160,96},{192,0},{224,... | collective-permute-start | bytes 61448 | tf_op jit(solution)/shard_map/ppermute | solution.py:281
  58.5 1.9 %collective-permute-start.6 = (f32[40,128]{1,0:T(8,128)S(1)}, f32[40,128]{1,0:T(8,128)S(1)}, u32[]{:S(2)}, u32[]{:S(2)}) collective-permute-start(f32[40,128]{1,0:T(8,128)S(1)} %add.20), channel_id=1, source_target_pairs={{0,128},{32,160},{64,192},{96,224},{128,0},{160,32},{192,64},{224,... | collective-permute-start | bytes 61448 | tf_op jit(solution)/shard_map/ppermute | solution.py:281
  60.4 0.3 collective-permute-start.5
  60.6 0.0 collective-permute-done.7
  60.6 4.4 %collective-permute-done.6 = f32[40,128]{1,0:T(8,128)S(1)} collective-permute-done((f32[40,128]{1,0:T(8,128)S(1)}, f32[40,128]{1,0:T(8,128)S(1)}, u32[]{:S(2)}, u32[]{:S(2)}) %collective-permute-start.6) | collective-permute-done | bytes 20512 | tf_op jit(solution)/shard_map/ppermute | solution.py:281
  65.0 0.0 collective-permute-done.5
  65.1 11.1 %all_to_all.22 = f32[16,40,128]{2,1,0:T(8,128)S(1)} all-to-all(f32[16,40,128]{2,1,0:T(8,128)S(1)} %broadcast_in_dim.3), channel_id=1, replica_groups=mesh['z'=8,'xh'=2,'y'=4,'xl'=2,'c'=2] {'xh','y','xl'}, dimensions={0} | all-to-all | bytes 655360 | tf_op jit(solution)/shard_map/all_to_all | solution.py:283
  76.1 5.1 %collective-permute-start.8 = (f32[640,128]{1,0:T(8,128)S(1)}, f32[640,128]{1,0:T(8,128)S(1)}, u32[]{:S(2)}, u32[]{:S(2)}) collective-permute-start(f32[640,128]{1,0:T(8,128)S(1)} %bitcast.15), channel_id=1, source_target_pairs={{0,1},{1,0},{2,3},{3,2},{4,5},{5,4},{6,7},{7,6},{8,9},{9,8},{10,11... | collective-permute-start | bytes 983048 | tf_op jit(solution)/shard_map/ppermute | solution.py:285
  81.3 1.3 %collective-permute-done.8.other = f32[640,128]{1,0:T(8,128)S(1)} collective-permute-done((f32[640,128]{1,0:T(8,128)S(1)}, f32[640,128]{1,0:T(8,128)S(1)}, u32[]{:S(2)}, u32[]{:S(2)}) %collective-permute-start.8) | collective-permute-done | bytes 327712 | tf_op jit(solution)/shard_map/ppermute | solution.py:285
  82.5 14.1 %factor.1 = (f32[512,512]{1,0:T(8,128)}, f32[8,3,32,128]{3,2,1,0:T(8,128)S(1)}) custom-call(s32[1]{0:T(128)} %bitcast.core, f32[640,128]{1,0:T(8,128)S(1)} %bitcast.16, f32[640,128]{1,0:T(8,128)S(1)} %collective-permute-done.8.other, f32[512,384]{1,0:T(8,128)S(1)} %get-tuple-element.7.fields), custom_call_target="tpu_custom_call" | custom-call | tf_op jit(solution)/shard_map/factor/pallas_call | solution.py:286
  96.6 10.8 %all_to_all.23 = f32[8,3,32,128]{3,2,1,0:T(8,128)S(1)} all-to-all(f32[8,3,32,128]{3,2,1,0:T(8,128)S(1)} %get-tuple-element.8), channel_id=1, replica_groups=mesh['z'=8,'xh'=2,'y'=4,'xl'=2,'c'=2] {'y','xl'}, dimensions={0} | all-to-all | bytes 786432 | tf_op jit(solution)/shard_map/all_to_all | solution.py:298
  107.4 0.8 copy.8
  (5 shorter events, 0.1 us)
Async XLA Ops:
  0.6 1.1 copy-start.1
  1.7 19.3 %copy-start = (f32[256,256]{1,0:T(8,128)S(1)}, f32[256,256]{1,0:T(8,128)}, u32[]{:S(2)}) copy-start(f32[256,256]{1,0:T(8,128)} %constant.20.clone.mat) | copy-start | bytes 786436
  1.8 13.9 %collective-permute-start.2 = (f32[204,256]{1,0:T(8,128)S(1)}, f32[204,256]{1,0:T(8,128)S(1)}, u32[]{:S(2)}, u32[]{:S(2)}) collective-permute-start(f32[204,256]{1,0:T(8,128)S(1)} %get-tuple-element.12), channel_id=1, source_target_pairs={{0,240},{16,32},{32,16},{48,64},{64,48},{80,96},{96,80},{112,128},... | collective-permute-start | bytes 626696 | tf_op jit(solution)/shard_map/ppermute | solution.py:250
  10.7 10.3 %collective-permute-start = (f32[204,256]{1,0:T(8,128)S(1)}, f32[204,256]{1,0:T(8,128)S(1)}, u32[]{:S(2)}, u32[]{:S(2)}) collective-permute-start(f32[204,256]{1,0:T(8,128)S(1)} %get-tuple-element.12), channel_id=1, source_target_pairs={{0,16},{16,0},{32,48},{48,32},{64,80},{80,64},{96,112},{112,96},{1... | collective-permute-start | bytes 626696 | tf_op jit(solution)/shard_map/ppermute | solution.py:250
  10.7 10.3 %collective-permute-start.1 = (f32[204,256]{1,0:T(8,128)S(1)}, f32[204,256]{1,0:T(8,128)S(1)}, u32[]{:S(2)}, u32[]{:S(2)}) collective-permute-start(f32[204,256]{1,0:T(8,128)S(1)} %get-tuple-element.13.own), channel_id=1, source_target_pairs={{0,224},{16,48},{32,0},{48,80},{64,32},{80,112},{96,64},{112,144},... | collective-permute-start | bytes 626696 | tf_op jit(solution)/shard_map/ppermute | solution.py:250
  35.6 3.8 %collective-permute-start.3 = (f32[16,3,16,128]{3,2,1,0:T(8,128)S(1)}, f32[16,3,16,128]{3,2,1,0:T(8,128)S(1)}, u32[]{:S(2)}, u32[]{:S(2)}) collective-permute-start(f32[16,3,16,128]{3,2,1,0:T(8,128)S(1)} %all_to_all.20.own), channel_id=1, source_target_pairs={{0,1},{1,0},{2,3},{3,2},{4,5},{5,4},{6,7},{7,6},{8,9},{9,8},{10,11... | collective-permute-start | bytes 1179656 | tf_op jit(solution)/shard_map/ppermute | solution.py:264
  51.7 2.7 %collective-permute-start.4 = (f32[40,128]{1,0:T(8,128)S(1)}, f32[40,128]{1,0:T(8,128)S(1)}, u32[]{:S(2)}, u32[]{:S(2)}) collective-permute-start(f32[40,128]{1,0:T(8,128)S(1)} %reduce_sum.9), channel_id=1, source_target_pairs={{0,32},{32,0},{64,96},{96,64},{128,160},{160,128},{192,224},{224,1... | collective-permute-start | bytes 61448 | tf_op jit(solution)/shard_map/ppermute | solution.py:280
  54.4 6.2 %collective-permute-start.7 = (f32[40,128]{1,0:T(8,128)S(1)}, f32[40,128]{1,0:T(8,128)S(1)}, u32[]{:S(2)}, u32[]{:S(2)}) collective-permute-start(f32[40,128]{1,0:T(8,128)S(1)} %add.20), channel_id=1, source_target_pairs={{0,192},{32,224},{64,128},{96,160},{128,64},{160,96},{192,0},{224,... | collective-permute-start | bytes 61448 | tf_op jit(solution)/shard_map/ppermute | solution.py:281
  58.5 6.6 %collective-permute-start.6 = (f32[40,128]{1,0:T(8,128)S(1)}, f32[40,128]{1,0:T(8,128)S(1)}, u32[]{:S(2)}, u32[]{:S(2)}) collective-permute-start(f32[40,128]{1,0:T(8,128)S(1)} %add.20), channel_id=1, source_target_pairs={{0,128},{32,160},{64,192},{96,224},{128,0},{160,32},{192,64},{224,... | collective-permute-start | bytes 61448 | tf_op jit(solution)/shard_map/ppermute | solution.py:281
  60.4 4.7 %collective-permute-start.5 = (f32[40,128]{1,0:T(8,128)S(1)}, f32[40,128]{1,0:T(8,128)S(1)}, u32[]{:S(2)}, u32[]{:S(2)}) collective-permute-start(f32[40,128]{1,0:T(8,128)S(1)} %add.20), channel_id=1, source_target_pairs={{0,64},{32,96},{64,0},{96,32},{128,192},{160,224},{192,128},{224,1... | collective-permute-start | bytes 61448 | tf_op jit(solution)/shard_map/ppermute | solution.py:281
  76.1 6.4 %collective-permute-start.8 = (f32[640,128]{1,0:T(8,128)S(1)}, f32[640,128]{1,0:T(8,128)S(1)}, u32[]{:S(2)}, u32[]{:S(2)}) collective-permute-start(f32[640,128]{1,0:T(8,128)S(1)} %bitcast.15), channel_id=1, source_target_pairs={{0,1},{1,0},{2,3},{3,2},{4,5},{5,4},{6,7},{7,6},{8,9},{9,8},{10,11... | collective-permute-start | bytes 983048 | tf_op jit(solution)/shard_map/ppermute | solution.py:285

commit v5 on v4

--- a/solution.py
+++ b/solution.py
@@ -184,7 +184,7 @@
             )
 
 
-def factor_kernel(core, own, other, fields, corr, out, work):
+def factor_kernel(core, own, other, fields, corr_hbm, out, work, corr, sem):
     first = core[0] == 0
     for k in range(5):
         rows = slice(k * TILE, (k + 1) * TILE)
@@ -194,6 +194,8 @@
             corr[i * TILE : (i + 1) * TILE, j * TILE : (j + 1) * TILE] = block
             if i != j:
                 corr[j * TILE : (j + 1) * TILE, i * TILE : (i + 1) * TILE] = block.T
+    copy = pltpu.make_async_copy(corr, corr_hbm, sem)
+    copy.start()
     work[...] = corr[...]
     count = work.shape[0]
     size = out.shape[2]
@@ -220,6 +222,7 @@
                 if side.start < side.stop:
                     work[rows, side] = work[rows, side] - dot32(lower, work[own_rows, side], ((1,), (0,)))
             work[rows, own_rows] = -dot32(lower, inverse, ((1,), (0,)))
+    copy.wait()
 
 
 VMEM = pl.BlockSpec(memory_space=pltpu.VMEM)
@@ -277,9 +280,8 @@
     )(core, mine, theirs)
 
     piece = lax.all_to_all(part.reshape(layer, 5 * TILE // layer, TILE), LAYER, 0, 0).sum(0)
-    piece = piece + lax.ppermute(piece, "z", flip("z", 1))
-    got = [lax.ppermute(piece, "z", flip("z", b)) for b in (2, 4, 6)]
-    piece = (piece + got[0]) + (got[1] + got[2])
+    depth = lax.axis_size("z")
+    piece = lax.all_to_all(jnp.broadcast_to(piece, (depth,) + piece.shape), "z", 0, 0).sum(0)
     spread = lax.all_to_all(jnp.broadcast_to(piece, (layer,) + piece.shape), LAYER, 0, 0)
     mine_g = spread.reshape(5 * TILE, TILE)
     theirs_g = lax.ppermute(mine_g, ("c",), flip("c", 1))
@@ -290,8 +292,12 @@
             jax.ShapeDtypeStruct((team, mine.shape[1], rows, TILE), jnp.float32),
         ),
         in_specs=[SMEM, VMEM, VMEM, VMEM],
-        out_specs=(VMEM, VMEM),
-        scratch_shapes=[pltpu.VMEM((count, count), jnp.float32)],
+        out_specs=(pl.BlockSpec(memory_space=pl.ANY), VMEM),
+        scratch_shapes=[
+            pltpu.VMEM((count, count), jnp.float32),
+            pltpu.VMEM((count, count), jnp.float32),
+            pltpu.SemaphoreType.DMA,
+        ],
         compiler_params=PARAMS,
         name="factor",
     )(core, mine_g, theirs_g, fields)

time: 108 us -> 108 us (level)
  blocking collectives: 45.8 us -> 60 us
  starting transfers between devices: 23.6 us -> 16.2 us
  waiting for transfers between devices: 19.2 us -> 12.2 us
    all_to_all x0 -> x1, blocking collectives: none -> 14.3 us  [per_device(): lax.all_to_all(jnp.broadcast_to(piece, (depth,) + piece.shape), 'z', 0, 0)]
    ppermute x4 -> x0, waiting for transfers between devices: 7.02 us -> none  [the longest x3 4.4 us: per_device(): got = [lax.ppermute(piece, 'z', flip('z', b)) for b in (2, 4, 6)]]
    ppermute x4 -> x0, starting transfers between devices: 6.29 us -> none  [the longest x3 6.2 us: per_device(): got = [lax.ppermute(piece, 'z', flip('z', b)) for b in (2, 4, 6)]]
    ppermute x1, starting transfers between devices: 5.15 us -> 4.04 us  [per_device(): theirs_g = lax.ppermute(mine_g, ('c',), flip('c', 1))]
  transfers between devices with their start and end apart: 9 -> 5, of which waited for: 6 -> 4; matrix products, arithmetic and copies ran while one was open for 0% -> 0% of each run, Pallas kernels for 0% -> 0%
where the time goes in v5:
time: 108 us
  blocking collectives  60 us (56%)
  Pallas kernels  17 us (16%)
  starting transfers between devices  16.2 us (15%)
  waiting for transfers between devices  12.2 us (11%)
  local copies, waits for them, and re-layouts  1.88 us (2%)
    all_to_all x1, blocking collectives, per_device(): lax.all_to_all(jnp.broadcast_to(piece, (depth,) + piece.shape), 'z', 0, 0)  14.3 us
    pallas_call x1, Pallas kernels, per_device(): pl.pallas_call(factor_kernel, out_shape=(jax.ShapeDtypeStruct((count, cou...  14.1 us
    all_to_all x1, blocking collectives, per_device(): lax.all_to_all(second.reshape(layer, 4 * planes // layer, half, TILE), LA...  12.7 us
    all_to_all x1, blocking collectives, per_device(): lax.all_to_all(part.reshape(layer, 5 * TILE // layer, TILE), LAYER, 0, 0)  11.2 us
    all_to_all x1, blocking collectives, per_device(): lax.all_to_all(jnp.broadcast_to(piece, (layer,) + piece.shape), LAYER, 0, 0)  11 us
    all_to_all x1, blocking collectives, per_device(): back = lax.all_to_all(turned, TEAM, 0, 0).reshape(planes, 2, rows, TILE)  10.8 us
    ppermute x3, starting transfers between devices, per_device(): lax.ppermute(x, SPACE, pairs)  9.68 us
    ppermute x3, waiting for transfers between devices, per_device(): lax.ppermute(x, SPACE, pairs)  9.55 us
  transfers between devices with their start and end apart: 5, of which 4 were waited for; matrix products, arithmetic and copies ran while one was open for 0% of the time, Pallas kernels for 0%

profile of v5, /device:TPU:1, one launch (start us, length us, event | category | flops | bytes accessed | tf_op | source)
XLA Modules:
  0.0 108.1 jit_solution(8967163041294934519)
XLA Ops:
  0.6 0.0 copy-start.1
  0.6 1.1 constant_dynamic-slice_fusion
  1.7 0.0 copy-done.1
  1.7 0.0 copy-start
  1.8 9.0 %collective-permute-start.2 = (f32[204,256]{1,0:T(8,128)S(1)}, f32[204,256]{1,0:T(8,128)S(1)}, u32[]{:S(2)}, u32[]{:S(2)}) collective-permute-start(f32[204,256]{1,0:T(8,128)S(1)} %get-tuple-element.12), channel_id=1, source_target_pairs={{0,240},{16,32},{32,16},{48,64},{64,48},{80,96},{96,80},{112,128},... | collective-permute-start | bytes 626696 | tf_op jit(solution)/shard_map/ppermute | solution.py:253
  10.7 0.0 collective-permute-start
  10.7 0.7 collective-permute-start.1
  11.5 4.2 %collective-permute-done.2.cross = f32[204,256]{1,0:T(8,128)S(1)} collective-permute-done((f32[204,256]{1,0:T(8,128)S(1)}, f32[204,256]{1,0:T(8,128)S(1)}, u32[]{:S(2)}, u32[]{:S(2)}) %collective-permute-start.2) | collective-permute-done | bytes 208928 | tf_op jit(solution)/shard_map/ppermute | solution.py:253
  15.7 5.3 %collective-permute-done.swap = f32[204,256]{1,0:T(8,128)S(1)} collective-permute-done((f32[204,256]{1,0:T(8,128)S(1)}, f32[204,256]{1,0:T(8,128)S(1)}, u32[]{:S(2)}, u32[]{:S(2)}) %collective-permute-start) | collective-permute-done | bytes 208928 | tf_op jit(solution)/shard_map/ppermute | solution.py:253
  21.0 0.0 collective-permute-done.1.near
  21.0 0.0 copy-done
  21.0 1.8 %filter.1 = f32[48,16,128]{2,1,0:T(8,128)S(1)} custom-call(s32[1]{0:T(128)} %bitcast.1.side, f32[204,256]{1,0:T(8,128)S(1)} %get-tuple-element.13.own, f32[204,256]{1,0:T(8,128)S(1)} %collective-permute-done.swap, f32[204,256]{1,0:T(8,128)S(1)} %collective-permute-done.1.near, f32[204,256]{1,0:T(8,128)S(1)} %collective-permute-done.2.cross, ...), custom_call_target="tpu_custom_call" | custom-call | tf_op jit(solution)/shard_map/filter/pallas_call | solution.py:255
  22.8 12.7 %all_to_all.25.own = f32[16,3,16,128]{3,2,1,0:T(8,128)S(1)} all-to-all(f32[16,3,16,128]{3,2,1,0:T(8,128)S(1)} %bitcast.14), channel_id=1, replica_groups=mesh['z'=8,'xh'=2,'y'=4,'xl'=2,'c'=2] {'xh','y','xl'}, dimensions={0} | all-to-all | bytes 786432 | tf_op jit(solution)/shard_map/all_to_all | solution.py:266
  35.6 2.5 %collective-permute-start.3 = (f32[16,3,16,128]{3,2,1,0:T(8,128)S(1)}, f32[16,3,16,128]{3,2,1,0:T(8,128)S(1)}, u32[]{:S(2)}, u32[]{:S(2)}) collective-permute-start(f32[16,3,16,128]{3,2,1,0:T(8,128)S(1)} %all_to_all.25.own), channel_id=1, source_target_pairs={{0,1},{1,0},{2,3},{3,2},{4,5},{5,4},{6,7},{7,6},{8,9},{9,8},{10,11... | collective-permute-start | bytes 1179656 | tf_op jit(solution)/shard_map/ppermute | solution.py:267
  38.0 1.3 %collective-permute-done.3.other = f32[16,3,16,128]{3,2,1,0:T(8,128)S(1)} collective-permute-done((f32[16,3,16,128]{3,2,1,0:T(8,128)S(1)}, f32[16,3,16,128]{3,2,1,0:T(8,128)S(1)}, u32[]{:S(2)}, u32[]{:S(2)}) %collective-permute-start.3) | collective-permute-done | bytes 393248 | tf_op jit(solution)/shard_map/ppermute | solution.py:267
  39.4 1.1 %gram.1 = (f32[640,128]{1,0:T(8,128)S(1)}, f32[512,384]{1,0:T(8,128)S(1)}) custom-call(s32[1]{0:T(128)} %bitcast.core, f32[16,3,16,128]{3,2,1,0:T(8,128)S(1)} %all_to_all.25.own, f32[16,3,16,128]{3,2,1,0:T(8,128)S(1)} %collective-permute-done.3.other), custom_call_target="tpu_custom_call" | custom-call | tf_op jit(solution)/shard_map/gram/pallas_call | solution.py:270
  40.5 11.2 %all_to_all.26 = f32[16,40,128]{2,1,0:T(8,128)S(1)} all-to-all(f32[16,40,128]{2,1,0:T(8,128)S(1)} %bitcast.17), channel_id=1, replica_groups=mesh['z'=8,'xh'=2,'y'=4,'xl'=2,'c'=2] {'xh','y','xl'}, dimensions={0} | all-to-all | bytes 655360 | tf_op jit(solution)/shard_map/all_to_all | solution.py:282
  51.7 14.3 %all_to_all.27 = f32[8,40,128]{2,1,0:T(8,128)S(1)} all-to-all(f32[8,40,128]{2,1,0:T(8,128)S(1)} %broadcast_in_dim.6), channel_id=1, replica_groups=mesh['z'=8,'xh'=2,'y'=4,'xl'=2,'c'=2] {'z'}, dimensions={0} | all-to-all | bytes 327680 | tf_op jit(solution)/shard_map/all_to_all | solution.py:284
  66.1 11.0 %all_to_all.28 = f32[16,40,128]{2,1,0:T(8,128)S(1)} all-to-all(f32[16,40,128]{2,1,0:T(8,128)S(1)} %broadcast_in_dim.7), channel_id=1, replica_groups=mesh['z'=8,'xh'=2,'y'=4,'xl'=2,'c'=2] {'xh','y','xl'}, dimensions={0} | all-to-all | bytes 655360 | tf_op jit(solution)/shard_map/all_to_all | solution.py:285
  77.1 4.0 %collective-permute-start.4 = (f32[640,128]{1,0:T(8,128)S(1)}, f32[640,128]{1,0:T(8,128)S(1)}, u32[]{:S(2)}, u32[]{:S(2)}) collective-permute-start(f32[640,128]{1,0:T(8,128)S(1)} %bitcast.15), channel_id=1, source_target_pairs={{0,1},{1,0},{2,3},{3,2},{4,5},{5,4},{6,7},{7,6},{8,9},{9,8},{10,11... | collective-permute-start | bytes 983048 | tf_op jit(solution)/shard_map/ppermute | solution.py:287
  81.1 1.3 %collective-permute-done.4.other = f32[640,128]{1,0:T(8,128)S(1)} collective-permute-done((f32[640,128]{1,0:T(8,128)S(1)}, f32[640,128]{1,0:T(8,128)S(1)}, u32[]{:S(2)}, u32[]{:S(2)}) %collective-permute-start.4) | collective-permute-done | bytes 327712 | tf_op jit(solution)/shard_map/ppermute | solution.py:287
  82.4 14.1 %factor.1 = (f32[512,512]{1,0:T(8,128)}, f32[8,3,32,128]{3,2,1,0:T(8,128)S(1)}) custom-call(s32[1]{0:T(128)} %bitcast.core, f32[640,128]{1,0:T(8,128)S(1)} %bitcast.16, f32[640,128]{1,0:T(8,128)S(1)} %collective-permute-done.4.other, f32[512,384]{1,0:T(8,128)S(1)} %get-tuple-element.7.fields), custom_call_target="tpu_custom_call" | custom-call | tf_op jit(solution)/shard_map/factor/pallas_call | solution.py:288
  96.5 10.8 %all_to_all.29 = f32[8,3,32,128]{3,2,1,0:T(8,128)S(1)} all-to-all(f32[8,3,32,128]{3,2,1,0:T(8,128)S(1)} %get-tuple-element.8), channel_id=1, replica_groups=mesh['z'=8,'xh'=2,'y'=4,'xl'=2,'c'=2] {'y','xl'}, dimensions={0} | all-to-all | bytes 786432 | tf_op jit(solution)/shard_map/all_to_all | solution.py:304
  107.3 0.8 copy.9
  (5 shorter events, 0.1 us)
Async XLA Ops:
  0.6 1.1 copy-start.1
  1.7 19.3 %copy-start = (f32[256,256]{1,0:T(8,128)S(1)}, f32[256,256]{1,0:T(8,128)}, u32[]{:S(2)}) copy-start(f32[256,256]{1,0:T(8,128)} %constant.20.clone.mat) | copy-start | bytes 786436
  1.8 13.9 %collective-permute-start.2 = (f32[204,256]{1,0:T(8,128)S(1)}, f32[204,256]{1,0:T(8,128)S(1)}, u32[]{:S(2)}, u32[]{:S(2)}) collective-permute-start(f32[204,256]{1,0:T(8,128)S(1)} %get-tuple-element.12), channel_id=1, source_target_pairs={{0,240},{16,32},{32,16},{48,64},{64,48},{80,96},{96,80},{112,128},... | collective-permute-start | bytes 626696 | tf_op jit(solution)/shard_map/ppermute | solution.py:253
  10.7 10.3 %collective-permute-start = (f32[204,256]{1,0:T(8,128)S(1)}, f32[204,256]{1,0:T(8,128)S(1)}, u32[]{:S(2)}, u32[]{:S(2)}) collective-permute-start(f32[204,256]{1,0:T(8,128)S(1)} %get-tuple-element.12), channel_id=1, source_target_pairs={{0,16},{16,0},{32,48},{48,32},{64,80},{80,64},{96,112},{112,96},{1... | collective-permute-start | bytes 626696 | tf_op jit(solution)/shard_map/ppermute | solution.py:253
  10.7 10.3 %collective-permute-start.1 = (f32[204,256]{1,0:T(8,128)S(1)}, f32[204,256]{1,0:T(8,128)S(1)}, u32[]{:S(2)}, u32[]{:S(2)}) collective-permute-start(f32[204,256]{1,0:T(8,128)S(1)} %get-tuple-element.13.own), channel_id=1, source_target_pairs={{0,224},{16,48},{32,0},{48,80},{64,32},{80,112},{96,64},{112,144},... | collective-permute-start | bytes 626696 | tf_op jit(solution)/shard_map/ppermute | solution.py:253
  35.6 3.8 %collective-permute-start.3 = (f32[16,3,16,128]{3,2,1,0:T(8,128)S(1)}, f32[16,3,16,128]{3,2,1,0:T(8,128)S(1)}, u32[]{:S(2)}, u32[]{:S(2)}) collective-permute-start(f32[16,3,16,128]{3,2,1,0:T(8,128)S(1)} %all_to_all.25.own), channel_id=1, source_target_pairs={{0,1},{1,0},{2,3},{3,2},{4,5},{5,4},{6,7},{7,6},{8,9},{9,8},{10,11... | collective-permute-start | bytes 1179656 | tf_op jit(solution)/shard_map/ppermute | solution.py:267
  77.1 5.3 %collective-permute-start.4 = (f32[640,128]{1,0:T(8,128)S(1)}, f32[640,128]{1,0:T(8,128)S(1)}, u32[]{:S(2)}, u32[]{:S(2)}) collective-permute-start(f32[640,128]{1,0:T(8,128)S(1)} %bitcast.15), channel_id=1, source_target_pairs={{0,1},{1,0},{2,3},{3,2},{4,5},{5,4},{6,7},{7,6},{8,9},{9,8},{10,11... | collective-permute-start | bytes 983048 | tf_op jit(solution)/shard_map/ppermute | solution.py:287

commit v6 on v5

--- a/solution.py
+++ b/solution.py
@@ -200,28 +200,51 @@
     count = work.shape[0]
     size = out.shape[2]
     pairs = TILE // (2 * size)
-    for k in range(0, count, TILE):
-        own_rows = slice(k, k + TILE)
-        factor_tile(work, k)
-        inverse = work[own_rows, own_rows]
-        for side in (slice(0, k), slice(k + TILE, count)):
-            if side.start < side.stop:
-                work[own_rows, side] = dot32(inverse, work[own_rows, side], ((1,), (0,)))
-        mine = [
-            work[pl.ds(pl.multiple_of(k + 2 * i * size + core[0] * size, size), size), 0 : k + TILE]
-            for i in range(pairs)
-        ]
-        turned = dot32(jnp.concatenate(mine, axis=0), fields[0 : k + TILE, :], ((1,), (0,)))
+
+    def own_part(k, columns):
+        picked = []
+        for at in range(k, k + TILE, 2 * size):
+            picked.append(
+                jnp.where(first, work[at : at + size, columns], work[at + size : at + 2 * size, columns])
+            )
+        return jnp.concatenate(picked, axis=0)
+
+    def put(k, turned):
         for i in range(pairs):
             for t in range(out.shape[1]):
                 out[k // TILE * pairs + i, t] = turned[i * size : (i + 1) * size, t * TILE : (t + 1) * TILE]
+
+    def next_tile(k):
+        here, after = slice(k, k + TILE), slice(k + TILE, k + 2 * TILE)
+        upper = dot32(work[here, here], work[here, after], ((1,), (0,)))
+        work[here, after] = upper
+        work[after, after] = work[after, after] - dot32(upper.T, upper, ((1,), (0,)))
+
+    def other_tiles(k):
+        here = slice(k, k + TILE)
+        inverse = work[here, here]
+        for side in (slice(k + 2 * TILE, count), slice(0, k)):
+            if side.start < side.stop:
+                work[here, side] = dot32(inverse, work[here, side], ((1,), (0,)))
         for r in range(k + TILE, count, TILE):
             rows = slice(r, r + TILE)
-            lower = work[own_rows, rows].T
-            for side in (slice(r, count), slice(0, k)):
+            lower = work[here, rows].T
+            for side in (slice(r + TILE if r == k + TILE else r, count), slice(0, k)):
                 if side.start < side.stop:
-                    work[rows, side] = work[rows, side] - dot32(lower, work[own_rows, side], ((1,), (0,)))
-            work[rows, own_rows] = -dot32(lower, inverse, ((1,), (0,)))
+                    work[rows, side] = work[rows, side] - dot32(lower, work[here, side], ((1,), (0,)))
+            work[rows, here] = -dot32(lower, inverse, ((1,), (0,)))
+        done = slice(0, k + TILE)
+        put(k, dot32(own_part(k, done), fields[done, :], ((1,), (0,))))
+
+    for k in range(0, count, TILE):
+        factor_tile(work, k)
+        if k:
+            other_tiles(k - TILE)
+        if k + TILE < count:
+            next_tile(k)
+    last = slice(k, count)
+    summed = dot32(work[last, 0:k], fields[0:k, :], ((1,), (0,))) + fields[last, :]
+    put(k, dot32(own_part(k, last), summed, ((1,), (0,))))
     copy.wait()
 
 

time: 108 us -> 108 us (level)
  no operation moved by 1% of the time
where the time goes in v6:
time: 108 us
  blocking collectives  60.1 us (56%)
  Pallas kernels  16.6 us (15%)
  starting transfers between devices  16.2 us (15%)
  waiting for transfers between devices  12.2 us (11%)
  local copies, waits for them, and re-layouts  1.88 us (2%)
    all_to_all x1, blocking collectives, per_device(): lax.all_to_all(jnp.broadcast_to(piece, (depth,) + piece.shape), 'z', 0, 0)  14.3 us
    pallas_call x1, Pallas kernels, per_device(): pl.pallas_call(factor_kernel, out_shape=(jax.ShapeDtypeStruct((count, cou...  13.6 us
    all_to_all x1, blocking collectives, per_device(): lax.all_to_all(second.reshape(layer, 4 * planes // layer, half, TILE), LA...  12.7 us
    all_to_all x1, blocking collectives, per_device(): lax.all_to_all(part.reshape(layer, 5 * TILE // layer, TILE), LAYER, 0, 0)  11.2 us
    all_to_all x1, blocking collectives, per_device(): lax.all_to_all(jnp.broadcast_to(piece, (layer,) + piece.shape), LAYER, 0, 0)  11 us
    all_to_all x1, blocking collectives, per_device(): back = lax.all_to_all(turned, TEAM, 0, 0).reshape(planes, 2, rows, TILE)  10.8 us
    ppermute x3, starting transfers between devices, per_device(): lax.ppermute(x, SPACE, pairs)  9.68 us
    ppermute x3, waiting for transfers between devices, per_device(): lax.ppermute(x, SPACE, pairs)  9.55 us
  transfers between devices with their start and end apart: 5, of which 4 were waited for; matrix products, arithmetic and copies ran while one was open for 0% of the time, Pallas kernels for 0%

profile of v6, /device:TPU:1, one launch (start us, length us, event | category | flops | bytes accessed | tf_op | source)
XLA Modules:
  0.0 107.6 jit_solution(14379277010553073157)
XLA Ops:
  0.6 0.0 copy-start.1
  0.6 1.1 constant_dynamic-slice_fusion
  1.7 0.0 copy-done.1
  1.7 0.0 copy-start
  1.8 9.0 %collective-permute-start.2 = (f32[204,256]{1,0:T(8,128)S(1)}, f32[204,256]{1,0:T(8,128)S(1)}, u32[]{:S(2)}, u32[]{:S(2)}) collective-permute-start(f32[204,256]{1,0:T(8,128)S(1)} %get-tuple-element.12), channel_id=1, source_target_pairs={{0,240},{16,32},{32,16},{48,64},{64,48},{80,96},{96,80},{112,128},... | collective-permute-start | bytes 626696 | tf_op jit(solution)/shard_map/ppermute | solution.py:276
  10.7 0.0 collective-permute-start
  10.7 0.7 collective-permute-start.1
  11.5 4.2 %collective-permute-done.2.cross = f32[204,256]{1,0:T(8,128)S(1)} collective-permute-done((f32[204,256]{1,0:T(8,128)S(1)}, f32[204,256]{1,0:T(8,128)S(1)}, u32[]{:S(2)}, u32[]{:S(2)}) %collective-permute-start.2) | collective-permute-done | bytes 208928 | tf_op jit(solution)/shard_map/ppermute | solution.py:276
  15.7 5.3 %collective-permute-done.swap = f32[204,256]{1,0:T(8,128)S(1)} collective-permute-done((f32[204,256]{1,0:T(8,128)S(1)}, f32[204,256]{1,0:T(8,128)S(1)}, u32[]{:S(2)}, u32[]{:S(2)}) %collective-permute-start) | collective-permute-done | bytes 208928 | tf_op jit(solution)/shard_map/ppermute | solution.py:276
  21.0 0.0 collective-permute-done.1.near
  21.0 0.0 copy-done
  21.0 1.8 %filter.1 = f32[48,16,128]{2,1,0:T(8,128)S(1)} custom-call(s32[1]{0:T(128)} %bitcast.1.side, f32[204,256]{1,0:T(8,128)S(1)} %get-tuple-element.13.own, f32[204,256]{1,0:T(8,128)S(1)} %collective-permute-done.swap, f32[204,256]{1,0:T(8,128)S(1)} %collective-permute-done.1.near, f32[204,256]{1,0:T(8,128)S(1)} %collective-permute-done.2.cross, ...), custom_call_target="tpu_custom_call" | custom-call | tf_op jit(solution)/shard_map/filter/pallas_call | solution.py:278
  22.8 12.7 %all_to_all.25.own = f32[16,3,16,128]{3,2,1,0:T(8,128)S(1)} all-to-all(f32[16,3,16,128]{3,2,1,0:T(8,128)S(1)} %bitcast.14), channel_id=1, replica_groups=mesh['z'=8,'xh'=2,'y'=4,'xl'=2,'c'=2] {'xh','y','xl'}, dimensions={0} | all-to-all | bytes 786432 | tf_op jit(solution)/shard_map/all_to_all | solution.py:289
  35.6 2.5 %collective-permute-start.3 = (f32[16,3,16,128]{3,2,1,0:T(8,128)S(1)}, f32[16,3,16,128]{3,2,1,0:T(8,128)S(1)}, u32[]{:S(2)}, u32[]{:S(2)}) collective-permute-start(f32[16,3,16,128]{3,2,1,0:T(8,128)S(1)} %all_to_all.25.own), channel_id=1, source_target_pairs={{0,1},{1,0},{2,3},{3,2},{4,5},{5,4},{6,7},{7,6},{8,9},{9,8},{10,11... | collective-permute-start | bytes 1179656 | tf_op jit(solution)/shard_map/ppermute | solution.py:290
  38.0 1.3 %collective-permute-done.3.other = f32[16,3,16,128]{3,2,1,0:T(8,128)S(1)} collective-permute-done((f32[16,3,16,128]{3,2,1,0:T(8,128)S(1)}, f32[16,3,16,128]{3,2,1,0:T(8,128)S(1)}, u32[]{:S(2)}, u32[]{:S(2)}) %collective-permute-start.3) | collective-permute-done | bytes 393248 | tf_op jit(solution)/shard_map/ppermute | solution.py:290
  39.4 1.1 %gram.1 = (f32[640,128]{1,0:T(8,128)S(1)}, f32[512,384]{1,0:T(8,128)S(1)}) custom-call(s32[1]{0:T(128)} %bitcast.core, f32[16,3,16,128]{3,2,1,0:T(8,128)S(1)} %all_to_all.25.own, f32[16,3,16,128]{3,2,1,0:T(8,128)S(1)} %collective-permute-done.3.other), custom_call_target="tpu_custom_call" | custom-call | tf_op jit(solution)/shard_map/gram/pallas_call | solution.py:293
  40.5 11.2 %all_to_all.26 = f32[16,40,128]{2,1,0:T(8,128)S(1)} all-to-all(f32[16,40,128]{2,1,0:T(8,128)S(1)} %bitcast.17), channel_id=1, replica_groups=mesh['z'=8,'xh'=2,'y'=4,'xl'=2,'c'=2] {'xh','y','xl'}, dimensions={0} | all-to-all | bytes 655360 | tf_op jit(solution)/shard_map/all_to_all | solution.py:305
  51.7 14.3 %all_to_all.27 = f32[8,40,128]{2,1,0:T(8,128)S(1)} all-to-all(f32[8,40,128]{2,1,0:T(8,128)S(1)} %broadcast_in_dim.6), channel_id=1, replica_groups=mesh['z'=8,'xh'=2,'y'=4,'xl'=2,'c'=2] {'z'}, dimensions={0} | all-to-all | bytes 327680 | tf_op jit(solution)/shard_map/all_to_all | solution.py:307
  66.1 11.0 %all_to_all.28 = f32[16,40,128]{2,1,0:T(8,128)S(1)} all-to-all(f32[16,40,128]{2,1,0:T(8,128)S(1)} %broadcast_in_dim.7), channel_id=1, replica_groups=mesh['z'=8,'xh'=2,'y'=4,'xl'=2,'c'=2] {'xh','y','xl'}, dimensions={0} | all-to-all | bytes 655360 | tf_op jit(solution)/shard_map/all_to_all | solution.py:308
  77.1 4.0 %collective-permute-start.4 = (f32[640,128]{1,0:T(8,128)S(1)}, f32[640,128]{1,0:T(8,128)S(1)}, u32[]{:S(2)}, u32[]{:S(2)}) collective-permute-start(f32[640,128]{1,0:T(8,128)S(1)} %bitcast.15), channel_id=1, source_target_pairs={{0,1},{1,0},{2,3},{3,2},{4,5},{5,4},{6,7},{7,6},{8,9},{9,8},{10,11... | collective-permute-start | bytes 983048 | tf_op jit(solution)/shard_map/ppermute | solution.py:310
  81.1 1.3 %collective-permute-done.4.other = f32[640,128]{1,0:T(8,128)S(1)} collective-permute-done((f32[640,128]{1,0:T(8,128)S(1)}, f32[640,128]{1,0:T(8,128)S(1)}, u32[]{:S(2)}, u32[]{:S(2)}) %collective-permute-start.4) | collective-permute-done | bytes 327712 | tf_op jit(solution)/shard_map/ppermute | solution.py:310
  82.4 13.6 %factor.1 = (f32[512,512]{1,0:T(8,128)}, f32[8,3,32,128]{3,2,1,0:T(8,128)S(1)}) custom-call(s32[1]{0:T(128)} %bitcast.core, f32[640,128]{1,0:T(8,128)S(1)} %bitcast.16, f32[640,128]{1,0:T(8,128)S(1)} %collective-permute-done.4.other, f32[512,384]{1,0:T(8,128)S(1)} %get-tuple-element.7.fields), custom_call_target="tpu_custom_call" | custom-call | tf_op jit(solution)/shard_map/factor/pallas_call | solution.py:311
  96.0 10.8 %all_to_all.29 = f32[8,3,32,128]{3,2,1,0:T(8,128)S(1)} all-to-all(f32[8,3,32,128]{3,2,1,0:T(8,128)S(1)} %get-tuple-element.8), channel_id=1, replica_groups=mesh['z'=8,'xh'=2,'y'=4,'xl'=2,'c'=2] {'y','xl'}, dimensions={0} | all-to-all | bytes 786432 | tf_op jit(solution)/shard_map/all_to_all | solution.py:327
  106.8 0.8 copy.9
  (5 shorter events, 0.1 us)
Async XLA Ops:
  0.6 1.1 copy-start.1
  1.7 19.3 %copy-start = (f32[256,256]{1,0:T(8,128)S(1)}, f32[256,256]{1,0:T(8,128)}, u32[]{:S(2)}) copy-start(f32[256,256]{1,0:T(8,128)} %constant.20.clone.mat) | copy-start | bytes 786436
  1.8 13.9 %collective-permute-start.2 = (f32[204,256]{1,0:T(8,128)S(1)}, f32[204,256]{1,0:T(8,128)S(1)}, u32[]{:S(2)}, u32[]{:S(2)}) collective-permute-start(f32[204,256]{1,0:T(8,128)S(1)} %get-tuple-element.12), channel_id=1, source_target_pairs={{0,240},{16,32},{32,16},{48,64},{64,48},{80,96},{96,80},{112,128},... | collective-permute-start | bytes 626696 | tf_op jit(solution)/shard_map/ppermute | solution.py:276
  10.7 10.3 %collective-permute-start = (f32[204,256]{1,0:T(8,128)S(1)}, f32[204,256]{1,0:T(8,128)S(1)}, u32[]{:S(2)}, u32[]{:S(2)}) collective-permute-start(f32[204,256]{1,0:T(8,128)S(1)} %get-tuple-element.12), channel_id=1, source_target_pairs={{0,16},{16,0},{32,48},{48,32},{64,80},{80,64},{96,112},{112,96},{1... | collective-permute-start | bytes 626696 | tf_op jit(solution)/shard_map/ppermute | solution.py:276
  10.7 10.3 %collective-permute-start.1 = (f32[204,256]{1,0:T(8,128)S(1)}, f32[204,256]{1,0:T(8,128)S(1)}, u32[]{:S(2)}, u32[]{:S(2)}) collective-permute-start(f32[204,256]{1,0:T(8,128)S(1)} %get-tuple-element.13.own), channel_id=1, source_target_pairs={{0,224},{16,48},{32,0},{48,80},{64,32},{80,112},{96,64},{112,144},... | collective-permute-start | bytes 626696 | tf_op jit(solution)/shard_map/ppermute | solution.py:276
  35.6 3.8 %collective-permute-start.3 = (f32[16,3,16,128]{3,2,1,0:T(8,128)S(1)}, f32[16,3,16,128]{3,2,1,0:T(8,128)S(1)}, u32[]{:S(2)}, u32[]{:S(2)}) collective-permute-start(f32[16,3,16,128]{3,2,1,0:T(8,128)S(1)} %all_to_all.25.own), channel_id=1, source_target_pairs={{0,1},{1,0},{2,3},{3,2},{4,5},{5,4},{6,7},{7,6},{8,9},{9,8},{10,11... | collective-permute-start | bytes 1179656 | tf_op jit(solution)/shard_map/ppermute | solution.py:290
  77.1 5.3 %collective-permute-start.4 = (f32[640,128]{1,0:T(8,128)S(1)}, f32[640,128]{1,0:T(8,128)S(1)}, u32[]{:S(2)}, u32[]{:S(2)}) collective-permute-start(f32[640,128]{1,0:T(8,128)S(1)} %bitcast.15), channel_id=1, source_target_pairs={{0,1},{1,0},{2,3},{3,2},{4,5},{5,4},{6,7},{7,6},{8,9},{9,8},{10,11... | collective-permute-start | bytes 983048 | tf_op jit(solution)/shard_map/ppermute | solution.py:310

commit v7 on v6

--- a/solution.py
+++ b/solution.py
@@ -186,17 +186,7 @@
 
 def factor_kernel(core, own, other, fields, corr_hbm, out, work, corr, sem):
     first = core[0] == 0
-    for k in range(5):
-        rows = slice(k * TILE, (k + 1) * TILE)
-        a, b = own[rows, :], other[rows, :]
-        for blocks, block in ((BLOCKS[0], jnp.where(first, a, b)), (BLOCKS[1], jnp.where(first, b, a))):
-            i, j = blocks[k]
-            corr[i * TILE : (i + 1) * TILE, j * TILE : (j + 1) * TILE] = block
-            if i != j:
-                corr[j * TILE : (j + 1) * TILE, i * TILE : (i + 1) * TILE] = block.T
-    copy = pltpu.make_async_copy(corr, corr_hbm, sem)
-    copy.start()
-    work[...] = corr[...]
+
     count = work.shape[0]
     size = out.shape[2]
     pairs = TILE // (2 * size)
@@ -213,6 +203,23 @@
         for i in range(pairs):
             for t in range(out.shape[1]):
                 out[k // TILE * pairs + i, t] = turned[i * size : (i + 1) * size, t * TILE : (t + 1) * TILE]
+
+    def join():
+        for k in range(5):
+            rows = slice(k * TILE, (k + 1) * TILE)
+            a, b = own[rows, :], other[rows, :]
+            for blocks, block in (
+                (BLOCKS[0], jnp.where(first, a, b)),
+                (BLOCKS[1], jnp.where(first, b, a)),
+            ):
+                i, j = (slice(t * TILE, (t + 1) * TILE) for t in blocks[k])
+                corr[i, j] = block
+                if i != j:
+                    turned = block.T
+                    corr[j, i] = turned
+                    work[j, i] = turned
+                if j.start or i.start:
+                    work[i, j] = block
 
     def next_tile(k):
         here, after = slice(k, k + TILE), slice(k + TILE, k + 2 * TILE)
@@ -236,10 +243,15 @@
         done = slice(0, k + TILE)
         put(k, dot32(own_part(k, done), fields[done, :], ((1,), (0,))))
 
+    work[0:TILE, 0:TILE] = jnp.where(first, own[0:TILE, :], other[0:TILE, :])
     for k in range(0, count, TILE):
         factor_tile(work, k)
         if k:
             other_tiles(k - TILE)
+        else:
+            join()
+            copy = pltpu.make_async_copy(corr, corr_hbm, sem)
+            copy.start()
         if k + TILE < count:
             next_tile(k)
     last = slice(k, count)

time: 108 us -> 108 us (level)
  no operation moved by 1% of the time
where the time goes in v7:
time: 108 us
  blocking collectives  60.1 us (56%)
  Pallas kernels  16.6 us (15%)
  starting transfers between devices  16.2 us (15%)
  waiting for transfers between devices  12.2 us (11%)
  local copies, waits for them, and re-layouts  1.88 us (2%)
    all_to_all x1, blocking collectives, per_device(): lax.all_to_all(jnp.broadcast_to(piece, (depth,) + piece.shape), 'z', 0, 0)  14.3 us
    pallas_call x1, Pallas kernels, per_device(): pl.pallas_call(factor_kernel, out_shape=(jax.ShapeDtypeStruct((count, cou...  13.6 us
    all_to_all x1, blocking collectives, per_device(): lax.all_to_all(second.reshape(layer, 4 * planes // layer, half, TILE), LA...  12.7 us
    all_to_all x1, blocking collectives, per_device(): lax.all_to_all(part.reshape(layer, 5 * TILE // layer, TILE), LAYER, 0, 0)  11.2 us
    all_to_all x1, blocking collectives, per_device(): lax.all_to_all(jnp.broadcast_to(piece, (layer,) + piece.shape), LAYER, 0, 0)  11 us
    all_to_all x1, blocking collectives, per_device(): back = lax.all_to_all(turned, TEAM, 0, 0).reshape(planes, 2, rows, TILE)  10.8 us
    ppermute x3, starting transfers between devices, per_device(): lax.ppermute(x, SPACE, pairs)  9.68 us
    ppermute x3, waiting for transfers between devices, per_device(): lax.ppermute(x, SPACE, pairs)  9.55 us
  transfers between devices with their start and end apart: 5, of which 4 were waited for; matrix products, arithmetic and copies ran while one was open for 0% of the time, Pallas kernels for 0%

profile of v7, /device:TPU:1, one launch (start us, length us, event | category | flops | bytes accessed | tf_op | source)
XLA Modules:
  0.0 107.6 jit_solution(1115861192365061767)
XLA Ops:
  0.6 0.0 copy-start.1
  0.6 1.1 constant_dynamic-slice_fusion
  1.7 0.0 copy-done.1
  1.7 0.0 copy-start
  1.8 9.0 %collective-permute-start.2 = (f32[204,256]{1,0:T(8,128)S(1)}, f32[204,256]{1,0:T(8,128)S(1)}, u32[]{:S(2)}, u32[]{:S(2)}) collective-permute-start(f32[204,256]{1,0:T(8,128)S(1)} %get-tuple-element.12), channel_id=1, source_target_pairs={{0,240},{16,32},{32,16},{48,64},{64,48},{80,96},{96,80},{112,128},... | collective-permute-start | bytes 626696 | tf_op jit(solution)/shard_map/ppermute | solution.py:288
  10.7 0.0 collective-permute-start
  10.7 0.7 collective-permute-start.1
  11.5 4.2 %collective-permute-done.2.cross = f32[204,256]{1,0:T(8,128)S(1)} collective-permute-done((f32[204,256]{1,0:T(8,128)S(1)}, f32[204,256]{1,0:T(8,128)S(1)}, u32[]{:S(2)}, u32[]{:S(2)}) %collective-permute-start.2) | collective-permute-done | bytes 208928 | tf_op jit(solution)/shard_map/ppermute | solution.py:288
  15.7 5.3 %collective-permute-done.swap = f32[204,256]{1,0:T(8,128)S(1)} collective-permute-done((f32[204,256]{1,0:T(8,128)S(1)}, f32[204,256]{1,0:T(8,128)S(1)}, u32[]{:S(2)}, u32[]{:S(2)}) %collective-permute-start) | collective-permute-done | bytes 208928 | tf_op jit(solution)/shard_map/ppermute | solution.py:288
  21.0 0.0 collective-permute-done.1.near
  21.0 0.0 copy-done
  21.0 1.8 %filter.1 = f32[48,16,128]{2,1,0:T(8,128)S(1)} custom-call(s32[1]{0:T(128)} %bitcast.1.side, f32[204,256]{1,0:T(8,128)S(1)} %get-tuple-element.13.own, f32[204,256]{1,0:T(8,128)S(1)} %collective-permute-done.swap, f32[204,256]{1,0:T(8,128)S(1)} %collective-permute-done.1.near, f32[204,256]{1,0:T(8,128)S(1)} %collective-permute-done.2.cross, ...), custom_call_target="tpu_custom_call" | custom-call | tf_op jit(solution)/shard_map/filter/pallas_call | solution.py:290
  22.8 12.7 %all_to_all.25.own = f32[16,3,16,128]{3,2,1,0:T(8,128)S(1)} all-to-all(f32[16,3,16,128]{3,2,1,0:T(8,128)S(1)} %bitcast.14), channel_id=1, replica_groups=mesh['z'=8,'xh'=2,'y'=4,'xl'=2,'c'=2] {'xh','y','xl'}, dimensions={0} | all-to-all | bytes 786432 | tf_op jit(solution)/shard_map/all_to_all | solution.py:301
  35.6 2.5 %collective-permute-start.3 = (f32[16,3,16,128]{3,2,1,0:T(8,128)S(1)}, f32[16,3,16,128]{3,2,1,0:T(8,128)S(1)}, u32[]{:S(2)}, u32[]{:S(2)}) collective-permute-start(f32[16,3,16,128]{3,2,1,0:T(8,128)S(1)} %all_to_all.25.own), channel_id=1, source_target_pairs={{0,1},{1,0},{2,3},{3,2},{4,5},{5,4},{6,7},{7,6},{8,9},{9,8},{10,11... | collective-permute-start | bytes 1179656 | tf_op jit(solution)/shard_map/ppermute | solution.py:302
  38.0 1.3 %collective-permute-done.3.other = f32[16,3,16,128]{3,2,1,0:T(8,128)S(1)} collective-permute-done((f32[16,3,16,128]{3,2,1,0:T(8,128)S(1)}, f32[16,3,16,128]{3,2,1,0:T(8,128)S(1)}, u32[]{:S(2)}, u32[]{:S(2)}) %collective-permute-start.3) | collective-permute-done | bytes 393248 | tf_op jit(solution)/shard_map/ppermute | solution.py:302
  39.4 1.1 %gram.1 = (f32[640,128]{1,0:T(8,128)S(1)}, f32[512,384]{1,0:T(8,128)S(1)}) custom-call(s32[1]{0:T(128)} %bitcast.core, f32[16,3,16,128]{3,2,1,0:T(8,128)S(1)} %all_to_all.25.own, f32[16,3,16,128]{3,2,1,0:T(8,128)S(1)} %collective-permute-done.3.other), custom_call_target="tpu_custom_call" | custom-call | tf_op jit(solution)/shard_map/gram/pallas_call | solution.py:305
  40.5 11.2 %all_to_all.26 = f32[16,40,128]{2,1,0:T(8,128)S(1)} all-to-all(f32[16,40,128]{2,1,0:T(8,128)S(1)} %bitcast.17), channel_id=1, replica_groups=mesh['z'=8,'xh'=2,'y'=4,'xl'=2,'c'=2] {'xh','y','xl'}, dimensions={0} | all-to-all | bytes 655360 | tf_op jit(solution)/shard_map/all_to_all | solution.py:317
  51.7 14.3 %all_to_all.27 = f32[8,40,128]{2,1,0:T(8,128)S(1)} all-to-all(f32[8,40,128]{2,1,0:T(8,128)S(1)} %broadcast_in_dim.6), channel_id=1, replica_groups=mesh['z'=8,'xh'=2,'y'=4,'xl'=2,'c'=2] {'z'}, dimensions={0} | all-to-all | bytes 327680 | tf_op jit(solution)/shard_map/all_to_all | solution.py:319
  66.1 11.0 %all_to_all.28 = f32[16,40,128]{2,1,0:T(8,128)S(1)} all-to-all(f32[16,40,128]{2,1,0:T(8,128)S(1)} %broadcast_in_dim.7), channel_id=1, replica_groups=mesh['z'=8,'xh'=2,'y'=4,'xl'=2,'c'=2] {'xh','y','xl'}, dimensions={0} | all-to-all | bytes 655360 | tf_op jit(solution)/shard_map/all_to_all | solution.py:320
  77.1 4.0 %collective-permute-start.4 = (f32[640,128]{1,0:T(8,128)S(1)}, f32[640,128]{1,0:T(8,128)S(1)}, u32[]{:S(2)}, u32[]{:S(2)}) collective-permute-start(f32[640,128]{1,0:T(8,128)S(1)} %bitcast.15), channel_id=1, source_target_pairs={{0,1},{1,0},{2,3},{3,2},{4,5},{5,4},{6,7},{7,6},{8,9},{9,8},{10,11... | collective-permute-start | bytes 983048 | tf_op jit(solution)/shard_map/ppermute | solution.py:322
  81.1 1.3 %collective-permute-done.4.other = f32[640,128]{1,0:T(8,128)S(1)} collective-permute-done((f32[640,128]{1,0:T(8,128)S(1)}, f32[640,128]{1,0:T(8,128)S(1)}, u32[]{:S(2)}, u32[]{:S(2)}) %collective-permute-start.4) | collective-permute-done | bytes 327712 | tf_op jit(solution)/shard_map/ppermute | solution.py:322
  82.4 13.6 %factor.1 = (f32[512,512]{1,0:T(8,128)}, f32[8,3,32,128]{3,2,1,0:T(8,128)S(1)}) custom-call(s32[1]{0:T(128)} %bitcast.core, f32[640,128]{1,0:T(8,128)S(1)} %bitcast.16, f32[640,128]{1,0:T(8,128)S(1)} %collective-permute-done.4.other, f32[512,384]{1,0:T(8,128)S(1)} %get-tuple-element.7.fields), custom_call_target="tpu_custom_call" | custom-call | tf_op jit(solution)/shard_map/factor/pallas_call | solution.py:323
  96.0 10.8 %all_to_all.29 = f32[8,3,32,128]{3,2,1,0:T(8,128)S(1)} all-to-all(f32[8,3,32,128]{3,2,1,0:T(8,128)S(1)} %get-tuple-element.8), channel_id=1, replica_groups=mesh['z'=8,'xh'=2,'y'=4,'xl'=2,'c'=2] {'y','xl'}, dimensions={0} | all-to-all | bytes 786432 | tf_op jit(solution)/shard_map/all_to_all | solution.py:339
  106.8 0.8 copy.9
  (5 shorter events, 0.1 us)
Async XLA Ops:
  0.6 1.1 copy-start.1
  1.7 19.3 %copy-start = (f32[256,256]{1,0:T(8,128)S(1)}, f32[256,256]{1,0:T(8,128)}, u32[]{:S(2)}) copy-start(f32[256,256]{1,0:T(8,128)} %constant.20.clone.mat) | copy-start | bytes 786436
  1.8 13.9 %collective-permute-start.2 = (f32[204,256]{1,0:T(8,128)S(1)}, f32[204,256]{1,0:T(8,128)S(1)}, u32[]{:S(2)}, u32[]{:S(2)}) collective-permute-start(f32[204,256]{1,0:T(8,128)S(1)} %get-tuple-element.12), channel_id=1, source_target_pairs={{0,240},{16,32},{32,16},{48,64},{64,48},{80,96},{96,80},{112,128},... | collective-permute-start | bytes 626696 | tf_op jit(solution)/shard_map/ppermute | solution.py:288
  10.7 10.3 %collective-permute-start = (f32[204,256]{1,0:T(8,128)S(1)}, f32[204,256]{1,0:T(8,128)S(1)}, u32[]{:S(2)}, u32[]{:S(2)}) collective-permute-start(f32[204,256]{1,0:T(8,128)S(1)} %get-tuple-element.12), channel_id=1, source_target_pairs={{0,16},{16,0},{32,48},{48,32},{64,80},{80,64},{96,112},{112,96},{1... | collective-permute-start | bytes 626696 | tf_op jit(solution)/shard_map/ppermute | solution.py:288
  10.7 10.3 %collective-permute-start.1 = (f32[204,256]{1,0:T(8,128)S(1)}, f32[204,256]{1,0:T(8,128)S(1)}, u32[]{:S(2)}, u32[]{:S(2)}) collective-permute-start(f32[204,256]{1,0:T(8,128)S(1)} %get-tuple-element.13.own), channel_id=1, source_target_pairs={{0,224},{16,48},{32,0},{48,80},{64,32},{80,112},{96,64},{112,144},... | collective-permute-start | bytes 626696 | tf_op jit(solution)/shard_map/ppermute | solution.py:288
  35.6 3.8 %collective-permute-start.3 = (f32[16,3,16,128]{3,2,1,0:T(8,128)S(1)}, f32[16,3,16,128]{3,2,1,0:T(8,128)S(1)}, u32[]{:S(2)}, u32[]{:S(2)}) collective-permute-start(f32[16,3,16,128]{3,2,1,0:T(8,128)S(1)} %all_to_all.25.own), channel_id=1, source_target_pairs={{0,1},{1,0},{2,3},{3,2},{4,5},{5,4},{6,7},{7,6},{8,9},{9,8},{10,11... | collective-permute-start | bytes 1179656 | tf_op jit(solution)/shard_map/ppermute | solution.py:302
  77.1 5.3 %collective-permute-start.4 = (f32[640,128]{1,0:T(8,128)S(1)}, f32[640,128]{1,0:T(8,128)S(1)}, u32[]{:S(2)}, u32[]{:S(2)}) collective-permute-start(f32[640,128]{1,0:T(8,128)S(1)} %bitcast.15), channel_id=1, source_target_pairs={{0,1},{1,0},{2,3},{3,2},{4,5},{5,4},{6,7},{7,6},{8,9},{9,8},{10,11... | collective-permute-start | bytes 983048 | tf_op jit(solution)/shard_map/ppermute | solution.py:322

commit v8 on v7

--- a/solution.py
+++ b/solution.py
@@ -53,36 +53,38 @@
     count = 2 * planes + 2 * RADIUS
 
     def filter_slabs(slabs):
-        def field(p):
-            return slabs[p // planes][p % planes * rows : (p % planes + 1) * rows, :]
-
-        def level(p):
+        def field(p, r, lanes):
+            at = p % planes * rows + r
+            return slabs[p // planes][at : at + 8, lanes]
+
+        def level(p, lanes):
             at = size + p % planes
-            return (slabs[p // planes][at : at + 1, :] - SHIFT_MID) / HALF_SPAN
-
-        def plane(q):
-            return first[q * rows : (q + 1) * rows, :]
+            return (slabs[p // planes][at : at + 1, lanes] - SHIFT_MID) / HALF_SPAN
 
         skip = planes - RADIUS
         for k, slab in enumerate(slabs):
             begin, end = max(k * planes, skip), min((k + 1) * planes, skip + count)
             part = slab[(begin - k * planes) * rows : (end - k * planes) * rows, :]
             first[(begin - skip) * rows : (end - skip) * rows, :] = dot32(part, mat[...], ((1,), (0,)))
-        for q in range(count):
-            p = q + skip
-            acc = plane(q) + level(p) * field(p)
-            for k in range(RADIUS):
-                acc = acc + (SCALE * COEFS[k]) * (field(p + k + 1) + field(p - k - 1))
-            first[q * rows : (q + 1) * rows, :] = acc
+        places = [(r, slice(l, l + TILE)) for r in range(0, rows, 8) for l in range(0, CELLS, TILE)]
+        for r, lanes in places:
+            for q in range(count):
+                p = q + skip
+                at = slice(q * rows + r, q * rows + r + 8)
+                acc = first[at, lanes] + level(p, lanes) * field(p, r, lanes)
+                for k in range(RADIUS):
+                    acc = acc + (SCALE * COEFS[k]) * (field(p + k + 1, r, lanes) + field(p - k - 1, r, lanes))
+                first[at, lanes] = acc
         inner = dot32(first[RADIUS * rows : RADIUS * rows + 2 * size, :], mat[...], ((1,), (0,)))
-        for z in range(2 * planes):
-            q = z + RADIUS
-            acc = inner[z * rows : (z + 1) * rows, :] + level(z + planes) * plane(q)
-            for k in range(RADIUS):
-                acc = acc + (SCALE * COEFS[k]) * (plane(q + k + 1) + plane(q - k - 1))
-            second = 2.0 * acc - field(z + planes)
-            out[2 * z] = second[:, :TILE]
-            out[2 * z + 1] = second[:, TILE:]
+        for r, lanes in places:
+            window = [first[q * rows + r : q * rows + r + 8, lanes] for q in range(count)]
+            for z in range(2 * planes):
+                q = z + RADIUS
+                acc = inner[z * rows + r : z * rows + r + 8, lanes] + level(z + planes, lanes) * window[q]
+                for k in range(RADIUS):
+                    acc = acc + (SCALE * COEFS[k]) * (window[q + k + 1] + window[q - k - 1])
+                second = 2.0 * acc - field(z + planes, r, lanes)
+                out[2 * z + lanes.start // TILE, r : r + 8, :] = second
 
     @pl.when(side[0] == 0)
     def _():

time: 108 us -> 108 us (level)
  no operation moved by 1% of the time
where the time goes in v8:
time: 108 us
  blocking collectives  60.1 us (56%)
  Pallas kernels  16.6 us (15%)
  starting transfers between devices  16.2 us (15%)
  waiting for transfers between devices  12.2 us (11%)
  local copies, waits for them, and re-layouts  1.88 us (2%)
    all_to_all x1, blocking collectives, per_device(): lax.all_to_all(jnp.broadcast_to(piece, (depth,) + piece.shape), 'z', 0, 0)  14.3 us
    pallas_call x1, Pallas kernels, per_device(): pl.pallas_call(factor_kernel, out_shape=(jax.ShapeDtypeStruct((count, cou...  13.6 us
    all_to_all x1, blocking collectives, per_device(): lax.all_to_all(second.reshape(layer, 4 * planes // layer, half, TILE), LA...  12.7 us
    all_to_all x1, blocking collectives, per_device(): lax.all_to_all(part.reshape(layer, 5 * TILE // layer, TILE), LAYER, 0, 0)  11.2 us
    all_to_all x1, blocking collectives, per_device(): lax.all_to_all(jnp.broadcast_to(piece, (layer,) + piece.shape), LAYER, 0, 0)  11 us
    all_to_all x1, blocking collectives, per_device(): back = lax.all_to_all(turned, TEAM, 0, 0).reshape(planes, 2, rows, TILE)  10.8 us
    ppermute x3, starting transfers between devices, per_device(): lax.ppermute(x, SPACE, pairs)  9.68 us
    ppermute x3, waiting for transfers between devices, per_device(): lax.ppermute(x, SPACE, pairs)  9.55 us
  transfers between devices with their start and end apart: 5, of which 4 were waited for; matrix products, arithmetic and copies ran while one was open for 0% of the time, Pallas kernels for 0%

profile of v8, /device:TPU:1, one launch (start us, length us, event | category | flops | bytes accessed | tf_op | source)
XLA Modules:
  0.0 107.6 jit_solution(1132827623205601587)
XLA Ops:
  0.6 0.0 copy-start.1
  0.6 1.1 constant_dynamic-slice_fusion
  1.7 0.0 copy-done.1
  1.7 0.0 copy-start
  1.8 9.0 %collective-permute-start.2 = (f32[204,256]{1,0:T(8,128)S(1)}, f32[204,256]{1,0:T(8,128)S(1)}, u32[]{:S(2)}, u32[]{:S(2)}) collective-permute-start(f32[204,256]{1,0:T(8,128)S(1)} %get-tuple-element.12), channel_id=1, source_target_pairs={{0,240},{16,32},{32,16},{48,64},{64,48},{80,96},{96,80},{112,128},... | collective-permute-start | bytes 626696 | tf_op jit(solution)/shard_map/ppermute | solution.py:290
  10.7 0.0 collective-permute-start
  10.7 0.7 collective-permute-start.1
  11.5 4.2 %collective-permute-done.2.cross = f32[204,256]{1,0:T(8,128)S(1)} collective-permute-done((f32[204,256]{1,0:T(8,128)S(1)}, f32[204,256]{1,0:T(8,128)S(1)}, u32[]{:S(2)}, u32[]{:S(2)}) %collective-permute-start.2) | collective-permute-done | bytes 208928 | tf_op jit(solution)/shard_map/ppermute | solution.py:290
  15.7 5.3 %collective-permute-done.swap = f32[204,256]{1,0:T(8,128)S(1)} collective-permute-done((f32[204,256]{1,0:T(8,128)S(1)}, f32[204,256]{1,0:T(8,128)S(1)}, u32[]{:S(2)}, u32[]{:S(2)}) %collective-permute-start) | collective-permute-done | bytes 208928 | tf_op jit(solution)/shard_map/ppermute | solution.py:290
  21.0 0.0 collective-permute-done.1.near
  21.0 0.0 copy-done
  21.0 1.8 %filter.1 = f32[48,16,128]{2,1,0:T(8,128)S(1)} custom-call(s32[1]{0:T(128)} %bitcast.1.side, f32[204,256]{1,0:T(8,128)S(1)} %get-tuple-element.13.own, f32[204,256]{1,0:T(8,128)S(1)} %collective-permute-done.swap, f32[204,256]{1,0:T(8,128)S(1)} %collective-permute-done.1.near, f32[204,256]{1,0:T(8,128)S(1)} %collective-permute-done.2.cross, ...), custom_call_target="tpu_custom_call" | custom-call | tf_op jit(solution)/shard_map/filter/pallas_call | solution.py:292
  22.9 12.7 %all_to_all.25.own = f32[16,3,16,128]{3,2,1,0:T(8,128)S(1)} all-to-all(f32[16,3,16,128]{3,2,1,0:T(8,128)S(1)} %bitcast.14), channel_id=1, replica_groups=mesh['z'=8,'xh'=2,'y'=4,'xl'=2,'c'=2] {'xh','y','xl'}, dimensions={0} | all-to-all | bytes 786432 | tf_op jit(solution)/shard_map/all_to_all | solution.py:303
  35.6 2.4 %collective-permute-start.3 = (f32[16,3,16,128]{3,2,1,0:T(8,128)S(1)}, f32[16,3,16,128]{3,2,1,0:T(8,128)S(1)}, u32[]{:S(2)}, u32[]{:S(2)}) collective-permute-start(f32[16,3,16,128]{3,2,1,0:T(8,128)S(1)} %all_to_all.25.own), channel_id=1, source_target_pairs={{0,1},{1,0},{2,3},{3,2},{4,5},{5,4},{6,7},{7,6},{8,9},{9,8},{10,11... | collective-permute-start | bytes 1179656 | tf_op jit(solution)/shard_map/ppermute | solution.py:304
  38.0 1.3 %collective-permute-done.3.other = f32[16,3,16,128]{3,2,1,0:T(8,128)S(1)} collective-permute-done((f32[16,3,16,128]{3,2,1,0:T(8,128)S(1)}, f32[16,3,16,128]{3,2,1,0:T(8,128)S(1)}, u32[]{:S(2)}, u32[]{:S(2)}) %collective-permute-start.3) | collective-permute-done | bytes 393248 | tf_op jit(solution)/shard_map/ppermute | solution.py:304
  39.4 1.1 %gram.1 = (f32[640,128]{1,0:T(8,128)S(1)}, f32[512,384]{1,0:T(8,128)S(1)}) custom-call(s32[1]{0:T(128)} %bitcast.core, f32[16,3,16,128]{3,2,1,0:T(8,128)S(1)} %all_to_all.25.own, f32[16,3,16,128]{3,2,1,0:T(8,128)S(1)} %collective-permute-done.3.other), custom_call_target="tpu_custom_call" | custom-call | tf_op jit(solution)/shard_map/gram/pallas_call | solution.py:307
  40.5 11.2 %all_to_all.26 = f32[16,40,128]{2,1,0:T(8,128)S(1)} all-to-all(f32[16,40,128]{2,1,0:T(8,128)S(1)} %bitcast.17), channel_id=1, replica_groups=mesh['z'=8,'xh'=2,'y'=4,'xl'=2,'c'=2] {'xh','y','xl'}, dimensions={0} | all-to-all | bytes 655360 | tf_op jit(solution)/shard_map/all_to_all | solution.py:319
  51.7 14.3 %all_to_all.27 = f32[8,40,128]{2,1,0:T(8,128)S(1)} all-to-all(f32[8,40,128]{2,1,0:T(8,128)S(1)} %broadcast_in_dim.6), channel_id=1, replica_groups=mesh['z'=8,'xh'=2,'y'=4,'xl'=2,'c'=2] {'z'}, dimensions={0} | all-to-all | bytes 327680 | tf_op jit(solution)/shard_map/all_to_all | solution.py:321
  66.1 11.0 %all_to_all.28 = f32[16,40,128]{2,1,0:T(8,128)S(1)} all-to-all(f32[16,40,128]{2,1,0:T(8,128)S(1)} %broadcast_in_dim.7), channel_id=1, replica_groups=mesh['z'=8,'xh'=2,'y'=4,'xl'=2,'c'=2] {'xh','y','xl'}, dimensions={0} | all-to-all | bytes 655360 | tf_op jit(solution)/shard_map/all_to_all | solution.py:322
  77.1 4.0 %collective-permute-start.4 = (f32[640,128]{1,0:T(8,128)S(1)}, f32[640,128]{1,0:T(8,128)S(1)}, u32[]{:S(2)}, u32[]{:S(2)}) collective-permute-start(f32[640,128]{1,0:T(8,128)S(1)} %bitcast.15), channel_id=1, source_target_pairs={{0,1},{1,0},{2,3},{3,2},{4,5},{5,4},{6,7},{7,6},{8,9},{9,8},{10,11... | collective-permute-start | bytes 983048 | tf_op jit(solution)/shard_map/ppermute | solution.py:324
  81.1 1.3 %collective-permute-done.4.other = f32[640,128]{1,0:T(8,128)S(1)} collective-permute-done((f32[640,128]{1,0:T(8,128)S(1)}, f32[640,128]{1,0:T(8,128)S(1)}, u32[]{:S(2)}, u32[]{:S(2)}) %collective-permute-start.4) | collective-permute-done | bytes 327712 | tf_op jit(solution)/shard_map/ppermute | solution.py:324
  82.4 13.6 %factor.1 = (f32[512,512]{1,0:T(8,128)}, f32[8,3,32,128]{3,2,1,0:T(8,128)S(1)}) custom-call(s32[1]{0:T(128)} %bitcast.core, f32[640,128]{1,0:T(8,128)S(1)} %bitcast.16, f32[640,128]{1,0:T(8,128)S(1)} %collective-permute-done.4.other, f32[512,384]{1,0:T(8,128)S(1)} %get-tuple-element.7.fields), custom_call_target="tpu_custom_call" | custom-call | tf_op jit(solution)/shard_map/factor/pallas_call | solution.py:325
  96.0 10.8 %all_to_all.29 = f32[8,3,32,128]{3,2,1,0:T(8,128)S(1)} all-to-all(f32[8,3,32,128]{3,2,1,0:T(8,128)S(1)} %get-tuple-element.8), channel_id=1, replica_groups=mesh['z'=8,'xh'=2,'y'=4,'xl'=2,'c'=2] {'y','xl'}, dimensions={0} | all-to-all | bytes 786432 | tf_op jit(solution)/shard_map/all_to_all | solution.py:341
  106.9 0.8 copy.9
  (5 shorter events, 0.1 us)
Async XLA Ops:
  0.6 1.1 copy-start.1
  1.7 19.3 %copy-start = (f32[256,256]{1,0:T(8,128)S(1)}, f32[256,256]{1,0:T(8,128)}, u32[]{:S(2)}) copy-start(f32[256,256]{1,0:T(8,128)} %constant.20.clone.mat) | copy-start | bytes 786436
  1.8 13.9 %collective-permute-start.2 = (f32[204,256]{1,0:T(8,128)S(1)}, f32[204,256]{1,0:T(8,128)S(1)}, u32[]{:S(2)}, u32[]{:S(2)}) collective-permute-start(f32[204,256]{1,0:T(8,128)S(1)} %get-tuple-element.12), channel_id=1, source_target_pairs={{0,240},{16,32},{32,16},{48,64},{64,48},{80,96},{96,80},{112,128},... | collective-permute-start | bytes 626696 | tf_op jit(solution)/shard_map/ppermute | solution.py:290
  10.7 10.3 %collective-permute-start = (f32[204,256]{1,0:T(8,128)S(1)}, f32[204,256]{1,0:T(8,128)S(1)}, u32[]{:S(2)}, u32[]{:S(2)}) collective-permute-start(f32[204,256]{1,0:T(8,128)S(1)} %get-tuple-element.12), channel_id=1, source_target_pairs={{0,16},{16,0},{32,48},{48,32},{64,80},{80,64},{96,112},{112,96},{1... | collective-permute-start | bytes 626696 | tf_op jit(solution)/shard_map/ppermute | solution.py:290
  10.7 10.3 %collective-permute-start.1 = (f32[204,256]{1,0:T(8,128)S(1)}, f32[204,256]{1,0:T(8,128)S(1)}, u32[]{:S(2)}, u32[]{:S(2)}) collective-permute-start(f32[204,256]{1,0:T(8,128)S(1)} %get-tuple-element.13.own), channel_id=1, source_target_pairs={{0,224},{16,48},{32,0},{48,80},{64,32},{80,112},{96,64},{112,144},... | collective-permute-start | bytes 626696 | tf_op jit(solution)/shard_map/ppermute | solution.py:290
  35.6 3.8 %collective-permute-start.3 = (f32[16,3,16,128]{3,2,1,0:T(8,128)S(1)}, f32[16,3,16,128]{3,2,1,0:T(8,128)S(1)}, u32[]{:S(2)}, u32[]{:S(2)}) collective-permute-start(f32[16,3,16,128]{3,2,1,0:T(8,128)S(1)} %all_to_all.25.own), channel_id=1, source_target_pairs={{0,1},{1,0},{2,3},{3,2},{4,5},{5,4},{6,7},{7,6},{8,9},{9,8},{10,11... | collective-permute-start | bytes 1179656 | tf_op jit(solution)/shard_map/ppermute | solution.py:304
  77.1 5.3 %collective-permute-start.4 = (f32[640,128]{1,0:T(8,128)S(1)}, f32[640,128]{1,0:T(8,128)S(1)}, u32[]{:S(2)}, u32[]{:S(2)}) collective-permute-start(f32[640,128]{1,0:T(8,128)S(1)} %bitcast.15), channel_id=1, source_target_pairs={{0,1},{1,0},{2,3},{3,2},{4,5},{5,4},{6,7},{7,6},{8,9},{9,8},{10,11... | collective-permute-start | bytes 983048 | tf_op jit(solution)/shard_map/ppermute | solution.py:324
